TPU v7x, 256 devices: a whole 4x4x8 slice. The times are simulated.
256 devices in a mesh: dp: 32 (over x, z_lo, core), mp: 8 (over y, z_hi).
Axes of the slice: x: 4, y: 4, z: 8 (z_hi: 2, z_lo: 4; z = z_hi * 4 + z_lo), core: 2. Of those that a mesh axis runs over, the one named last changes fastest.
Arguments:
- tokens: bfloat16 [32, 1024, 3584], P('dp'), may hold values from -14 to 14
- modality: int32 [32, 8], P('dp'), may hold values from 0 to 1, as said below
- block_mask: int32 [32, 8, 8], P('dp'), may hold values from 0 to 2, as said below
- q_weight: bfloat16 [2, 3584, 2048], P(None, 'dp', 'mp'), may hold values from -0.09375 to 0.09375
- kv_weight: bfloat16 [2, 3584, 1024], P(None, 'dp'), may hold values from -0.09375 to 0.09375
- o_weight: bfloat16 [2, 2048, 3584], P(None, 'mp', 'dp'), may hold values from -0.125 to 0.125
Outputs:
- attn_out: bfloat16 [32, 1024, 3584], P('dp', 'mp')
Inputs may be any that keep to these rules, and one draw needn't show every extreme that they name: modality[s, b] names the section (0 text, 1 image) whose weights serve the 128 tokens of block b of sequence s. block_mask[s, i, j] tells which tokens of block i see block j: 0 none, 1 all, 2 those at or before the query's position; every diagonal entry is 1 or 2, every entry off the diagonal is 0 or 1.
All inputs are finite; a program needn't handle non-finite values.
Results may differ from a plain program's by a relative error of at most 0.015.
Values may be sent and summed in bfloat16 or wider, within the bound.
No kernel may reach another device: no remote copies, remote signals or barrier semaphores. Data moves between devices by JAX's collectives and lax.ppermute only.
A program may use at most 128 MiB of HBM per device.

v0:
```python
import functools

import jax
import jax.numpy as jnp
import numpy as np
from jax import lax
from jax.experimental import pallas as pl
from jax.experimental.pallas import tpu as pltpu
from jax.sharding import Mesh
from jax.sharding import PartitionSpec as P

D = 3584
HD = 128
BLK = 128
NBLK = 8
SEQ = 1024
ROWS = 112
NG = 32
NY = 4
QB = 4
HEADS = 4
WID = HEADS * HD
ROPE_THETA = 1000000.0
NEG = -1e30
ANY = pl.BlockSpec(memory_space=pl.ANY)
SM = pl.BlockSpec(memory_space=pltpu.SMEM)


def rotary_tables():
    half = HD // 2
    freq = ROPE_THETA ** (-np.arange(half, dtype=np.float64) * 2.0 / HD)
    freq = np.concatenate([freq, freq])[None, :]
    fine = np.arange(BLK, dtype=np.float64)[:, None] * freq
    base = BLK * np.arange(NBLK, dtype=np.float64)[:, None] * freq
    return [np.asarray(t, np.float32) for t in (np.cos(fine), np.sin(fine), np.cos(base), np.sin(base))]


def block_tables(tables, b):
    cf, sf = tables[0][...], tables[1][...]
    cb, sb = tables[2][pl.ds(b, 1), :], tables[3][pl.ds(b, 1), :]
    sign = jnp.where(lax.broadcasted_iota(jnp.int32, (1, HD), 1) < HD // 2, -1.0, 1.0)
    return cb * cf - sb * sf, sign * (sb * cf + cb * sf)


def rotate(x, cos, sin):
    return x * cos + pltpu.roll(x, HD // 2, 1) * sin


DX = (0, -1, 1, 2)
DZ = (0, -1, 1, -2, 2, -3, 3, 4)
Q_AT, O_AT, KV_AT, POS = 0, 64, 128, 160


def piece_tables(x, z, c, y):
    cc = jnp.stack([c, 1 - c])[:, None, None]
    four, eight = np.array(DX), np.array(DZ)

    def group(dx, dz):
        zs = (z + dz) & 7
        return (((x + dx) & 3) * 4 + (zs & 3)) * 2 + cc, zs >> 2

    gq, hq = group(four[None, None, :], eight[None, :, None])
    go, ho = group(four[None, :, None], eight[None, None, :])
    gk, _ = group(four[None, :, None], four[None, None, :])
    parts = (gq * 2 + hq, go * 2 + ho, gk)
    parts += (y, z >> 2)
    return jnp.concatenate([t.reshape(-1) for t in parts]).astype(jnp.int32)


def fetch(tab, base, refs, w, sem):
    for ref in refs:

        def start(j, carry, ref=ref, base=base):
            at = tab[base + j]
            cols = pl.ds(pl.multiple_of((at & 1) * (2 * HD), 2 * HD), 2 * HD)
            pltpu.make_async_copy(ref.at[j], w.at[:, at >> 1, :, cols], sem).start()
            return carry

        lax.fori_loop(0, ref.shape[0], start, 0)
        base += ref.shape[0]


def attend(i, zh, mask, q, k, v, s, out):
    b = 2 * i + zh
    diff = lax.broadcasted_iota(jnp.int32, (BLK, BLK), 1) - lax.broadcasted_iota(
        jnp.int32, (BLK, BLK), 0
    )
    diff = jnp.concatenate([diff, diff], axis=0)

    def heads(n, carry):
        qq = q[i, pl.ds(pl.multiple_of(n * 2 * BLK, 2 * BLK), 2 * BLK), :]
        for j in range(NBLK):
            mb = mask[b, j]
            off = jnp.where(mb == 1, 4096, jnp.where(mb == 2, BLK * (b - j), -4096))
            sj = lax.dot_general(
                qq,
                k[j * BLK : (j + 1) * BLK, :],
                (((1,), (1,)), ((), ())),
                preferred_element_type=jnp.float32,
            )
            s[:, j * BLK : (j + 1) * BLK] = jnp.where(diff <= off, sj, NEG)
        sv = s[...]
        p = jnp.exp((sv - jnp.max(sv, axis=1, keepdims=True)) * (HD**-0.5))
        total = jnp.sum(p, axis=1, keepdims=True)
        a = jnp.dot(p.astype(BF), v[...], preferred_element_type=jnp.float32) / total
        a = a.astype(BF)
        cols = pl.ds(pl.multiple_of(n * 2 * HD, 2 * HD), 2 * HD)
        out[:, cols] = jnp.concatenate([a[:BLK], a[BLK:]], axis=1)
        return carry

    lax.fori_loop(0, HEADS // 2, heads, 0)


def project_out(a, w, sec, out, first, count):
    quarter = D // 4

    def chunk(g, carry):
        wt = w[sec, pl.ds(pl.multiple_of(8 * (first + g), 8), 8)].reshape(quarter, WID)
        r = lax.dot_general(a, wt, (((1,), (1,)), ((), ())), preferred_element_type=jnp.float32)
        out[:, pl.ds(pl.multiple_of(g * quarter, BLK), quarter)] = r.astype(BF)
        return carry

    lax.fori_loop(0, count, chunk, 0)


def head_body(mod, mask, tab, *refs):
    kv_refs, q_refs, o_refs, x_hbm, tables = refs[:6], refs[6:17], refs[17:24], refs[24], refs[25:29]
    q, k, v = refs[29:32]
    outs = refs[32:34]
    x, wk, wq, wo, att, s, inv, xsem, ksem, qsem, osem = refs[34:]
    y0, zh = tab[POS], tab[POS + 1]
    for a in range(4):

        def start(j, carry, a=a):
            at = [tab[KV_AT + n * 16 + a * 4 + j] for n in range(2)]
            if a < 3:
                pltpu.make_async_copy(kv_refs[a].at[:, j], wk.at[:, at[0]], ksem).start()
            else:
                for m in range(2):
                    pltpu.make_async_copy(kv_refs[3 + m].at[j], wk.at[m, at[0]], ksem).start()
            src = kv_refs[5].at[pl.ds(2 * a, 2), j]
            pltpu.make_async_copy(src, wk.at[:, at[1]], ksem).start()
            return carry

        lax.fori_loop(0, 4, start, 0)
    order = [2 * i + zh for i in range(QB)] + [2 * i + 1 - zh for i in range(QB)]
    kinds = [mod[b] for b in order]
    n1 = sum(kinds)
    h0 = (NBLK - n1 + 1) // 2
    passes = h0 + (n1 + 1) // 2
    for t in range(NBLK + 2):
        inv[t] = -1
    c0, c1 = 0, 0
    for n, (b, kind) in enumerate(zip(order, kinds)):
        inv[jnp.where(kind == 0, c0, 2 * h0 + c1)] = b
        c0, c1 = c0 + 1 - kind, c1 + kind
        if n == QB - 1:
            p0, p1 = (c0 + 1) // 2, (c1 + 1) // 2

    def block_copy(t):
        rows = pl.ds(pl.multiple_of(inv[t] * BLK, BLK), BLK)
        return pltpu.make_async_copy(x_hbm.at[rows], x.at[t], xsem.at[t])

    def start_x(t, carry):
        @pl.when(inv[t] >= 0)
        def _():
            block_copy(t).start()

        return carry

    lax.fori_loop(0, NBLK + 2, start_x, 0)
    fetch(tab, Q_AT, q_refs, wq, qsem)
    fetch(tab, O_AT, o_refs, wo, osem)
    pltpu.make_async_copy(wk, wk, ksem).wait()

    def project_kv(p, carry):
        sec = jnp.where(p >= h0, 1, 0)
        ids = [inv[2 * p + t] for t in range(2)]
        for t in range(2):

            @pl.when(ids[t] >= 0)
            def _():
                block_copy(2 * p + t).wait()

        lhs = x[pl.ds(2 * p, 2)].reshape(2 * BLK, D)
        y = jnp.dot(lhs, wk[sec].reshape(D, 2 * HD), preferred_element_type=jnp.float32)
        for t in range(2):

            @pl.when(ids[t] >= 0)
            def _():
                yt = y[t * BLK : (t + 1) * BLK]
                cos, sin = block_tables(tables, ids[t])
                rows = pl.ds(pl.multiple_of(ids[t] * BLK, BLK), BLK)
                k[rows, :] = rotate(yt[:, :HD], cos, sin).astype(BF)
                v[rows, :] = yt[:, HD:].astype(BF)

        return carry

    lax.fori_loop(0, passes, project_kv, 0)
    pltpu.make_async_copy(wq, wq, qsem).wait()

    def project_q(p, carry):
        sec = jnp.where(p >= p0, 1, 0)
        slot = jnp.where(p >= p0, 2 * (h0 + p - p0), 2 * p)
        lhs = x[pl.ds(slot, 2)].reshape(2 * BLK, D)
        y = jnp.dot(lhs, wq[sec].reshape(D, WID), preferred_element_type=jnp.float32)
        for t in range(2):
            b = inv[slot + t]

            @pl.when((b >= 0) & ((b & 1) == zh))
            def _():
                cos, sin = block_tables(tables, b)
                for h in range(HEADS):
                    yt = y[t * BLK : (t + 1) * BLK, h * HD : (h + 1) * HD]
                    q[b >> 1, h * BLK : (h + 1) * BLK, :] = rotate(yt, cos, sin).astype(BF)

        return carry

    lax.fori_loop(0, p0 + p1, project_q, 0)
    far = (y0 + 2) & 3
    attend(far, zh, mask, q, k, v, s, att)
    pltpu.make_async_copy(wo, wo, osem).wait()
    for n in range(2):
        project_out(att[...], wo, mod[2 * far + zh], outs[n], 2 * n, 2)


def tail_body(first, count, mod, mask, tab, *refs):
    o_refs, (q, k, v, out, wo, att, s, osem) = refs[:7], refs[7:]
    y0, zh = tab[POS], tab[POS + 1]
    fetch(tab, O_AT, o_refs, wo, osem)

    def one(n, carry):
        attend((y0 + first + 2 * n) & 3, zh, mask, q, k, v, s, att.at[n])
        return carry

    lax.fori_loop(0, count, one, 0)
    pltpu.make_async_copy(wo, wo, osem).wait()

    def two(n, carry):
        sec = mod[2 * ((y0 + first + 2 * n) & 3) + zh]
        project_out(att[n], wo, sec, out.at[n], 0, 4)
        return carry

    lax.fori_loop(0, count, two, 0)


VM = pl.BlockSpec(memory_space=pltpu.VMEM)
BF = jnp.bfloat16
HALF_BLOCK = jax.ShapeDtypeStruct((BLK, D // 2), BF)


def head(mod, mask, tab, kv_all, q_all, o_all, x, tables):
    return pl.pallas_call(
        head_body,
        out_shape=[
            jax.ShapeDtypeStruct((QB, HEADS * BLK, HD), BF),
            jax.ShapeDtypeStruct((SEQ, HD), BF),
            jax.ShapeDtypeStruct((SEQ, HD), BF),
            HALF_BLOCK,
            HALF_BLOCK,
        ],
        in_specs=[SM] * 3 + [ANY] * 25 + [VM] * 4,
        out_specs=[VM] * 5,
        scratch_shapes=[
            pltpu.VMEM((NBLK + 2, BLK, D), BF),
            pltpu.VMEM((2, NG, ROWS, 2 * HD), BF),
            pltpu.VMEM((2, NG, ROWS, WID), BF),
            pltpu.VMEM((2, NG, ROWS, WID), BF),
            pltpu.VMEM((BLK, WID), BF),
            pltpu.VMEM((2 * BLK, SEQ), jnp.float32),
            pltpu.SMEM((NBLK + 2,), jnp.int32),
            pltpu.SemaphoreType.DMA((NBLK + 2,)),
            pltpu.SemaphoreType.DMA,
            pltpu.SemaphoreType.DMA,
            pltpu.SemaphoreType.DMA,
        ],
        name="head",
        cost_estimate=pl.CostEstimate(
            flops=2 * SEQ * D * 2 * HD + 2 * QB * BLK * D * WID,
            bytes_accessed=2 * SEQ * D + 8 * D * HD + 8 * D * WID,
            transcendentals=BLK * HEADS * SEQ,
        ),
    )(mod, mask, tab, *kv_all, *q_all, *o_all, x, *tables)


def tail(first, count, mod, mask, tab, o_all, q, k, v):
    return pl.pallas_call(
        functools.partial(tail_body, first, count),
        out_shape=jax.ShapeDtypeStruct((count, BLK, D), BF),
        in_specs=[SM] * 3 + [ANY] * 7 + [VM] * 3,
        out_specs=VM,
        scratch_shapes=[
            pltpu.VMEM((2, NG, ROWS, WID), BF),
            pltpu.VMEM((count, BLK, WID), BF),
            pltpu.VMEM((2 * BLK, SEQ), jnp.float32),
            pltpu.SemaphoreType.DMA,
        ],
        name="tail",
        cost_estimate=pl.CostEstimate(
            flops=count * (2 * BLK * D * WID + 4 * BLK * SEQ * WID),
            bytes_accessed=4 * D * WID,
            transcendentals=count * BLK * HEADS * SEQ,
        ),
    )(mod, mask, tab, *o_all, q, k, v)


def along_x(a, step):
    return lax.ppermute(a, "x", [(i, (i + step) % 4) for i in range(4)])


def along_z(a, step):
    at = [(z & 3) * 2 + (z >> 2) for z in range(8)]
    return lax.ppermute(a, ("zl", "zh"), [(at[z], at[(z + step) % 8]) for z in range(8)])


def swap(a):
    return lax.ppermute(a, "c", [(0, 1), (1, 0)])


def gather(kv, q, o, at):
    p1p, p1m = along_x(q, 1), along_x(q, -1)
    own = jnp.concatenate([kv[:1], o, kv[1:]], axis=0)
    r1p, r1m = along_z(own, 1), along_z(own, -1)
    p2p, p2m = along_x(p1p[0], 1), along_x(p1m[1], -1)
    r2p, r2m = along_z(r1p[:3], 1), along_z(r1m[1:], -1)
    kb = jnp.stack(
        [
            jnp.stack([own[0], r1p[0], r1m[0], r2p[0]]),
            jnp.stack([own[3], r1p[3], r1m[3], r2m[2]]),
        ]
    )
    k1p, k1m = along_x(kb, 1), along_x(kb, -1)
    r2p, r2m = r2p[1:], r2m[:2]
    r3p, r3m = along_z(r2p, 1), along_z(r2m, -1)
    b = jnp.stack([q, p1p, p1m, jnp.stack([p2p, p2m])])
    b, r3p, r3m = lax.optimization_barrier((b, r3p, r3m))
    r4 = jnp.stack([along_z(r3p[0], 1), along_z(r3m[1], -1)])
    t1p, t1m = along_z(b, 1), along_z(b, -1)
    t1p, t1m, r4, k1p, k1m = lax.optimization_barrier((t1p, t1m, r4, k1p, k1m))
    ob = jnp.stack([o, r1p[1:3], r1m[1:3], r2p, r2m, r3p, r3m, r4])
    o1p, o1m = along_x(ob, 1), along_x(ob, -1)
    t2p, t2m = along_z(t1p, 1), along_z(t1m, -1)
    k2p, k2m = along_x(k1p[0], 1), along_x(k1m[1], -1)
    kv_all = [kb, k1p, k1m, k2p, k2m]
    kv_all.append(swap(jnp.concatenate([kb, k1p, k1m, jnp.stack([k2p, k2m])])))
    t2p, t2m, at = lax.optimization_barrier((t2p, t2m, at))
    tab = piece_tables(*at)
    t3p, t3m = along_z(t2p, 1), along_z(t2m, -1)
    o1p, o1m, t3p, t3m = lax.optimization_barrier((o1p, o1m, t3p, t3m))
    o2p, o2m = along_x(o1p[:4], 1), along_x(o1m[4:], -1)
    t4p, t4m = along_z(t3p[:2], 1), along_z(t3m[2:], -1)
    q_all = [b, t1p, t1m, t2p, t2m, t3p, t3m, t4p, t4m]
    q_all.append(swap(jnp.concatenate([b, t1p, t1m, t2p, t2m])))
    q_all.append(swap(jnp.concatenate([t3p, t3m, t4p, t4m])))
    o_all = [ob, o1p, o1m, o2p, o2m]
    o_all.append(swap(jnp.concatenate([ob, o1p, o1m])))
    o_all.append(swap(jnp.concatenate([o2p, o2m])))
    return kv_all, q_all, o_all, tab


def local(tokens, modality, block_mask, q_weight, kv_weight, o_weight):
    y, zh, c = lax.axis_index("y"), lax.axis_index("zh"), lax.axis_index("c")
    at = (lax.axis_index("x"), zh * 4 + lax.axis_index("zl"), c, y)
    tables = [jnp.asarray(t) for t in rotary_tables()]
    kv = lax.dynamic_slice_in_dim(kv_weight, y * (2 * HD), 2 * HD, 2)
    kv_all, q_all, o_all, tab = gather(kv, q_weight, jnp.swapaxes(o_weight, 1, 2), at)
    small = (modality[0], block_mask[0], tab)
    q, k, v, o2a, o2b = head(*small, kv_all, q_all, o_all, tokens[0], tables)
    up = [(i, (i + 1) % NY) for i in range(NY)]
    down = [(i, (i - 1) % NY) for i in range(NY)]
    f32, half = jnp.float32, D // 2

    def add(a, b):
        return (a.astype(f32) + b.astype(f32)).astype(BF)

    far_a = lax.ppermute(o2a, "y", up)
    far_b = lax.ppermute(o2b, "y", down)
    o3, o1 = tail(3, 2, *small, o_all, q, k, v)
    p = jnp.concatenate([add(o1[:, :half], far_a), o1[:, half:]], axis=1)
    m = jnp.concatenate([o3[:, :half], add(o3[:, half:], far_b)], axis=1)
    p = lax.ppermute(p, "y", up)
    m = lax.ppermute(m, "y", down)
    o0 = tail(0, 1, *small, o_all, q, k, v)[0]
    return (o0.astype(f32) + p.astype(f32) + m.astype(f32)).astype(BF)[None]


def solution(mesh):
    fine = Mesh(mesh.devices.reshape(4, 4, 2, 4, 2), ("x", "zl", "c", "y", "zh"))
    dp = ("x", "zl", "c")
    mp = ("y", "zh")
    in_specs = (
        P(dp, None, None),
        P(dp, None),
        P(dp, None, None),
        P(None, dp, mp),
        P(None, dp, None),
        P(None, mp, dp),
    )
    return jax.shard_map(local, mesh=fine, in_specs=in_specs, out_specs=P(dp, mp, None), check_vma=False)
```

profile of v0, /device:TPU:32, one launch (start us, length us, event | category | flops | bytes accessed | tf_op | source)
XLA Modules:
  0.0 182.1 jit_solution(6712487089255864958)
XLA Ops:
  0.0 1.5 collective-permute-start
  3.3 2.0 %collective-permute-start.4 = (bf16[4,112,256]{2,1,0:T(8,128)(2,1)S(1)}, bf16[4,112,256]{2,1,0:T(8,128)(2,1)S(1)}, u32[]{:S(2)}, u32[]{:S(2)}) collective-permute-start(bf16[4,112,256]{2,1,0:T(8,128)(2,1)S(1)} %fusion.3), channel_id=1, source_target_pairs={{0,16},{16,32},{32,48},{48,1},{1,17},{17,33},{33,49},{49,0},{2,18}... | collective-permute-start | bytes 688136 | tf_op jit(solution)/shard_map/ppermute | solution.py:313
  5.4 1.7 collective-permute-start.1
  7.5 2.9 %collective-permute-done.1 = bf16[2,112,256]{2,1,0:T(8,128)(2,1)S(1)} collective-permute-done((bf16[2,112,256]{2,1,0:T(8,128)(2,1)}, bf16[2,112,256]{2,1,0:T(8,128)(2,1)S(1)}, u32[]{:S(2)}, u32[]{:S(2)}) %collective-permute-start.1) | collective-permute-done | bytes 114720 | tf_op jit(solution)/shard_map/ppermute | solution.py:308
  10.4 3.0 %collective-permute-start.3 = (bf16[112,256]{1,0:T(8,128)(2,1)S(1)}, bf16[112,256]{1,0:T(8,128)(2,1)S(1)}, u32[]{:S(2)}, u32[]{:S(2)}) collective-permute-start(bf16[112,256]{1,0:T(8,128)(2,1)S(1)} %slice_bitcast_fusion.6), channel_id=1, source_target_pairs={{0,192},{64,0},{128,64},{192,128},{1,193},{65,1},{129,65},{193,129... | collective-permute-start | bytes 172040 | tf_op jit(solution)/shard_map/ppermute | solution.py:308
  13.3 1.6 bitcast_dynamic-update-slice_fusion.2
  16.2 2.0 %collective-permute-start.5 = (bf16[3,112,256]{2,1,0:T(8,128)(2,1)S(1)}, bf16[3,112,256]{2,1,0:T(8,128)(2,1)S(1)}, u32[]{:S(2)}, u32[]{:S(2)}) collective-permute-start(bf16[3,112,256]{2,1,0:T(8,128)(2,1)S(1)} %slice.114), channel_id=1, source_target_pairs={{0,16},{16,32},{32,48},{48,1},{1,17},{17,33},{33,49},{49,0},{2,18}... | collective-permute-start | bytes 516104 | tf_op jit(solution)/shard_map/ppermute | solution.py:313
  18.2 2.2 %collective-permute-start.8 = (bf16[3,112,256]{2,1,0:T(8,128)(2,1)S(1)}, bf16[3,112,256]{2,1,0:T(8,128)(2,1)S(1)}, u32[]{:S(2)}, u32[]{:S(2)}) collective-permute-start(bf16[3,112,256]{2,1,0:T(8,128)(2,1)S(1)} %slice.116), channel_id=1, source_target_pairs={{0,49},{16,0},{32,16},{48,32},{1,48},{17,1},{33,17},{49,33},{2,51}... | collective-permute-start | bytes 516104 | tf_op jit(solution)/shard_map/ppermute | solution.py:313
  21.8 1.9 %collective-permute-done.5 = bf16[3,112,256]{2,1,0:T(8,128)(2,1)S(1)} collective-permute-done((bf16[3,112,256]{2,1,0:T(8,128)(2,1)S(1)}, bf16[3,112,256]{2,1,0:T(8,128)(2,1)S(1)}, u32[]{:S(2)}, u32[]{:S(2)}) %collective-permute-start.5) | collective-permute-done | bytes 172064 | tf_op jit(solution)/shard_map/ppermute | solution.py:313
  25.8 2.8 %collective-permute-start.15 = (bf16[2,4,112,256]{3,2,1,0:T(8,128)(2,1)S(1)}, bf16[2,4,112,256]{3,2,1,0:T(8,128)(2,1)S(1)}, u32[]{:S(2)}, u32[]{:S(2)}) collective-permute-start(bf16[2,4,112,256]{3,2,1,0:T(8,128)(2,1)S(1)} %pad_maximum_fusion.5.refs_0_), channel_id=1, source_target_pairs={{0,192},{64,0},{128,64},{192,128},{1,193},{65,1},{129,65},{193,129... | collective-permute-start | bytes 1376264 | tf_op jit(solution)/shard_map/ppermute | solution.py:308
  29.3 3.3 %collective-permute-start.6 = (bf16[2,112,256]{2,1,0:T(8,128)(2,1)S(1)}, bf16[2,112,256]{2,1,0:T(8,128)(2,1)S(1)}, u32[]{:S(2)}, u32[]{:S(2)}) collective-permute-start(bf16[2,112,256]{2,1,0:T(8,128)(2,1)S(1)} %slice.115), channel_id=1, source_target_pairs={{0,16},{16,32},{32,48},{48,1},{1,17},{17,33},{33,49},{49,0},{2,18}... | collective-permute-start | bytes 344072 | tf_op jit(solution)/shard_map/ppermute | solution.py:313
  34.9 4.9 %collective-permute-done.9 = bf16[2,112,256]{2,1,0:T(8,128)(2,1)S(1)} collective-permute-done((bf16[2,112,256]{2,1,0:T(8,128)(2,1)S(1)}, bf16[2,112,256]{2,1,0:T(8,128)(2,1)S(1)}, u32[]{:S(2)}, u32[]{:S(2)}) %collective-permute-start.9) | collective-permute-done | bytes 114720 | tf_op jit(solution)/shard_map/ppermute | solution.py:313
  39.9 2.0 %collective-permute-start.10 = (bf16[4,2,112,256]{3,2,1,0:T(8,128)(2,1)S(1)}, bf16[4,2,112,256]{3,2,1,0:T(8,128)(2,1)S(1)}, u32[]{:S(2)}, u32[]{:S(2)}) collective-permute-start(bf16[4,2,112,256]{3,2,1,0:T(8,128)(2,1)S(1)} %pad_maximum_fusion.4.refs_6_), channel_id=1, source_target_pairs={{0,16},{16,32},{32,48},{48,1},{1,17},{17,33},{33,49},{49,0},{2,18}... | collective-permute-start | bytes 1376264 | tf_op jit(solution)/shard_map/ppermute | solution.py:313
  41.9 2.0 %collective-permute-start.12 = (bf16[112,256]{1,0:T(8,128)(2,1)S(1)}, bf16[112,256]{1,0:T(8,128)(2,1)S(1)}, u32[]{:S(2)}, u32[]{:S(2)}) collective-permute-start(bf16[112,256]{1,0:T(8,128)(2,1)S(1)} %slice_bitcast_fusion.9), channel_id=1, source_target_pairs={{0,16},{16,32},{32,48},{48,1},{1,17},{17,33},{33,49},{49,0},{2,18}... | collective-permute-start | bytes 172040 | tf_op jit(solution)/shard_map/ppermute | solution.py:313
  45.3 3.7 %collective-permute-done.12 = bf16[112,256]{1,0:T(8,128)(2,1)S(1)} collective-permute-done((bf16[112,256]{1,0:T(8,128)(2,1)S(1)}, bf16[112,256]{1,0:T(8,128)(2,1)S(1)}, u32[]{:S(2)}, u32[]{:S(2)}) %collective-permute-start.12) | collective-permute-done | bytes 57376 | tf_op jit(solution)/shard_map/ppermute | solution.py:313
  50.1 3.0 %collective-permute-done.13 = bf16[112,256]{1,0:T(8,128)(2,1)S(1)} collective-permute-done((bf16[112,256]{1,0:T(8,128)(2,1)S(1)}, bf16[112,256]{1,0:T(8,128)(2,1)S(1)}, u32[]{:S(2)}, u32[]{:S(2)}) %collective-permute-start.13) | collective-permute-done | bytes 57376 | tf_op jit(solution)/shard_map/ppermute | solution.py:313
  54.0 3.2 %collective-permute-start.19 = (bf16[8,2,112,256]{3,2,1,0:T(8,128)(2,1)S(1)}, bf16[8,2,112,256]{3,2,1,0:T(8,128)(2,1)S(1)}, u32[]{:S(2)}, u32[]{:S(2)}) collective-permute-start(bf16[8,2,112,256]{3,2,1,0:T(8,128)(2,1)S(1)} %get-tuple-element.68.refs_17_.refs_0_), channel_id=1, source_target_pairs={{0,192},{64,0},{128,64},{192,128},{1,193},{65,1},{129,65},{193,129... | collective-permute-start | bytes 2752520 | tf_op jit(solution)/shard_map/ppermute | solution.py:308
  57.3 2.0 %collective-permute-start.16 = (bf16[4,2,112,256]{3,2,1,0:T(8,128)(2,1)S(1)}, bf16[4,2,112,256]{3,2,1,0:T(8,128)(2,1)S(1)}, u32[]{:S(2)}, u32[]{:S(2)}) collective-permute-start(bf16[4,2,112,256]{3,2,1,0:T(8,128)(2,1)S(1)} %collective-permute-done.10.refs_7_), channel_id=1, source_target_pairs={{0,16},{16,32},{32,48},{48,1},{1,17},{17,33},{33,49},{49,0},{2,18}... | collective-permute-start | bytes 1376264 | tf_op jit(solution)/shard_map/ppermute | solution.py:313
  62.7 6.7 %collective-permute-done.16.refs_9_ = bf16[4,2,112,256]{3,2,1,0:T(8,128)(2,1)S(1)} collective-permute-done((bf16[4,2,112,256]{3,2,1,0:T(8,128)(2,1)S(1)}, bf16[4,2,112,256]{3,2,1,0:T(8,128)(2,1)S(1)}, u32[]{:S(2)}, u32[]{:S(2)}) %collective-permute-start.16) | collective-permute-done | bytes 458784 | tf_op jit(solution)/shard_map/ppermute | solution.py:313
  69.4 1.3 collective-permute-start.27
  70.7 2.8 %collective-permute-start.20 = (bf16[4,2,112,256]{3,2,1,0:T(8,128)(2,1)S(1)}, bf16[4,2,112,256]{3,2,1,0:T(8,128)(2,1)S(1)}, u32[]{:S(2)}, u32[]{:S(2)}) collective-permute-start(bf16[4,2,112,256]{3,2,1,0:T(8,128)(2,1)S(1)} %collective-permute-done.16.refs_9_), channel_id=1, source_target_pairs={{0,16},{16,32},{32,48},{48,1},{1,17},{17,33},{33,49},{49,0},{2,18}... | collective-permute-start | bytes 1376264 | tf_op jit(solution)/shard_map/ppermute | solution.py:313
  73.9 2.3 %collective-permute-start.21 = (bf16[4,2,112,256]{3,2,1,0:T(8,128)(2,1)S(1)}, bf16[4,2,112,256]{3,2,1,0:T(8,128)(2,1)S(1)}, u32[]{:S(2)}, u32[]{:S(2)}) collective-permute-start(bf16[4,2,112,256]{3,2,1,0:T(8,128)(2,1)S(1)} %collective-permute-done.17.refs_10_), channel_id=1, source_target_pairs={{0,49},{16,0},{32,16},{48,32},{1,48},{17,1},{33,17},{49,33},{2,51}... | collective-permute-start | bytes 1376264 | tf_op jit(solution)/shard_map/ppermute | solution.py:313
  78.5 1.3 collective-permute-done.20.refs_11_
  79.8 2.7 %collective-permute-done.21.refs_12_ = bf16[4,2,112,256]{3,2,1,0:T(8,128)(2,1)S(1)} collective-permute-done((bf16[4,2,112,256]{3,2,1,0:T(8,128)(2,1)S(1)}, bf16[4,2,112,256]{3,2,1,0:T(8,128)(2,1)S(1)}, u32[]{:S(2)}, u32[]{:S(2)}) %collective-permute-start.21) | collective-permute-done | bytes 458784 | tf_op jit(solution)/shard_map/ppermute | solution.py:313
  82.5 1.1 constant_dynamic-update-slice_fusion.1
  86.0 3.6 %collective-permute-start.29 = (bf16[2,2,112,256]{3,2,1,0:T(8,128)(2,1)S(1)}, bf16[2,2,112,256]{3,2,1,0:T(8,128)(2,1)S(1)}, u32[]{:S(2)}, u32[]{:S(2)}) collective-permute-start(bf16[2,2,112,256]{3,2,1,0:T(8,128)(2,1)S(1)} %slice.106), channel_id=1, source_target_pairs={{0,16},{16,32},{32,48},{48,1},{1,17},{17,33},{33,49},{49,0},{2,18}... | collective-permute-start | bytes 688136 | tf_op jit(solution)/shard_map/ppermute | solution.py:313
  90.8 1.1 slice.102
  92.0 1.0 slice.103
  93.1 1.6 collective-permute-done.29.refs_13_
  94.7 4.7 %collective-permute-done.30.refs_14_ = bf16[2,2,112,256]{3,2,1,0:T(8,128)(2,1)S(1)} collective-permute-done((bf16[2,2,112,256]{3,2,1,0:T(8,128)(2,1)S(1)}, bf16[2,2,112,256]{3,2,1,0:T(8,128)(2,1)S(1)}, u32[]{:S(2)}, u32[]{:S(2)}) %collective-permute-start.30) | collective-permute-done | bytes 229408 | tf_op jit(solution)/shard_map/ppermute | solution.py:313
  100.0 1.3 pad_maximum_fusion
  101.3 4.0 %collective-permute-done.22.refs_20_.refs_3_ = bf16[4,2,112,256]{3,2,1,0:T(8,128)(2,1)S(1)} collective-permute-done((bf16[4,2,112,256]{3,2,1,0:T(8,128)(2,1)S(1)}, bf16[4,2,112,256]{3,2,1,0:T(8,128)(2,1)S(1)}, u32[]{:S(2)}, u32[]{:S(2)}) %collective-permute-start.22) | collective-permute-done | bytes 458784 | tf_op jit(solution)/shard_map/ppermute | solution.py:308
  105.4 5.7 %collective-permute-done.23.refs_21_.refs_4_ = bf16[4,2,112,256]{3,2,1,0:T(8,128)(2,1)S(1)} collective-permute-done((bf16[4,2,112,256]{3,2,1,0:T(8,128)(2,1)S(1)}, bf16[4,2,112,256]{3,2,1,0:T(8,128)(2,1)S(1)}, u32[]{:S(2)}, u32[]{:S(2)}) %collective-permute-start.23) | collective-permute-done | bytes 458784 | tf_op jit(solution)/shard_map/ppermute | solution.py:308
  111.8 1.0 pad_maximum_fusion.1
  114.1 1.6 collective-permute-done.25.refs_23_.refs_6_
  115.7 1.5 copy-done
  117.2 15.6 %head.1 = (bf16[4,512,128]{2,1,0:T(8,128)(2,1)}, bf16[1024,128]{1,0:T(8,128)(2,1)}, bf16[1024,128]{1,0:T(8,128)(2,1)}, bf16[128,1792]{1,0:T(8,128)(2,1)}, bf16[128,1792]{1,0:T(8,128)(2,1)}) custom-call(s32[8]{0:T(128)} %bitcast.107, s32[8,8]{1,0:T(8,128)} %bitcast.104, s32[162]{0:T(256)} %concatenate.30.tab, bf16[2,4,112,256]{3,2,1,0:T(8,128)(2,1)} %copy-done.13, ...), custom_call_target="tpu_custom_call" | custom-call | flops 3758096384 | bytes 25690112 | tf_op jit(solution)/shard_map/head/pallas_call | solution.py:253
  132.8 1.7 collective-permute-start.33
  134.5 10.1 %tail.3 = bf16[2,128,3584]{2,1,0:T(8,128)(2,1)} custom-call(s32[8]{0:T(128)} %bitcast.108, s32[8,8]{1,0:T(8,128)} %bitcast.105, s32[162]{0:T(256)} %concatenate.30.tab, bf16[8,2,112,256]{3,2,1,0:T(8,128)(2,1)} %copy-done.3, bf16[8,2,112,256]{3,2,1,0:T(8,128)(2,1)} %copy-done.1, bf16[8,2,112,256]{3,2,1,0:T(8,128)(2,1)} %copy-done.2, ...), custom_call_target="tpu_custom_call" | custom-call | flops 1476395008 | bytes 7340032 | tf_op jit(solution)/shard_map/tail/pallas_call | solution.py:287
  144.6 1.6 slice_bitcast_fusion.1
  146.3 1.7 collective-permute-start.35
  148.7 8.8 %collective-permute-done.35 = bf16[128,1792]{1,0:T(8,128)(2,1)S(1)} collective-permute-done((bf16[128,1792]{1,0:T(8,128)(2,1)S(1)}, bf16[128,1792]{1,0:T(8,128)(2,1)S(1)}, u32[]{:S(2)}, u32[]{:S(2)}) %collective-permute-start.35) | collective-permute-done | bytes 458784 | tf_op jit(solution)/shard_map/ppermute | solution.py:377
  157.7 1.0 pad_maximum_fusion.3
  158.7 2.9 %collective-permute-start.36 = (bf16[128,3584]{1,0:T(8,128)(2,1)}, bf16[128,3584]{1,0:T(8,128)(2,1)S(1)}, u32[]{:S(2)}, u32[]{:S(2)}) collective-permute-start(bf16[128,3584]{1,0:T(8,128)(2,1)} %pad_maximum_fusion.3), channel_id=1, source_target_pairs={{0,6},{2,0},{4,2},{6,4},{1,7},{3,1},{5,3},{7,5},{8,14},{10,8},{12,... | collective-permute-start | bytes 2752520 | tf_op jit(solution)/shard_map/ppermute | solution.py:382
  161.6 7.3 %tail.2 = bf16[1,128,3584]{2,1,0:T(8,128)(2,1)} custom-call(s32[8]{0:T(128)} %bitcast.109, s32[8,8]{1,0:T(8,128)} %bitcast.106, s32[162]{0:T(256)} %concatenate.30.tab, bf16[8,2,112,256]{3,2,1,0:T(8,128)(2,1)} %copy-done.3, bf16[8,2,112,256]{3,2,1,0:T(8,128)(2,1)} %copy-done.1, bf16[8,2,112,256]{3,2,1,0:T(8,128)(2,1)} %copy-done.2, ...), custom_call_target="tpu_custom_call" | custom-call | flops 738197504 | bytes 7340032 | tf_op jit(solution)/shard_map/tail/pallas_call | solution.py:287
  168.9 1.4 collective-permute-done.34
  170.4 9.3 %collective-permute-done.36 = bf16[128,3584]{1,0:T(8,128)(2,1)S(1)} collective-permute-done((bf16[128,3584]{1,0:T(8,128)(2,1)}, bf16[128,3584]{1,0:T(8,128)(2,1)S(1)}, u32[]{:S(2)}, u32[]{:S(2)}) %collective-permute-start.36) | collective-permute-done | bytes 917536 | tf_op jit(solution)/shard_map/ppermute | solution.py:382
  179.7 2.4 %fusion.2 = bf16[1,128,3584]{2,1,0:T(8,128)(2,1)} fusion(bf16[128,3584]{1,0:T(8,128)(2,1)S(1)} %collective-permute-done.36, bf16[128,3584]{1,0:T(8,128)(2,1)S(1)} %collective-permute-done.34, bf16[1,128,3584]{2,1,0:T(8,128)(2,1)} %tail.2), kind=kLoop, calls=%fused_computation.4 | loop fusion | flops 2752512 | bytes 3670016 | tf_op jit(solution)/shard_map/broadcast_in_dim | solution.py:384
  (155 shorter events, 26.3 us)
Async XLA Ops:
  0.0 7.1 %collective-permute-start = (bf16[2,112,256]{2,1,0:T(8,128)(2,1)}, bf16[2,112,256]{2,1,0:T(8,128)(2,1)S(1)}, u32[]{:S(2)}, u32[]{:S(2)}) collective-permute-start(bf16[2,112,256]{2,1,0:T(8,128)(2,1)} %param.19), channel_id=1, source_target_pairs={{0,64},{64,128},{128,192},{192,0},{1,65},{65,129},{129,193},{193,1... | collective-permute-start | bytes 344072 | tf_op jit(solution)/shard_map/ppermute | solution.py:308
  3.3 12.9 %collective-permute-start.4 = (bf16[4,112,256]{2,1,0:T(8,128)(2,1)S(1)}, bf16[4,112,256]{2,1,0:T(8,128)(2,1)S(1)}, u32[]{:S(2)}, u32[]{:S(2)}) collective-permute-start(bf16[4,112,256]{2,1,0:T(8,128)(2,1)S(1)} %fusion.3), channel_id=1, source_target_pairs={{0,16},{16,32},{32,48},{48,1},{1,17},{17,33},{33,49},{49,0},{2,18}... | collective-permute-start | bytes 688136 | tf_op jit(solution)/shard_map/ppermute | solution.py:313
  5.3 12.9 %collective-permute-start.7 = (bf16[4,112,256]{2,1,0:T(8,128)(2,1)S(1)}, bf16[4,112,256]{2,1,0:T(8,128)(2,1)S(1)}, u32[]{:S(2)}, u32[]{:S(2)}) collective-permute-start(bf16[4,112,256]{2,1,0:T(8,128)(2,1)S(1)} %fusion.3), channel_id=1, source_target_pairs={{0,49},{16,0},{32,16},{48,32},{1,48},{17,1},{33,17},{49,33},{2,51}... | collective-permute-start | bytes 688136 | tf_op jit(solution)/shard_map/ppermute | solution.py:313
  5.4 5.0 %collective-permute-start.1 = (bf16[2,112,256]{2,1,0:T(8,128)(2,1)}, bf16[2,112,256]{2,1,0:T(8,128)(2,1)S(1)}, u32[]{:S(2)}, u32[]{:S(2)}) collective-permute-start(bf16[2,112,256]{2,1,0:T(8,128)(2,1)} %param.19), channel_id=1, source_target_pairs={{0,192},{64,0},{128,64},{192,128},{1,193},{65,1},{129,65},{193,129... | collective-permute-start | bytes 344072 | tf_op jit(solution)/shard_map/ppermute | solution.py:308
  7.1 7.8 %collective-permute-start.2 = (bf16[112,256]{1,0:T(8,128)(2,1)S(1)}, bf16[112,256]{1,0:T(8,128)(2,1)S(1)}, u32[]{:S(2)}, u32[]{:S(2)}) collective-permute-start(bf16[112,256]{1,0:T(8,128)(2,1)S(1)} %slice_bitcast_fusion.7), channel_id=1, source_target_pairs={{0,64},{64,128},{128,192},{192,0},{1,65},{65,129},{129,193},{193,1... | collective-permute-start | bytes 172040 | tf_op jit(solution)/shard_map/ppermute | solution.py:308
  10.4 4.8 %collective-permute-start.3 = (bf16[112,256]{1,0:T(8,128)(2,1)S(1)}, bf16[112,256]{1,0:T(8,128)(2,1)S(1)}, u32[]{:S(2)}, u32[]{:S(2)}) collective-permute-start(bf16[112,256]{1,0:T(8,128)(2,1)S(1)} %slice_bitcast_fusion.6), channel_id=1, source_target_pairs={{0,192},{64,0},{128,64},{192,128},{1,193},{65,1},{129,65},{193,129... | collective-permute-start | bytes 172040 | tf_op jit(solution)/shard_map/ppermute | solution.py:308
  16.2 33.1 %copy-start.6 = (bf16[4,2,112,256]{3,2,1,0:T(8,128)(2,1)}, bf16[4,2,112,256]{3,2,1,0:T(8,128)(2,1)S(1)}, u32[]{:S(2)}) copy-start(bf16[4,2,112,256]{3,2,1,0:T(8,128)(2,1)S(1)} %pad_maximum_fusion.4.refs_6_) | copy-start | bytes 1376260
  16.2 7.5 %collective-permute-start.5 = (bf16[3,112,256]{2,1,0:T(8,128)(2,1)S(1)}, bf16[3,112,256]{2,1,0:T(8,128)(2,1)S(1)}, u32[]{:S(2)}, u32[]{:S(2)}) collective-permute-start(bf16[3,112,256]{2,1,0:T(8,128)(2,1)S(1)} %slice.114), channel_id=1, source_target_pairs={{0,16},{16,32},{32,48},{48,1},{1,17},{17,33},{33,49},{49,0},{2,18}... | collective-permute-start | bytes 516104 | tf_op jit(solution)/shard_map/ppermute | solution.py:313
  18.2 6.5 %collective-permute-start.8 = (bf16[3,112,256]{2,1,0:T(8,128)(2,1)S(1)}, bf16[3,112,256]{2,1,0:T(8,128)(2,1)S(1)}, u32[]{:S(2)}, u32[]{:S(2)}) collective-permute-start(bf16[3,112,256]{2,1,0:T(8,128)(2,1)S(1)} %slice.116), channel_id=1, source_target_pairs={{0,49},{16,0},{32,16},{48,32},{1,48},{17,1},{33,17},{49,33},{2,51}... | collective-permute-start | bytes 516104 | tf_op jit(solution)/shard_map/ppermute | solution.py:313
  24.8 35.3 %copy-start.13 = (bf16[2,4,112,256]{3,2,1,0:T(8,128)(2,1)}, bf16[2,4,112,256]{3,2,1,0:T(8,128)(2,1)S(1)}, u32[]{:S(2)}) copy-start(bf16[2,4,112,256]{3,2,1,0:T(8,128)(2,1)S(1)} %pad_maximum_fusion.5.refs_0_) | copy-start | bytes 1376260
  24.8 28.4 %collective-permute-start.14 = (bf16[2,4,112,256]{3,2,1,0:T(8,128)(2,1)S(1)}, bf16[2,4,112,256]{3,2,1,0:T(8,128)(2,1)S(1)}, u32[]{:S(2)}, u32[]{:S(2)}) collective-permute-start(bf16[2,4,112,256]{3,2,1,0:T(8,128)(2,1)S(1)} %pad_maximum_fusion.5.refs_0_), channel_id=1, source_target_pairs={{0,64},{64,128},{128,192},{192,0},{1,65},{65,129},{129,193},{193,1... | collective-permute-start | bytes 1376264 | tf_op jit(solution)/shard_map/ppermute | solution.py:308
  25.8 27.4 %collective-permute-start.15 = (bf16[2,4,112,256]{3,2,1,0:T(8,128)(2,1)S(1)}, bf16[2,4,112,256]{3,2,1,0:T(8,128)(2,1)S(1)}, u32[]{:S(2)}, u32[]{:S(2)}) collective-permute-start(bf16[2,4,112,256]{3,2,1,0:T(8,128)(2,1)S(1)} %pad_maximum_fusion.5.refs_0_), channel_id=1, source_target_pairs={{0,192},{64,0},{128,64},{192,128},{1,193},{65,1},{129,65},{193,129... | collective-permute-start | bytes 1376264 | tf_op jit(solution)/shard_map/ppermute | solution.py:308
  29.3 5.7 %collective-permute-start.6 = (bf16[2,112,256]{2,1,0:T(8,128)(2,1)S(1)}, bf16[2,112,256]{2,1,0:T(8,128)(2,1)S(1)}, u32[]{:S(2)}, u32[]{:S(2)}) collective-permute-start(bf16[2,112,256]{2,1,0:T(8,128)(2,1)S(1)} %slice.115), channel_id=1, source_target_pairs={{0,16},{16,32},{32,48},{48,1},{1,17},{17,33},{33,49},{49,0},{2,18}... | collective-permute-start | bytes 344072 | tf_op jit(solution)/shard_map/ppermute | solution.py:313
  32.6 7.3 %collective-permute-start.9 = (bf16[2,112,256]{2,1,0:T(8,128)(2,1)S(1)}, bf16[2,112,256]{2,1,0:T(8,128)(2,1)S(1)}, u32[]{:S(2)}, u32[]{:S(2)}) collective-permute-start(bf16[2,112,256]{2,1,0:T(8,128)(2,1)S(1)} %slice.117), channel_id=1, source_target_pairs={{0,49},{16,0},{32,16},{48,32},{1,48},{17,1},{33,17},{49,33},{2,51}... | collective-permute-start | bytes 344072 | tf_op jit(solution)/shard_map/ppermute | solution.py:313
  39.9 13.3 %collective-permute-start.10 = (bf16[4,2,112,256]{3,2,1,0:T(8,128)(2,1)S(1)}, bf16[4,2,112,256]{3,2,1,0:T(8,128)(2,1)S(1)}, u32[]{:S(2)}, u32[]{:S(2)}) collective-permute-start(bf16[4,2,112,256]{3,2,1,0:T(8,128)(2,1)S(1)} %pad_maximum_fusion.4.refs_6_), channel_id=1, source_target_pairs={{0,16},{16,32},{32,48},{48,1},{1,17},{17,33},{33,49},{49,0},{2,18}... | collective-permute-start | bytes 1376264 | tf_op jit(solution)/shard_map/ppermute | solution.py:313
  41.9 11.3 %collective-permute-start.11 = (bf16[4,2,112,256]{3,2,1,0:T(8,128)(2,1)S(1)}, bf16[4,2,112,256]{3,2,1,0:T(8,128)(2,1)S(1)}, u32[]{:S(2)}, u32[]{:S(2)}) collective-permute-start(bf16[4,2,112,256]{3,2,1,0:T(8,128)(2,1)S(1)} %pad_maximum_fusion.4.refs_6_), channel_id=1, source_target_pairs={{0,49},{16,0},{32,16},{48,32},{1,48},{17,1},{33,17},{49,33},{2,51}... | collective-permute-start | bytes 1376264 | tf_op jit(solution)/shard_map/ppermute | solution.py:313
  41.9 7.1 %collective-permute-start.12 = (bf16[112,256]{1,0:T(8,128)(2,1)S(1)}, bf16[112,256]{1,0:T(8,128)(2,1)S(1)}, u32[]{:S(2)}, u32[]{:S(2)}) collective-permute-start(bf16[112,256]{1,0:T(8,128)(2,1)S(1)} %slice_bitcast_fusion.9), channel_id=1, source_target_pairs={{0,16},{16,32},{32,48},{48,1},{1,17},{17,33},{33,49},{49,0},{2,18}... | collective-permute-start | bytes 172040 | tf_op jit(solution)/shard_map/ppermute | solution.py:313
  49.0 4.2 %collective-permute-start.13 = (bf16[112,256]{1,0:T(8,128)(2,1)S(1)}, bf16[112,256]{1,0:T(8,128)(2,1)S(1)}, u32[]{:S(2)}, u32[]{:S(2)}) collective-permute-start(bf16[112,256]{1,0:T(8,128)(2,1)S(1)} %slice_bitcast_fusion.8), channel_id=1, source_target_pairs={{0,49},{16,0},{32,16},{48,32},{1,48},{17,1},{33,17},{49,33},{2,51}... | collective-permute-start | bytes 172040 | tf_op jit(solution)/shard_map/ppermute | solution.py:313
  54.0 24.4 %collective-permute-start.18 = (bf16[8,2,112,256]{3,2,1,0:T(8,128)(2,1)S(1)}, bf16[8,2,112,256]{3,2,1,0:T(8,128)(2,1)S(1)}, u32[]{:S(2)}, u32[]{:S(2)}) collective-permute-start(bf16[8,2,112,256]{3,2,1,0:T(8,128)(2,1)S(1)} %get-tuple-element.68.refs_17_.refs_0_), channel_id=1, source_target_pairs={{0,64},{64,128},{128,192},{192,0},{1,65},{65,129},{129,193},{193,1... | collective-permute-start | bytes 2752520 | tf_op jit(solution)/shard_map/ppermute | solution.py:308
  54.0 24.4 %collective-permute-start.19 = (bf16[8,2,112,256]{3,2,1,0:T(8,128)(2,1)S(1)}, bf16[8,2,112,256]{3,2,1,0:T(8,128)(2,1)S(1)}, u32[]{:S(2)}, u32[]{:S(2)}) collective-permute-start(bf16[8,2,112,256]{3,2,1,0:T(8,128)(2,1)S(1)} %get-tuple-element.68.refs_17_.refs_0_), channel_id=1, source_target_pairs={{0,192},{64,0},{128,64},{192,128},{1,193},{65,1},{129,65},{193,129... | collective-permute-start | bytes 2752520 | tf_op jit(solution)/shard_map/ppermute | solution.py:308
  57.3 12.1 %collective-permute-start.16 = (bf16[4,2,112,256]{3,2,1,0:T(8,128)(2,1)S(1)}, bf16[4,2,112,256]{3,2,1,0:T(8,128)(2,1)S(1)}, u32[]{:S(2)}, u32[]{:S(2)}) collective-permute-start(bf16[4,2,112,256]{3,2,1,0:T(8,128)(2,1)S(1)} %collective-permute-done.10.refs_7_), channel_id=1, source_target_pairs={{0,16},{16,32},{32,48},{48,1},{1,17},{17,33},{33,49},{49,0},{2,18}... | collective-permute-start | bytes 1376264 | tf_op jit(solution)/shard_map/ppermute | solution.py:313
  59.3 11.4 %collective-permute-start.17 = (bf16[4,2,112,256]{3,2,1,0:T(8,128)(2,1)S(1)}, bf16[4,2,112,256]{3,2,1,0:T(8,128)(2,1)S(1)}, u32[]{:S(2)}, u32[]{:S(2)}) collective-permute-start(bf16[4,2,112,256]{3,2,1,0:T(8,128)(2,1)S(1)} %collective-permute-done.11.refs_8_), channel_id=1, source_target_pairs={{0,49},{16,0},{32,16},{48,32},{1,48},{17,1},{33,17},{49,33},{2,51}... | collective-permute-start | bytes 1376264 | tf_op jit(solution)/shard_map/ppermute | solution.py:313
  60.9 12.9 %collective-permute-start.26 = (bf16[4,112,256]{2,1,0:T(8,128)(2,1)S(1)}, bf16[4,112,256]{2,1,0:T(8,128)(2,1)S(1)}, u32[]{:S(2)}, u32[]{:S(2)}) collective-permute-start(bf16[4,112,256]{2,1,0:T(8,128)(2,1)S(1)} %slice_bitcast_fusion.3), channel_id=1, source_target_pairs={{0,64},{64,128},{128,192},{192,0},{1,65},{65,129},{129,193},{193,1... | collective-permute-start | bytes 688136 | tf_op jit(solution)/shard_map/ppermute | solution.py:308
  69.4 13.1 %copy-start.16 = (bf16[4,2,112,256]{3,2,1,0:T(8,128)(2,1)}, bf16[4,2,112,256]{3,2,1,0:T(8,128)(2,1)S(1)}, u32[]{:S(2)}) copy-start(bf16[4,2,112,256]{3,2,1,0:T(8,128)(2,1)S(1)} %collective-permute-done.16.refs_9_) | copy-start | bytes 1376260
  69.4 7.5 %collective-permute-start.27 = (bf16[4,112,256]{2,1,0:T(8,128)(2,1)S(1)}, bf16[4,112,256]{2,1,0:T(8,128)(2,1)S(1)}, u32[]{:S(2)}, u32[]{:S(2)}) collective-permute-start(bf16[4,112,256]{2,1,0:T(8,128)(2,1)S(1)} %slice_bitcast_fusion.2), channel_id=1, source_target_pairs={{0,192},{64,0},{128,64},{192,128},{1,193},{65,1},{129,65},{193,129... | collective-permute-start | bytes 688136 | tf_op jit(solution)/shard_map/ppermute | solution.py:308
  70.7 13.9 %copy-start.17 = (bf16[4,2,112,256]{3,2,1,0:T(8,128)(2,1)}, bf16[4,2,112,256]{3,2,1,0:T(8,128)(2,1)S(1)}, u32[]{:S(2)}) copy-start(bf16[4,2,112,256]{3,2,1,0:T(8,128)(2,1)S(1)} %collective-permute-done.17.refs_10_) | copy-start | bytes 1376260
  70.7 9.2 %collective-permute-start.20 = (bf16[4,2,112,256]{3,2,1,0:T(8,128)(2,1)S(1)}, bf16[4,2,112,256]{3,2,1,0:T(8,128)(2,1)S(1)}, u32[]{:S(2)}, u32[]{:S(2)}) collective-permute-start(bf16[4,2,112,256]{3,2,1,0:T(8,128)(2,1)S(1)} %collective-permute-done.16.refs_9_), channel_id=1, source_target_pairs={{0,16},{16,32},{32,48},{48,1},{1,17},{17,33},{33,49},{49,0},{2,18}... | collective-permute-start | bytes 1376264 | tf_op jit(solution)/shard_map/ppermute | solution.py:313
  73.9 10.7 %copy-start.18 = (bf16[4,112,256]{2,1,0:T(8,128)(2,1)}, bf16[4,112,256]{2,1,0:T(8,128)(2,1)S(1)}, u32[]{:S(2)}) copy-start(bf16[4,112,256]{2,1,0:T(8,128)(2,1)S(1)} %collective-permute-done.26.refs_3_) | copy-start | bytes 688132
  73.9 8.6 %collective-permute-start.21 = (bf16[4,2,112,256]{3,2,1,0:T(8,128)(2,1)S(1)}, bf16[4,2,112,256]{3,2,1,0:T(8,128)(2,1)S(1)}, u32[]{:S(2)}, u32[]{:S(2)}) collective-permute-start(bf16[4,2,112,256]{3,2,1,0:T(8,128)(2,1)S(1)} %collective-permute-done.17.refs_10_), channel_id=1, source_target_pairs={{0,49},{16,0},{32,16},{48,32},{1,48},{17,1},{33,17},{49,33},{2,51}... | collective-permute-start | bytes 1376264 | tf_op jit(solution)/shard_map/ppermute | solution.py:313
  84.6 31.1 %collective-permute-start.24 = (bf16[24,2,112,256]{3,2,1,0:T(8,128)(2,1)}, bf16[24,2,112,256]{3,2,1,0:T(8,128)(2,1)S(1)}, u32[]{:S(2)}, u32[]{:S(2)}) collective-permute-start(bf16[24,2,112,256]{3,2,1,0:T(8,128)(2,1)} %constant_dynamic-update-slice_fusion), channel_id=1, source_target_pairs={{0,8},{8,0},{1,9},{9,1},{2,10},{10,2},{3,11},{11,3},{4,12},{12,4},... | collective-permute-start | bytes 8257544 | tf_op jit(solution)/shard_map/ppermute | solution.py:317
  85.5 30.2 %collective-permute-start.31 = (bf16[20,2,112,256]{3,2,1,0:T(8,128)(2,1)}, bf16[20,2,112,256]{3,2,1,0:T(8,128)(2,1)}, u32[]{:S(2)}, u32[]{:S(2)}) collective-permute-start(bf16[20,2,112,256]{3,2,1,0:T(8,128)(2,1)} %constant_dynamic-update-slice_fusion.6), channel_id=1, source_target_pairs={{0,8},{8,0},{1,9},{9,1},{2,10},{10,2},{3,11},{11,3},{4,12},{12,4},... | collective-permute-start | bytes 6881288 | tf_op jit(solution)/shard_map/ppermute | solution.py:317
  86.0 14.0 %copy-start.12 = (bf16[4,2,112,256]{3,2,1,0:T(8,128)(2,1)S(1)}, bf16[4,2,112,256]{3,2,1,0:T(8,128)(2,1)}, u32[]{:S(2)}) copy-start(bf16[4,2,112,256]{3,2,1,0:T(8,128)(2,1)} %copy-done.11) | copy-start | bytes 1376260
  86.0 14.0 %copy-start.10 = (bf16[4,2,112,256]{3,2,1,0:T(8,128)(2,1)S(1)}, bf16[4,2,112,256]{3,2,1,0:T(8,128)(2,1)}, u32[]{:S(2)}) copy-start(bf16[4,2,112,256]{3,2,1,0:T(8,128)(2,1)} %copy-done.9) | copy-start | bytes 1376260
  86.0 8.7 %collective-permute-start.29 = (bf16[2,2,112,256]{3,2,1,0:T(8,128)(2,1)S(1)}, bf16[2,2,112,256]{3,2,1,0:T(8,128)(2,1)S(1)}, u32[]{:S(2)}, u32[]{:S(2)}) collective-permute-start(bf16[2,2,112,256]{3,2,1,0:T(8,128)(2,1)S(1)} %slice.106), channel_id=1, source_target_pairs={{0,16},{16,32},{32,48},{48,1},{1,17},{17,33},{33,49},{49,0},{2,18}... | collective-permute-start | bytes 688136 | tf_op jit(solution)/shard_map/ppermute | solution.py:313
  90.6 8.8 %collective-permute-start.30 = (bf16[2,2,112,256]{3,2,1,0:T(8,128)(2,1)S(1)}, bf16[2,2,112,256]{3,2,1,0:T(8,128)(2,1)S(1)}, u32[]{:S(2)}, u32[]{:S(2)}) collective-permute-start(bf16[2,2,112,256]{3,2,1,0:T(8,128)(2,1)S(1)} %slice.107), channel_id=1, source_target_pairs={{0,49},{16,0},{32,16},{48,32},{1,48},{17,1},{33,17},{49,33},{2,51}... | collective-permute-start | bytes 688136 | tf_op jit(solution)/shard_map/ppermute | solution.py:313
  90.8 14.5 %copy-start.24 = (s32[1,1,8]{2,1,0:T(1,128)S(1)}, s32[1,1,8]{2,1,0:T(1,128)}, u32[]{:S(2)}) copy-start(s32[1,1,8]{2,1,0:T(1,128)} %constant.19.clone) | copy-start | bytes 100
  91.9 13.5 %collective-permute-start.22 = (bf16[4,2,112,256]{3,2,1,0:T(8,128)(2,1)S(1)}, bf16[4,2,112,256]{3,2,1,0:T(8,128)(2,1)S(1)}, u32[]{:S(2)}, u32[]{:S(2)}) collective-permute-start(bf16[4,2,112,256]{3,2,1,0:T(8,128)(2,1)S(1)} %slice.102), channel_id=1, source_target_pairs={{0,64},{64,128},{128,192},{192,0},{1,65},{65,129},{129,193},{193,1... | collective-permute-start | bytes 1376264 | tf_op jit(solution)/shard_map/ppermute | solution.py:308
  94.7 18.1 %copy-start.20 = (bf16[2,2,112,256]{3,2,1,0:T(8,128)(2,1)}, bf16[2,2,112,256]{3,2,1,0:T(8,128)(2,1)S(1)}, u32[]{:S(2)}) copy-start(bf16[2,2,112,256]{3,2,1,0:T(8,128)(2,1)S(1)} %collective-permute-done.29.refs_13_) | copy-start | bytes 688132
  94.7 19.3 %collective-permute-start.28 = (bf16[8,4,112,256]{3,2,1,0:T(8,128)(2,1)}, bf16[8,4,112,256]{3,2,1,0:T(8,128)(2,1)}, u32[]{:S(2)}, u32[]{:S(2)}) collective-permute-start(bf16[8,4,112,256]{3,2,1,0:T(8,128)(2,1)} %bitcast_dynamic-update-slice_fusion), channel_id=1, source_target_pairs={{0,8},{8,0},{1,9},{9,1},{2,10},{10,2},{3,11},{11,3},{4,12},{12,4},... | collective-permute-start | bytes 5505032 | tf_op jit(solution)/shard_map/ppermute | solution.py:317
  99.5 13.4 %copy-start.21 = (bf16[2,2,112,256]{3,2,1,0:T(8,128)(2,1)}, bf16[2,2,112,256]{3,2,1,0:T(8,128)(2,1)S(1)}, u32[]{:S(2)}) copy-start(bf16[2,2,112,256]{3,2,1,0:T(8,128)(2,1)S(1)} %collective-permute-done.30.refs_14_) | copy-start | bytes 688132
  99.5 11.6 %collective-permute-start.23 = (bf16[4,2,112,256]{3,2,1,0:T(8,128)(2,1)S(1)}, bf16[4,2,112,256]{3,2,1,0:T(8,128)(2,1)S(1)}, u32[]{:S(2)}, u32[]{:S(2)}) collective-permute-start(bf16[4,2,112,256]{3,2,1,0:T(8,128)(2,1)S(1)} %slice.103), channel_id=1, source_target_pairs={{0,192},{64,0},{128,64},{192,128},{1,193},{65,1},{129,65},{193,129... | collective-permute-start | bytes 1376264 | tf_op jit(solution)/shard_map/ppermute | solution.py:308
  100.0 13.2 %copy-start.23 = (s32[1,8,1]{1,2,0:T(1,128)S(1)}, s32[1,8,1]{1,2,0:T(1,128)}, u32[]{:S(2)}) copy-start(s32[1,8,1]{1,2,0:T(1,128)} %constant.17.clone) | copy-start | bytes 100
  105.3 10.4 %collective-permute-start.32 = (bf16[12,2,112,256]{3,2,1,0:T(8,128)(2,1)}, bf16[12,2,112,256]{3,2,1,0:T(8,128)(2,1)}, u32[]{:S(2)}, u32[]{:S(2)}) collective-permute-start(bf16[12,2,112,256]{3,2,1,0:T(8,128)(2,1)} %pad_maximum_fusion), channel_id=1, source_target_pairs={{0,8},{8,0},{1,9},{9,1},{2,10},{10,2},{3,11},{11,3},{4,12},{12,4},... | collective-permute-start | bytes 4128776 | tf_op jit(solution)/shard_map/ppermute | solution.py:317
  112.9 2.8 %collective-permute-start.25 = (bf16[8,2,112,256]{3,2,1,0:T(8,128)(2,1)}, bf16[8,2,112,256]{3,2,1,0:T(8,128)(2,1)}, u32[]{:S(2)}, u32[]{:S(2)}) collective-permute-start(bf16[8,2,112,256]{3,2,1,0:T(8,128)(2,1)} %pad_maximum_fusion.1), channel_id=1, source_target_pairs={{0,8},{8,0},{1,9},{9,1},{2,10},{10,2},{3,11},{11,3},{4,12},{12,4},... | collective-permute-start | bytes 2752520 | tf_op jit(solution)/shard_map/ppermute | solution.py:317
  132.8 15.3 %collective-permute-start.33 = (bf16[128,1792]{1,0:T(8,128)(2,1)}, bf16[128,1792]{1,0:T(8,128)(2,1)S(1)}, u32[]{:S(2)}, u32[]{:S(2)}) collective-permute-start(bf16[128,1792]{1,0:T(8,128)(2,1)} %get-tuple-element.49), channel_id=1, source_target_pairs={{0,2},{2,4},{4,6},{6,0},{1,3},{3,5},{5,7},{7,1},{8,10},{10,12},{12... | collective-permute-start | bytes 1376264 | tf_op jit(solution)/shard_map/ppermute | solution.py:376
  146.3 11.2 %collective-permute-start.35 = (bf16[128,1792]{1,0:T(8,128)(2,1)S(1)}, bf16[128,1792]{1,0:T(8,128)(2,1)S(1)}, u32[]{:S(2)}, u32[]{:S(2)}) collective-permute-start(bf16[128,1792]{1,0:T(8,128)(2,1)S(1)} %copy-done.25), channel_id=1, source_target_pairs={{0,6},{2,0},{4,2},{6,4},{1,7},{3,1},{5,3},{7,5},{8,14},{10,8},{12,... | collective-permute-start | bytes 1376264 | tf_op jit(solution)/shard_map/ppermute | solution.py:377
  148.3 22.1 %collective-permute-start.34 = (bf16[128,3584]{1,0:T(8,128)(2,1)S(1)}, bf16[128,3584]{1,0:T(8,128)(2,1)S(1)}, u32[]{:S(2)}, u32[]{:S(2)}) collective-permute-start(bf16[128,3584]{1,0:T(8,128)(2,1)S(1)} %pad_maximum_fusion.2), channel_id=1, source_target_pairs={{0,2},{2,4},{4,6},{6,0},{1,3},{3,5},{5,7},{7,1},{8,10},{10,12},{12... | collective-permute-start | bytes 2752520 | tf_op jit(solution)/shard_map/ppermute | solution.py:381
  158.7 21.0 %collective-permute-start.36 = (bf16[128,3584]{1,0:T(8,128)(2,1)}, bf16[128,3584]{1,0:T(8,128)(2,1)S(1)}, u32[]{:S(2)}, u32[]{:S(2)}) collective-permute-start(bf16[128,3584]{1,0:T(8,128)(2,1)} %pad_maximum_fusion.3), channel_id=1, source_target_pairs={{0,6},{2,0},{4,2},{6,4},{1,7},{3,1},{5,3},{7,5},{8,14},{10,8},{12,... | collective-permute-start | bytes 2752520 | tf_op jit(solution)/shard_map/ppermute | solution.py:382
  (16 other events, 94.5 us)
where the time goes:
time: 185 us; the launch traced here: 182 us
  waiting for transfers between devices  66.4 us (36%)
  starting transfers between devices  47.6 us (26%)
  Pallas kernels  33.1 us (18%)
  local copies, waits for them, and re-layouts  24.4 us (13%)
  other arithmetic  10.1 us (5%)
    ppermute x16, waiting for transfers between devices, along_z(): lax.ppermute(a, ('zl', 'zh'), [(at[z], at[(z + step) % 8]) for z in range...  32 us
    ppermute x16, starting transfers between devices, along_z(): lax.ppermute(a, ('zl', 'zh'), [(at[z], at[(z + step) % 8]) for z in range...  25 us
    pallas_call x2, Pallas kernels, tail(): pl.pallas_call(functools.partial(tail_body, first, count), out_shape=jax....  17.4 us
    pallas_call x1, Pallas kernels, head(): pl.pallas_call(head_body, out_shape=[jax.ShapeDtypeStruct((QB, HEADS * BL...  15.6 us
    ppermute x12, starting transfers between devices, along_x(): return lax.ppermute(a, 'x', [(i, (i + step) % 4) for i in range(4)])  15.4 us
    unnamed x70, local copies, waits for them, and re-layouts  15.2 us
    ppermute x12, waiting for transfers between devices, along_x(): return lax.ppermute(a, 'x', [(i, (i + step) % 4) for i in range(4)])  13.3 us
    ppermute x1, waiting for transfers between devices, local(): m = lax.ppermute(m, 'y', down)  9.28 us
  transfers between devices with their start and end apart: 37, of which 20 were waited for; matrix products, arithmetic and copies ran while one was open for 15% of the time, Pallas kernels for 10%

commit v1 on v0

--- a/solution.py
+++ b/solution.py
@@ -225,7 +225,7 @@
 
 
 def tail_body(first, count, mod, mask, tab, *refs):
-    o_refs, (q, k, v, out, wo, att, s, osem) = refs[:7], refs[7:]
+    o_refs, (q, k, v), outs, (wo, att, s, osem) = refs[:7], refs[7:10], refs[10:-4], refs[-4:]
     y0, zh = tab[POS], tab[POS + 1]
     fetch(tab, O_AT, o_refs, wo, osem)
 
@@ -236,12 +236,9 @@
     lax.fori_loop(0, count, one, 0)
     pltpu.make_async_copy(wo, wo, osem).wait()
 
-    def two(n, carry):
+    for n, out in enumerate(outs):
         sec = mod[2 * ((y0 + first + 2 * n) & 3) + zh]
-        project_out(att[n], wo, sec, out.at[n], 0, 4)
-        return carry
-
-    lax.fori_loop(0, count, two, 0)
+        project_out(att[n], wo, sec, out, 0, 4)
 
 
 VM = pl.BlockSpec(memory_space=pltpu.VMEM)
@@ -286,9 +283,9 @@
 def tail(first, count, mod, mask, tab, o_all, q, k, v):
     return pl.pallas_call(
         functools.partial(tail_body, first, count),
-        out_shape=jax.ShapeDtypeStruct((count, BLK, D), BF),
+        out_shape=[jax.ShapeDtypeStruct((BLK, D), BF)] * count,
         in_specs=[SM] * 3 + [ANY] * 7 + [VM] * 3,
-        out_specs=VM,
+        out_specs=[VM] * count,
         scratch_shapes=[
             pltpu.VMEM((2, NG, ROWS, WID), BF),
             pltpu.VMEM((count, BLK, WID), BF),
@@ -336,7 +333,7 @@
     b, r3p, r3m = lax.optimization_barrier((b, r3p, r3m))
     r4 = jnp.stack([along_z(r3p[0], 1), along_z(r3m[1], -1)])
     t1p, t1m = along_z(b, 1), along_z(b, -1)
-    t1p, t1m, r4, k1p, k1m = lax.optimization_barrier((t1p, t1m, r4, k1p, k1m))
+    t1p, t1m, _, k1p, k1m = lax.optimization_barrier((t1p, t1m, r4, k1p, k1m))
     ob = jnp.stack([o, r1p[1:3], r1m[1:3], r2p, r2m, r3p, r3m, r4])
     o1p, o1m = along_x(ob, 1), along_x(ob, -1)
     t2p, t2m = along_z(t1p, 1), along_z(t1m, -1)
@@ -346,7 +343,6 @@
     t2p, t2m, at = lax.optimization_barrier((t2p, t2m, at))
     tab = piece_tables(*at)
     t3p, t3m = along_z(t2p, 1), along_z(t2m, -1)
-    o1p, o1m, t3p, t3m = lax.optimization_barrier((o1p, o1m, t3p, t3m))
     o2p, o2m = along_x(o1p[:4], 1), along_x(o1m[4:], -1)
     t4p, t4m = along_z(t3p[:2], 1), along_z(t3m[2:], -1)
     q_all = [b, t1p, t1m, t2p, t2m, t3p, t3m, t4p, t4m]

time: 185 us -> 187 us (1.011)
  the two profiles are of different devices: /device:TPU:32 before, /device:TPU:126 now
where the time goes in v1:
time: 187 us
  waiting for transfers between devices  78.3 us (42%)
  starting transfers between devices  35.9 us (19%)
  Pallas kernels  32.9 us (18%)
  local copies, waits for them, and re-layouts  26.4 us (14%)
  other arithmetic  12.8 us (7%)
    ppermute x12, waiting for transfers between devices, along_x(): return lax.ppermute(a, 'x', [(i, (i + step) % 4) for i in range(4)])  32.1 us
    ppermute x16, waiting for transfers between devices, along_z(): lax.ppermute(a, ('zl', 'zh'), [(at[z], at[(z + step) % 8]) for z in range...  21.2 us
    ppermute x16, starting transfers between devices, along_z(): lax.ppermute(a, ('zl', 'zh'), [(at[z], at[(z + step) % 8]) for z in range...  18.9 us
    pallas_call x2, Pallas kernels, tail(): pl.pallas_call(functools.partial(tail_body, first, count), out_shape=[jax...  17.2 us
    unnamed x61, local copies, waits for them, and re-layouts  15.7 us
    pallas_call x1, Pallas kernels, head(): pl.pallas_call(head_body, out_shape=[jax.ShapeDtypeStruct((QB, HEADS * BL...  15.6 us
    ppermute x12, starting transfers between devices, along_x(): return lax.ppermute(a, 'x', [(i, (i + step) % 4) for i in range(4)])  12.2 us
    ppermute x1, waiting for transfers between devices, local(): m = lax.ppermute(m, 'y', down)  11.7 us
  transfers between devices with their start and end apart: 37, of which 19 were waited for; matrix products, arithmetic and copies ran while one was open for 18% of the time, Pallas kernels for 9%

profile of v1, /device:TPU:126, one launch (start us, length us, event | category | flops | bytes accessed | tf_op | source)
XLA Modules:
  0.0 186.7 jit_solution(1968743378069026477)
XLA Ops:
  2.3 3.2 %collective-permute-start.4 = (bf16[4,112,256]{2,1,0:T(8,128)(2,1)S(1)}, bf16[4,112,256]{2,1,0:T(8,128)(2,1)S(1)}, u32[]{:S(2)}, u32[]{:S(2)}) collective-permute-start(bf16[4,112,256]{2,1,0:T(8,128)(2,1)S(1)} %fusion.1), channel_id=1, source_target_pairs={{0,16},{16,32},{32,48},{48,1},{1,17},{17,33},{33,49},{49,0},{2,18}... | collective-permute-start | bytes 688136 | tf_op jit(solution)/shard_map/ppermute | solution.py:310
  5.5 1.5 collective-permute-start.1
  7.0 1.8 collective-permute-start.2
  8.8 2.9 %collective-permute-done.1 = bf16[2,112,256]{2,1,0:T(8,128)(2,1)S(1)} collective-permute-done((bf16[2,112,256]{2,1,0:T(8,128)(2,1)}, bf16[2,112,256]{2,1,0:T(8,128)(2,1)S(1)}, u32[]{:S(2)}, u32[]{:S(2)}) %collective-permute-start.1) | collective-permute-done | bytes 114720 | tf_op jit(solution)/shard_map/ppermute | solution.py:305
  12.0 1.5 bitcast_dynamic-update-slice_fusion.2
  13.6 3.5 %collective-permute-done.3 = bf16[112,256]{1,0:T(8,128)(2,1)S(1)} collective-permute-done((bf16[112,256]{1,0:T(8,128)(2,1)S(1)}, bf16[112,256]{1,0:T(8,128)(2,1)S(1)}, u32[]{:S(2)}, u32[]{:S(2)}) %collective-permute-start.3) | collective-permute-done | bytes 57376 | tf_op jit(solution)/shard_map/ppermute | solution.py:305
  18.1 3.3 %collective-permute-start.5 = (bf16[3,112,256]{2,1,0:T(8,128)(2,1)S(1)}, bf16[3,112,256]{2,1,0:T(8,128)(2,1)S(1)}, u32[]{:S(2)}, u32[]{:S(2)}) collective-permute-start(bf16[3,112,256]{2,1,0:T(8,128)(2,1)S(1)} %slice.114), channel_id=1, source_target_pairs={{0,16},{16,32},{32,48},{48,1},{1,17},{17,33},{33,49},{49,0},{2,18}... | collective-permute-start | bytes 516104 | tf_op jit(solution)/shard_map/ppermute | solution.py:310
  22.9 1.5 collective-permute-done.5
  24.4 3.7 %collective-permute-done.8 = bf16[3,112,256]{2,1,0:T(8,128)(2,1)S(1)} collective-permute-done((bf16[3,112,256]{2,1,0:T(8,128)(2,1)S(1)}, bf16[3,112,256]{2,1,0:T(8,128)(2,1)S(1)}, u32[]{:S(2)}, u32[]{:S(2)}) %collective-permute-start.8) | collective-permute-done | bytes 172064 | tf_op jit(solution)/shard_map/ppermute | solution.py:310
  28.3 2.0 %collective-permute-start.15 = (bf16[2,4,112,256]{3,2,1,0:T(8,128)(2,1)S(1)}, bf16[2,4,112,256]{3,2,1,0:T(8,128)(2,1)S(1)}, u32[]{:S(2)}, u32[]{:S(2)}) collective-permute-start(bf16[2,4,112,256]{3,2,1,0:T(8,128)(2,1)S(1)} %pad_maximum_fusion.5.refs_0_), channel_id=1, source_target_pairs={{0,192},{64,0},{128,64},{192,128},{1,193},{65,1},{129,65},{193,129... | collective-permute-start | bytes 1376264 | tf_op jit(solution)/shard_map/ppermute | solution.py:305
  31.2 2.1 %collective-permute-start.9 = (bf16[2,112,256]{2,1,0:T(8,128)(2,1)S(1)}, bf16[2,112,256]{2,1,0:T(8,128)(2,1)S(1)}, u32[]{:S(2)}, u32[]{:S(2)}) collective-permute-start(bf16[2,112,256]{2,1,0:T(8,128)(2,1)S(1)} %slice.117), channel_id=1, source_target_pairs={{0,49},{16,0},{32,16},{48,32},{1,48},{17,1},{33,17},{49,33},{2,51}... | collective-permute-start | bytes 344072 | tf_op jit(solution)/shard_map/ppermute | solution.py:310
  35.3 1.9 %collective-permute-done.6 = bf16[2,112,256]{2,1,0:T(8,128)(2,1)S(1)} collective-permute-done((bf16[2,112,256]{2,1,0:T(8,128)(2,1)S(1)}, bf16[2,112,256]{2,1,0:T(8,128)(2,1)S(1)}, u32[]{:S(2)}, u32[]{:S(2)}) %collective-permute-start.6) | collective-permute-done | bytes 114720 | tf_op jit(solution)/shard_map/ppermute | solution.py:310
  37.1 1.3 collective-permute-done.9
  38.5 2.0 %collective-permute-start.11 = (bf16[4,2,112,256]{3,2,1,0:T(8,128)(2,1)S(1)}, bf16[4,2,112,256]{3,2,1,0:T(8,128)(2,1)S(1)}, u32[]{:S(2)}, u32[]{:S(2)}) collective-permute-start(bf16[4,2,112,256]{3,2,1,0:T(8,128)(2,1)S(1)} %pad_maximum_fusion.4.refs_6_), channel_id=1, source_target_pairs={{0,49},{16,0},{32,16},{48,32},{1,48},{17,1},{33,17},{49,33},{2,51}... | collective-permute-start | bytes 1376264 | tf_op jit(solution)/shard_map/ppermute | solution.py:310
  40.5 1.2 collective-permute-start.12
  43.0 4.5 %collective-permute-done.12 = bf16[112,256]{1,0:T(8,128)(2,1)S(1)} collective-permute-done((bf16[112,256]{1,0:T(8,128)(2,1)S(1)}, bf16[112,256]{1,0:T(8,128)(2,1)S(1)}, u32[]{:S(2)}, u32[]{:S(2)}) %collective-permute-start.12) | collective-permute-done | bytes 57376 | tf_op jit(solution)/shard_map/ppermute | solution.py:310
  49.2 4.3 %collective-permute-done.13 = bf16[112,256]{1,0:T(8,128)(2,1)S(1)} collective-permute-done((bf16[112,256]{1,0:T(8,128)(2,1)S(1)}, bf16[112,256]{1,0:T(8,128)(2,1)S(1)}, u32[]{:S(2)}, u32[]{:S(2)}) %collective-permute-start.13) | collective-permute-done | bytes 57376 | tf_op jit(solution)/shard_map/ppermute | solution.py:310
  54.9 1.2 collective-permute-start.19
  57.4 1.7 collective-permute-start.17
  60.7 2.0 %collective-permute-start.24 = (bf16[4,112,256]{2,1,0:T(8,128)(2,1)S(1)}, bf16[4,112,256]{2,1,0:T(8,128)(2,1)S(1)}, u32[]{:S(2)}, u32[]{:S(2)}) collective-permute-start(bf16[4,112,256]{2,1,0:T(8,128)(2,1)S(1)} %slice_bitcast_fusion.1), channel_id=1, source_target_pairs={{0,64},{64,128},{128,192},{192,0},{1,65},{65,129},{129,193},{193,1... | collective-permute-start | bytes 688136 | tf_op jit(solution)/shard_map/ppermute | solution.py:305
  63.6 9.7 %collective-permute-done.24.refs_3_ = bf16[4,112,256]{2,1,0:T(8,128)(2,1)S(1)} collective-permute-done((bf16[4,112,256]{2,1,0:T(8,128)(2,1)S(1)}, bf16[4,112,256]{2,1,0:T(8,128)(2,1)S(1)}, u32[]{:S(2)}, u32[]{:S(2)}) %collective-permute-start.24) | collective-permute-done | bytes 229408 | tf_op jit(solution)/shard_map/ppermute | solution.py:305
  74.2 6.3 %collective-permute-done.25.refs_4_ = bf16[4,112,256]{2,1,0:T(8,128)(2,1)S(1)} collective-permute-done((bf16[4,112,256]{2,1,0:T(8,128)(2,1)S(1)}, bf16[4,112,256]{2,1,0:T(8,128)(2,1)S(1)}, u32[]{:S(2)}, u32[]{:S(2)}) %collective-permute-start.25) | collective-permute-done | bytes 229408 | tf_op jit(solution)/shard_map/ppermute | solution.py:305
  81.5 1.7 collective-permute-start.28
  83.3 1.8 constant_dynamic-update-slice_fusion.7
  85.1 1.1 constant_dynamic-update-slice_fusion.1
  86.2 1.1 constant_dynamic-update-slice_fusion
  87.3 1.9 %constant_dynamic-update-slice_fusion.6 = bf16[20,2,112,256]{3,2,1,0:T(8,128)(2,1)} fusion(bf16[20,2,112,256]{3,2,1,0:T(8,128)(2,1)} %constant_dynamic-update-slice_fusion.7, bf16[4,2,112,256]{3,2,1,0:T(8,128)(2,1)} %collective-permute-done.17.refs_10_), kind=kLoop, calls=%fused_computation.47 | loop fusion | bytes 917504 | tf_op jit(solution)/shard_map/concatenate | solution.py:349
  89.9 1.6 collective-permute-start.29
  93.2 1.1 slice.126
  94.2 1.7 collective-permute-start.20
  97.4 3.5 %collective-permute-done.30.refs_14_ = bf16[2,2,112,256]{3,2,1,0:T(8,128)(2,1)S(1)} collective-permute-done((bf16[2,2,112,256]{3,2,1,0:T(8,128)(2,1)S(1)}, bf16[2,2,112,256]{3,2,1,0:T(8,128)(2,1)S(1)}, u32[]{:S(2)}, u32[]{:S(2)}) %collective-permute-start.30) | collective-permute-done | bytes 229408 | tf_op jit(solution)/shard_map/ppermute | solution.py:310
  100.9 2.4 %pad_maximum_fusion = bf16[12,2,112,256]{3,2,1,0:T(8,128)(2,1)} fusion(bf16[2,2,112,256]{3,2,1,0:T(8,128)(2,1)S(1)} %collective-permute-done.30.refs_14_, bf16[2,2,112,256]{3,2,1,0:T(8,128)(2,1)S(1)} %collective-permute-done.29.refs_13_, bf16[4,2,112,256]{3,2,1,0:T(8,128)(2,1)} %collective-permute-done.28.refs_12_, bf16[4,2,112,256]{3,2,1,0:T(8,128)(2,1)} %copy-done.9), kind=kLoop, calls=%fused_computation.1 | loop fusion | flops 2064384 | bytes 2752512 | tf_op jit(solution)/shard_map/concatenate | solution.py:350
  103.4 2.6 %collective-permute-done.20.refs_20_.refs_3_ = bf16[4,2,112,256]{3,2,1,0:T(8,128)(2,1)S(1)} collective-permute-done((bf16[4,2,112,256]{3,2,1,0:T(8,128)(2,1)S(1)}, bf16[4,2,112,256]{3,2,1,0:T(8,128)(2,1)S(1)}, u32[]{:S(2)}, u32[]{:S(2)}) %collective-permute-start.20) | collective-permute-done | bytes 458784 | tf_op jit(solution)/shard_map/ppermute | solution.py:305
  106.0 7.2 %collective-permute-done.21.refs_21_.refs_4_ = bf16[4,2,112,256]{3,2,1,0:T(8,128)(2,1)S(1)} collective-permute-done((bf16[4,2,112,256]{3,2,1,0:T(8,128)(2,1)S(1)}, bf16[4,2,112,256]{3,2,1,0:T(8,128)(2,1)S(1)}, u32[]{:S(2)}, u32[]{:S(2)}) %collective-permute-start.21) | collective-permute-done | bytes 458784 | tf_op jit(solution)/shard_map/ppermute | solution.py:305
  116.2 1.6 collective-permute-done.23.refs_23_.refs_6_
  117.9 1.5 copy-done
  119.4 15.6 %head.1 = (bf16[4,512,128]{2,1,0:T(8,128)(2,1)}, bf16[1024,128]{1,0:T(8,128)(2,1)}, bf16[1024,128]{1,0:T(8,128)(2,1)}, bf16[128,1792]{1,0:T(8,128)(2,1)}, bf16[128,1792]{1,0:T(8,128)(2,1)}) custom-call(s32[8]{0:T(128)} %bitcast.100, s32[8,8]{1,0:T(8,128)} %bitcast.97, s32[162]{0:T(256)} %concatenate.30.tab, bf16[2,4,112,256]{3,2,1,0:T(8,128)(2,1)} %copy-done.10, ...), custom_call_target="tpu_custom_call" | custom-call | flops 3758096384 | bytes 25690112 | tf_op jit(solution)/shard_map/head/pallas_call | solution.py:250
  135.3 9.9 %tail.3 = (bf16[128,3584]{1,0:T(8,128)(2,1)}, bf16[128,3584]{1,0:T(8,128)(2,1)}) custom-call(s32[8]{0:T(128)} %bitcast.101, s32[8,8]{1,0:T(8,128)} %bitcast.98, s32[162]{0:T(256)} %concatenate.30.tab, bf16[8,2,112,256]{3,2,1,0:T(8,128)(2,1)} %copy-done.3, bf16[8,2,112,256]{3,2,1,0:T(8,128)(2,1)} %copy-done.1, bf16[8,2,112,256]{3,2,1,0:T(8,128)(2,1)} %copy-done.2, ...), custom_call_target="tpu_custom_call" | custom-call | flops 1476395008 | bytes 7340032 | tf_op jit(solution)/shard_map/tail/pallas_call | solution.py:284
  145.2 1.1 slice.109
  146.3 1.9 %collective-permute-start.35 = (bf16[128,1792]{1,0:T(8,128)(2,1)S(1)}, bf16[128,1792]{1,0:T(8,128)(2,1)S(1)}, u32[]{:S(2)}, u32[]{:S(2)}) collective-permute-start(bf16[128,1792]{1,0:T(8,128)(2,1)S(1)} %copy-done.21), channel_id=1, source_target_pairs={{0,6},{2,0},{4,2},{6,4},{1,7},{3,1},{5,3},{7,5},{8,14},{10,8},{12,... | collective-permute-start | bytes 1376264 | tf_op jit(solution)/shard_map/ppermute | solution.py:373
  148.1 1.0 slice.110
  149.2 1.1 add_convert_fusion.2
  150.4 1.5 collective-permute-start.34
  151.9 8.2 %collective-permute-done.35 = bf16[128,1792]{1,0:T(8,128)(2,1)S(1)} collective-permute-done((bf16[128,1792]{1,0:T(8,128)(2,1)S(1)}, bf16[128,1792]{1,0:T(8,128)(2,1)S(1)}, u32[]{:S(2)}, u32[]{:S(2)}) %collective-permute-start.35) | collective-permute-done | bytes 458784 | tf_op jit(solution)/shard_map/ppermute | solution.py:373
  161.8 7.3 %tail.2 = bf16[128,3584]{1,0:T(8,128)(2,1)} custom-call(s32[8]{0:T(128)} %bitcast.102, s32[8,8]{1,0:T(8,128)} %bitcast.99, s32[162]{0:T(256)} %concatenate.30.tab, bf16[8,2,112,256]{3,2,1,0:T(8,128)(2,1)} %copy-done.3, bf16[8,2,112,256]{3,2,1,0:T(8,128)(2,1)} %copy-done.1, bf16[8,2,112,256]{3,2,1,0:T(8,128)(2,1)} %copy-done.2, ...), custom_call_target="tpu_custom_call" | custom-call | flops 738197504 | bytes 7340032 | tf_op jit(solution)/shard_map/tail/pallas_call | solution.py:284
  169.1 3.4 %collective-permute-done.34 = bf16[128,3584]{1,0:T(8,128)(2,1)S(1)} collective-permute-done((bf16[128,3584]{1,0:T(8,128)(2,1)S(1)}, bf16[128,3584]{1,0:T(8,128)(2,1)S(1)}, u32[]{:S(2)}, u32[]{:S(2)}) %collective-permute-start.34) | collective-permute-done | bytes 917536 | tf_op jit(solution)/shard_map/ppermute | solution.py:377
  172.5 11.7 %collective-permute-done.36 = bf16[128,3584]{1,0:T(8,128)(2,1)S(1)} collective-permute-done((bf16[128,3584]{1,0:T(8,128)(2,1)}, bf16[128,3584]{1,0:T(8,128)(2,1)S(1)}, u32[]{:S(2)}, u32[]{:S(2)}) %collective-permute-start.36) | collective-permute-done | bytes 917536 | tf_op jit(solution)/shard_map/ppermute | solution.py:378
  184.2 2.4 %fusion = bf16[1,128,3584]{2,1,0:T(8,128)(2,1)} fusion(bf16[128,3584]{1,0:T(8,128)(2,1)S(1)} %collective-permute-done.36, bf16[128,3584]{1,0:T(8,128)(2,1)S(1)} %collective-permute-done.34, bf16[128,3584]{1,0:T(8,128)(2,1)} %tail.2), kind=kLoop, calls=%fused_computation.2 | loop fusion | flops 2752512 | bytes 3670016 | tf_op jit(solution)/shard_map/broadcast_in_dim | solution.py:380
  (145 shorter events, 27.2 us)
Async XLA Ops:
  0.0 7.0 %collective-permute-start = (bf16[2,112,256]{2,1,0:T(8,128)(2,1)}, bf16[2,112,256]{2,1,0:T(8,128)(2,1)S(1)}, u32[]{:S(2)}, u32[]{:S(2)}) collective-permute-start(bf16[2,112,256]{2,1,0:T(8,128)(2,1)} %param.19), channel_id=1, source_target_pairs={{0,64},{64,128},{128,192},{192,0},{1,65},{65,129},{129,193},{193,1... | collective-permute-start | bytes 344072 | tf_op jit(solution)/shard_map/ppermute | solution.py:305
  2.3 15.8 %collective-permute-start.4 = (bf16[4,112,256]{2,1,0:T(8,128)(2,1)S(1)}, bf16[4,112,256]{2,1,0:T(8,128)(2,1)S(1)}, u32[]{:S(2)}, u32[]{:S(2)}) collective-permute-start(bf16[4,112,256]{2,1,0:T(8,128)(2,1)S(1)} %fusion.1), channel_id=1, source_target_pairs={{0,16},{16,32},{32,48},{48,1},{1,17},{17,33},{33,49},{49,0},{2,18}... | collective-permute-start | bytes 688136 | tf_op jit(solution)/shard_map/ppermute | solution.py:310
  5.5 15.9 %collective-permute-start.7 = (bf16[4,112,256]{2,1,0:T(8,128)(2,1)S(1)}, bf16[4,112,256]{2,1,0:T(8,128)(2,1)S(1)}, u32[]{:S(2)}, u32[]{:S(2)}) collective-permute-start(bf16[4,112,256]{2,1,0:T(8,128)(2,1)S(1)} %fusion.1), channel_id=1, source_target_pairs={{0,49},{16,0},{32,16},{48,32},{1,48},{17,1},{33,17},{49,33},{2,51}... | collective-permute-start | bytes 688136 | tf_op jit(solution)/shard_map/ppermute | solution.py:310
  5.5 6.2 %collective-permute-start.1 = (bf16[2,112,256]{2,1,0:T(8,128)(2,1)}, bf16[2,112,256]{2,1,0:T(8,128)(2,1)S(1)}, u32[]{:S(2)}, u32[]{:S(2)}) collective-permute-start(bf16[2,112,256]{2,1,0:T(8,128)(2,1)} %param.19), channel_id=1, source_target_pairs={{0,192},{64,0},{128,64},{192,128},{1,193},{65,1},{129,65},{193,129... | collective-permute-start | bytes 344072 | tf_op jit(solution)/shard_map/ppermute | solution.py:305
  7.0 6.5 %collective-permute-start.2 = (bf16[112,256]{1,0:T(8,128)(2,1)S(1)}, bf16[112,256]{1,0:T(8,128)(2,1)S(1)}, u32[]{:S(2)}, u32[]{:S(2)}) collective-permute-start(bf16[112,256]{1,0:T(8,128)(2,1)S(1)} %slice_bitcast_fusion.5), channel_id=1, source_target_pairs={{0,64},{64,128},{128,192},{192,0},{1,65},{65,129},{129,193},{193,1... | collective-permute-start | bytes 172040 | tf_op jit(solution)/shard_map/ppermute | solution.py:305
  11.7 5.4 %collective-permute-start.3 = (bf16[112,256]{1,0:T(8,128)(2,1)S(1)}, bf16[112,256]{1,0:T(8,128)(2,1)S(1)}, u32[]{:S(2)}, u32[]{:S(2)}) collective-permute-start(bf16[112,256]{1,0:T(8,128)(2,1)S(1)} %slice_bitcast_fusion.4), channel_id=1, source_target_pairs={{0,192},{64,0},{128,64},{192,128},{1,193},{65,1},{129,65},{193,129... | collective-permute-start | bytes 172040 | tf_op jit(solution)/shard_map/ppermute | solution.py:305
  18.1 30.3 %copy-start.6 = (bf16[4,2,112,256]{3,2,1,0:T(8,128)(2,1)}, bf16[4,2,112,256]{3,2,1,0:T(8,128)(2,1)S(1)}, u32[]{:S(2)}) copy-start(bf16[4,2,112,256]{3,2,1,0:T(8,128)(2,1)S(1)} %pad_maximum_fusion.4.refs_6_) | copy-start | bytes 1376260
  18.1 6.2 %collective-permute-start.5 = (bf16[3,112,256]{2,1,0:T(8,128)(2,1)S(1)}, bf16[3,112,256]{2,1,0:T(8,128)(2,1)S(1)}, u32[]{:S(2)}, u32[]{:S(2)}) collective-permute-start(bf16[3,112,256]{2,1,0:T(8,128)(2,1)S(1)} %slice.114), channel_id=1, source_target_pairs={{0,16},{16,32},{32,48},{48,1},{1,17},{17,33},{33,49},{49,0},{2,18}... | collective-permute-start | bytes 516104 | tf_op jit(solution)/shard_map/ppermute | solution.py:310
  21.4 6.7 %collective-permute-start.8 = (bf16[3,112,256]{2,1,0:T(8,128)(2,1)S(1)}, bf16[3,112,256]{2,1,0:T(8,128)(2,1)S(1)}, u32[]{:S(2)}, u32[]{:S(2)}) collective-permute-start(bf16[3,112,256]{2,1,0:T(8,128)(2,1)S(1)} %slice.116), channel_id=1, source_target_pairs={{0,49},{16,0},{32,16},{48,32},{1,48},{17,1},{33,17},{49,33},{2,51}... | collective-permute-start | bytes 516104 | tf_op jit(solution)/shard_map/ppermute | solution.py:310
  28.2 29.1 %copy-start.10 = (bf16[2,4,112,256]{3,2,1,0:T(8,128)(2,1)}, bf16[2,4,112,256]{3,2,1,0:T(8,128)(2,1)S(1)}, u32[]{:S(2)}) copy-start(bf16[2,4,112,256]{3,2,1,0:T(8,128)(2,1)S(1)} %pad_maximum_fusion.5.refs_0_) | copy-start | bytes 1376260
  28.2 26.7 %collective-permute-start.14 = (bf16[2,4,112,256]{3,2,1,0:T(8,128)(2,1)S(1)}, bf16[2,4,112,256]{3,2,1,0:T(8,128)(2,1)S(1)}, u32[]{:S(2)}, u32[]{:S(2)}) collective-permute-start(bf16[2,4,112,256]{3,2,1,0:T(8,128)(2,1)S(1)} %pad_maximum_fusion.5.refs_0_), channel_id=1, source_target_pairs={{0,64},{64,128},{128,192},{192,0},{1,65},{65,129},{129,193},{193,1... | collective-permute-start | bytes 1376264 | tf_op jit(solution)/shard_map/ppermute | solution.py:305
  28.3 27.8 %collective-permute-start.15 = (bf16[2,4,112,256]{3,2,1,0:T(8,128)(2,1)S(1)}, bf16[2,4,112,256]{3,2,1,0:T(8,128)(2,1)S(1)}, u32[]{:S(2)}, u32[]{:S(2)}) collective-permute-start(bf16[2,4,112,256]{3,2,1,0:T(8,128)(2,1)S(1)} %pad_maximum_fusion.5.refs_0_), channel_id=1, source_target_pairs={{0,192},{64,0},{128,64},{192,128},{1,193},{65,1},{129,65},{193,129... | collective-permute-start | bytes 1376264 | tf_op jit(solution)/shard_map/ppermute | solution.py:305
  31.1 6.1 %collective-permute-start.6 = (bf16[2,112,256]{2,1,0:T(8,128)(2,1)S(1)}, bf16[2,112,256]{2,1,0:T(8,128)(2,1)S(1)}, u32[]{:S(2)}, u32[]{:S(2)}) collective-permute-start(bf16[2,112,256]{2,1,0:T(8,128)(2,1)S(1)} %slice.115), channel_id=1, source_target_pairs={{0,16},{16,32},{32,48},{48,1},{1,17},{17,33},{33,49},{49,0},{2,18}... | collective-permute-start | bytes 344072 | tf_op jit(solution)/shard_map/ppermute | solution.py:310
  31.2 7.3 %collective-permute-start.9 = (bf16[2,112,256]{2,1,0:T(8,128)(2,1)S(1)}, bf16[2,112,256]{2,1,0:T(8,128)(2,1)S(1)}, u32[]{:S(2)}, u32[]{:S(2)}) collective-permute-start(bf16[2,112,256]{2,1,0:T(8,128)(2,1)S(1)} %slice.117), channel_id=1, source_target_pairs={{0,49},{16,0},{32,16},{48,32},{1,48},{17,1},{33,17},{49,33},{2,51}... | collective-permute-start | bytes 344072 | tf_op jit(solution)/shard_map/ppermute | solution.py:310
  38.5 17.7 %collective-permute-start.10 = (bf16[4,2,112,256]{3,2,1,0:T(8,128)(2,1)S(1)}, bf16[4,2,112,256]{3,2,1,0:T(8,128)(2,1)S(1)}, u32[]{:S(2)}, u32[]{:S(2)}) collective-permute-start(bf16[4,2,112,256]{3,2,1,0:T(8,128)(2,1)S(1)} %pad_maximum_fusion.4.refs_6_), channel_id=1, source_target_pairs={{0,16},{16,32},{32,48},{48,1},{1,17},{17,33},{33,49},{49,0},{2,18}... | collective-permute-start | bytes 1376264 | tf_op jit(solution)/shard_map/ppermute | solution.py:310
  38.5 17.7 %collective-permute-start.11 = (bf16[4,2,112,256]{3,2,1,0:T(8,128)(2,1)S(1)}, bf16[4,2,112,256]{3,2,1,0:T(8,128)(2,1)S(1)}, u32[]{:S(2)}, u32[]{:S(2)}) collective-permute-start(bf16[4,2,112,256]{3,2,1,0:T(8,128)(2,1)S(1)} %pad_maximum_fusion.4.refs_6_), channel_id=1, source_target_pairs={{0,49},{16,0},{32,16},{48,32},{1,48},{17,1},{33,17},{49,33},{2,51}... | collective-permute-start | bytes 1376264 | tf_op jit(solution)/shard_map/ppermute | solution.py:310
  40.5 7.1 %collective-permute-start.12 = (bf16[112,256]{1,0:T(8,128)(2,1)S(1)}, bf16[112,256]{1,0:T(8,128)(2,1)S(1)}, u32[]{:S(2)}, u32[]{:S(2)}) collective-permute-start(bf16[112,256]{1,0:T(8,128)(2,1)S(1)} %slice_bitcast_fusion.7), channel_id=1, source_target_pairs={{0,16},{16,32},{32,48},{48,1},{1,17},{17,33},{33,49},{49,0},{2,18}... | collective-permute-start | bytes 172040 | tf_op jit(solution)/shard_map/ppermute | solution.py:310
  47.6 5.9 %collective-permute-start.13 = (bf16[112,256]{1,0:T(8,128)(2,1)S(1)}, bf16[112,256]{1,0:T(8,128)(2,1)S(1)}, u32[]{:S(2)}, u32[]{:S(2)}) collective-permute-start(bf16[112,256]{1,0:T(8,128)(2,1)S(1)} %slice_bitcast_fusion.6), channel_id=1, source_target_pairs={{0,49},{16,0},{32,16},{48,32},{1,48},{17,1},{33,17},{49,33},{2,51}... | collective-permute-start | bytes 172040 | tf_op jit(solution)/shard_map/ppermute | solution.py:310
  54.1 9.4 %copy-start.3 = (bf16[8,2,112,256]{3,2,1,0:T(8,128)(2,1)}, bf16[8,2,112,256]{3,2,1,0:T(8,128)(2,1)S(1)}, u32[]{:S(2)}) copy-start(bf16[8,2,112,256]{3,2,1,0:T(8,128)(2,1)S(1)} %get-tuple-element.60.refs_17_.refs_0_) | copy-start | bytes 2752516
  54.1 31.0 %collective-permute-start.18 = (bf16[8,2,112,256]{3,2,1,0:T(8,128)(2,1)S(1)}, bf16[8,2,112,256]{3,2,1,0:T(8,128)(2,1)S(1)}, u32[]{:S(2)}, u32[]{:S(2)}) collective-permute-start(bf16[8,2,112,256]{3,2,1,0:T(8,128)(2,1)S(1)} %get-tuple-element.60.refs_17_.refs_0_), channel_id=1, source_target_pairs={{0,64},{64,128},{128,192},{192,0},{1,65},{65,129},{129,193},{193,1... | collective-permute-start | bytes 2752520 | tf_op jit(solution)/shard_map/ppermute | solution.py:305
  54.9 31.3 %collective-permute-start.19 = (bf16[8,2,112,256]{3,2,1,0:T(8,128)(2,1)S(1)}, bf16[8,2,112,256]{3,2,1,0:T(8,128)(2,1)S(1)}, u32[]{:S(2)}, u32[]{:S(2)}) collective-permute-start(bf16[8,2,112,256]{3,2,1,0:T(8,128)(2,1)S(1)} %get-tuple-element.60.refs_17_.refs_0_), channel_id=1, source_target_pairs={{0,192},{64,0},{128,64},{192,128},{1,193},{65,1},{129,65},{193,129... | collective-permute-start | bytes 2752520 | tf_op jit(solution)/shard_map/ppermute | solution.py:305
  56.2 25.1 %collective-permute-start.16 = (bf16[4,2,112,256]{3,2,1,0:T(8,128)(2,1)S(1)}, bf16[4,2,112,256]{3,2,1,0:T(8,128)(2,1)}, u32[]{:S(2)}, u32[]{:S(2)}) collective-permute-start(bf16[4,2,112,256]{3,2,1,0:T(8,128)(2,1)S(1)} %collective-permute-done.10.refs_7_), channel_id=1, source_target_pairs={{0,16},{16,32},{32,48},{48,1},{1,17},{17,33},{33,49},{49,0},{2,18}... | collective-permute-start | bytes 1376264 | tf_op jit(solution)/shard_map/ppermute | solution.py:310
  57.4 23.9 %collective-permute-start.17 = (bf16[4,2,112,256]{3,2,1,0:T(8,128)(2,1)S(1)}, bf16[4,2,112,256]{3,2,1,0:T(8,128)(2,1)}, u32[]{:S(2)}, u32[]{:S(2)}) collective-permute-start(bf16[4,2,112,256]{3,2,1,0:T(8,128)(2,1)S(1)} %collective-permute-done.11.refs_8_), channel_id=1, source_target_pairs={{0,49},{16,0},{32,16},{48,32},{1,48},{17,1},{33,17},{49,33},{2,51}... | collective-permute-start | bytes 1376264 | tf_op jit(solution)/shard_map/ppermute | solution.py:310
  60.7 12.5 %collective-permute-start.24 = (bf16[4,112,256]{2,1,0:T(8,128)(2,1)S(1)}, bf16[4,112,256]{2,1,0:T(8,128)(2,1)S(1)}, u32[]{:S(2)}, u32[]{:S(2)}) collective-permute-start(bf16[4,112,256]{2,1,0:T(8,128)(2,1)S(1)} %slice_bitcast_fusion.1), channel_id=1, source_target_pairs={{0,64},{64,128},{128,192},{192,0},{1,65},{65,129},{129,193},{193,1... | collective-permute-start | bytes 688136 | tf_op jit(solution)/shard_map/ppermute | solution.py:305
  73.2 14.1 %copy-start.13 = (bf16[4,112,256]{2,1,0:T(8,128)(2,1)}, bf16[4,112,256]{2,1,0:T(8,128)(2,1)S(1)}, u32[]{:S(2)}) copy-start(bf16[4,112,256]{2,1,0:T(8,128)(2,1)S(1)} %collective-permute-done.24.refs_3_) | copy-start | bytes 688132
  73.2 7.2 %collective-permute-start.25 = (bf16[4,112,256]{2,1,0:T(8,128)(2,1)S(1)}, bf16[4,112,256]{2,1,0:T(8,128)(2,1)S(1)}, u32[]{:S(2)}, u32[]{:S(2)}) collective-permute-start(bf16[4,112,256]{2,1,0:T(8,128)(2,1)S(1)} %slice_bitcast_fusion), channel_id=1, source_target_pairs={{0,192},{64,0},{128,64},{192,128},{1,193},{65,1},{129,65},{193,129... | collective-permute-start | bytes 688136 | tf_op jit(solution)/shard_map/ppermute | solution.py:305
  81.2 8.7 %collective-permute-start.27 = (bf16[4,2,112,256]{3,2,1,0:T(8,128)(2,1)}, bf16[4,2,112,256]{3,2,1,0:T(8,128)(2,1)S(1)}, u32[]{:S(2)}, u32[]{:S(2)}) collective-permute-start(bf16[4,2,112,256]{3,2,1,0:T(8,128)(2,1)} %collective-permute-done.16.refs_9_), channel_id=1, source_target_pairs={{0,16},{16,32},{32,48},{48,1},{1,17},{17,33},{33,49},{49,0},{2,18}... | collective-permute-start | bytes 1376264 | tf_op jit(solution)/shard_map/ppermute | solution.py:310
  81.5 10.0 %collective-permute-start.28 = (bf16[4,2,112,256]{3,2,1,0:T(8,128)(2,1)}, bf16[4,2,112,256]{3,2,1,0:T(8,128)(2,1)}, u32[]{:S(2)}, u32[]{:S(2)}) collective-permute-start(bf16[4,2,112,256]{3,2,1,0:T(8,128)(2,1)} %collective-permute-done.17.refs_10_), channel_id=1, source_target_pairs={{0,49},{16,0},{32,16},{48,32},{1,48},{17,1},{33,17},{49,33},{2,51}... | collective-permute-start | bytes 1376264 | tf_op jit(solution)/shard_map/ppermute | solution.py:310
  87.3 30.5 %collective-permute-start.22 = (bf16[24,2,112,256]{3,2,1,0:T(8,128)(2,1)}, bf16[24,2,112,256]{3,2,1,0:T(8,128)(2,1)S(1)}, u32[]{:S(2)}, u32[]{:S(2)}) collective-permute-start(bf16[24,2,112,256]{3,2,1,0:T(8,128)(2,1)} %constant_dynamic-update-slice_fusion), channel_id=1, source_target_pairs={{0,8},{8,0},{1,9},{9,1},{2,10},{10,2},{3,11},{11,3},{4,12},{12,4},... | collective-permute-start | bytes 8257544 | tf_op jit(solution)/shard_map/ppermute | solution.py:314
  89.2 28.7 %collective-permute-start.31 = (bf16[20,2,112,256]{3,2,1,0:T(8,128)(2,1)}, bf16[20,2,112,256]{3,2,1,0:T(8,128)(2,1)}, u32[]{:S(2)}, u32[]{:S(2)}) collective-permute-start(bf16[20,2,112,256]{3,2,1,0:T(8,128)(2,1)} %constant_dynamic-update-slice_fusion.6), channel_id=1, source_target_pairs={{0,8},{8,0},{1,9},{9,1},{2,10},{10,2},{3,11},{11,3},{4,12},{12,4},... | collective-permute-start | bytes 6881288 | tf_op jit(solution)/shard_map/ppermute | solution.py:314
  89.9 7.4 %collective-permute-start.29 = (bf16[2,2,112,256]{3,2,1,0:T(8,128)(2,1)S(1)}, bf16[2,2,112,256]{3,2,1,0:T(8,128)(2,1)S(1)}, u32[]{:S(2)}, u32[]{:S(2)}) collective-permute-start(bf16[2,2,112,256]{3,2,1,0:T(8,128)(2,1)S(1)} %slice.128), channel_id=1, source_target_pairs={{0,16},{16,32},{32,48},{48,1},{1,17},{17,33},{33,49},{49,0},{2,18}... | collective-permute-start | bytes 688136 | tf_op jit(solution)/shard_map/ppermute | solution.py:310
  92.5 8.4 %collective-permute-start.30 = (bf16[2,2,112,256]{3,2,1,0:T(8,128)(2,1)S(1)}, bf16[2,2,112,256]{3,2,1,0:T(8,128)(2,1)S(1)}, u32[]{:S(2)}, u32[]{:S(2)}) collective-permute-start(bf16[2,2,112,256]{3,2,1,0:T(8,128)(2,1)S(1)} %slice.129), channel_id=1, source_target_pairs={{0,49},{16,0},{32,16},{48,32},{1,48},{17,1},{33,17},{49,33},{2,51}... | collective-permute-start | bytes 688136 | tf_op jit(solution)/shard_map/ppermute | solution.py:310
  93.2 12.9 %copy-start.20 = (s32[1,1,8]{2,1,0:T(1,128)S(1)}, s32[1,1,8]{2,1,0:T(1,128)}, u32[]{:S(2)}) copy-start(s32[1,1,8]{2,1,0:T(1,128)} %constant.19.clone) | copy-start | bytes 100
  94.2 11.8 %collective-permute-start.20 = (bf16[4,2,112,256]{3,2,1,0:T(8,128)(2,1)S(1)}, bf16[4,2,112,256]{3,2,1,0:T(8,128)(2,1)S(1)}, u32[]{:S(2)}, u32[]{:S(2)}) collective-permute-start(bf16[4,2,112,256]{3,2,1,0:T(8,128)(2,1)S(1)} %slice.126), channel_id=1, source_target_pairs={{0,64},{64,128},{128,192},{192,0},{1,65},{65,129},{129,193},{193,1... | collective-permute-start | bytes 1376264 | tf_op jit(solution)/shard_map/ppermute | solution.py:305
  97.4 17.6 %copy-start.15 = (bf16[2,2,112,256]{3,2,1,0:T(8,128)(2,1)}, bf16[2,2,112,256]{3,2,1,0:T(8,128)(2,1)S(1)}, u32[]{:S(2)}) copy-start(bf16[2,2,112,256]{3,2,1,0:T(8,128)(2,1)S(1)} %collective-permute-done.29.refs_13_) | copy-start | bytes 688132
  97.4 20.5 %collective-permute-start.26 = (bf16[8,4,112,256]{3,2,1,0:T(8,128)(2,1)}, bf16[8,4,112,256]{3,2,1,0:T(8,128)(2,1)}, u32[]{:S(2)}, u32[]{:S(2)}) collective-permute-start(bf16[8,4,112,256]{3,2,1,0:T(8,128)(2,1)} %bitcast_dynamic-update-slice_fusion), channel_id=1, source_target_pairs={{0,8},{8,0},{1,9},{9,1},{2,10},{10,2},{3,11},{11,3},{4,12},{12,4},... | collective-permute-start | bytes 5505032 | tf_op jit(solution)/shard_map/ppermute | solution.py:314
  100.9 14.2 %copy-start.16 = (bf16[2,2,112,256]{3,2,1,0:T(8,128)(2,1)}, bf16[2,2,112,256]{3,2,1,0:T(8,128)(2,1)S(1)}, u32[]{:S(2)}) copy-start(bf16[2,2,112,256]{3,2,1,0:T(8,128)(2,1)S(1)} %collective-permute-done.30.refs_14_) | copy-start | bytes 688132
  100.9 12.3 %collective-permute-start.21 = (bf16[4,2,112,256]{3,2,1,0:T(8,128)(2,1)S(1)}, bf16[4,2,112,256]{3,2,1,0:T(8,128)(2,1)S(1)}, u32[]{:S(2)}, u32[]{:S(2)}) collective-permute-start(bf16[4,2,112,256]{3,2,1,0:T(8,128)(2,1)S(1)} %slice.127), channel_id=1, source_target_pairs={{0,192},{64,0},{128,64},{192,128},{1,193},{65,1},{129,65},{193,129... | collective-permute-start | bytes 1376264 | tf_op jit(solution)/shard_map/ppermute | solution.py:305
  100.9 14.4 %copy-start.19 = (s32[1,8,1]{1,2,0:T(1,128)S(1)}, s32[1,8,1]{1,2,0:T(1,128)}, u32[]{:S(2)}) copy-start(s32[1,8,1]{1,2,0:T(1,128)} %constant.17.clone) | copy-start | bytes 100
  106.0 11.9 %copy-start.4 = (bf16[4,2,112,256]{3,2,1,0:T(8,128)(2,1)}, bf16[4,2,112,256]{3,2,1,0:T(8,128)(2,1)S(1)}, u32[]{:S(2)}) copy-start(bf16[4,2,112,256]{3,2,1,0:T(8,128)(2,1)S(1)} %collective-permute-done.20.refs_20_.refs_3_) | copy-start | bytes 1376260
  106.0 11.8 %collective-permute-start.32 = (bf16[12,2,112,256]{3,2,1,0:T(8,128)(2,1)}, bf16[12,2,112,256]{3,2,1,0:T(8,128)(2,1)}, u32[]{:S(2)}, u32[]{:S(2)}) collective-permute-start(bf16[12,2,112,256]{3,2,1,0:T(8,128)(2,1)} %pad_maximum_fusion), channel_id=1, source_target_pairs={{0,8},{8,0},{1,9},{9,1},{2,10},{10,2},{3,11},{11,3},{4,12},{12,4},... | collective-permute-start | bytes 4128776 | tf_op jit(solution)/shard_map/ppermute | solution.py:314
  115.0 2.8 %collective-permute-start.23 = (bf16[8,2,112,256]{3,2,1,0:T(8,128)(2,1)}, bf16[8,2,112,256]{3,2,1,0:T(8,128)(2,1)}, u32[]{:S(2)}, u32[]{:S(2)}) collective-permute-start(bf16[8,2,112,256]{3,2,1,0:T(8,128)(2,1)} %pad_maximum_fusion.1), channel_id=1, source_target_pairs={{0,8},{8,0},{1,9},{9,1},{2,10},{10,2},{3,11},{11,3},{4,12},{12,4},... | collective-permute-start | bytes 2752520 | tf_op jit(solution)/shard_map/ppermute | solution.py:314
  135.0 14.2 %collective-permute-start.33 = (bf16[128,1792]{1,0:T(8,128)(2,1)}, bf16[128,1792]{1,0:T(8,128)(2,1)S(1)}, u32[]{:S(2)}, u32[]{:S(2)}) collective-permute-start(bf16[128,1792]{1,0:T(8,128)(2,1)} %get-tuple-element.42), channel_id=1, source_target_pairs={{0,2},{2,4},{4,6},{6,0},{1,3},{3,5},{5,7},{7,1},{8,10},{10,12},{12... | collective-permute-start | bytes 1376264 | tf_op jit(solution)/shard_map/ppermute | solution.py:372
  135.3 11.0 %copy-start.21 = (bf16[128,1792]{1,0:T(8,128)(2,1)S(1)}, bf16[128,1792]{1,0:T(8,128)(2,1)}, u32[]{:S(2)}) copy-start(bf16[128,1792]{1,0:T(8,128)(2,1)} %get-tuple-element.44) | copy-start | bytes 1376260
  146.3 13.9 %copy-start.17 = (bf16[128,3584]{1,0:T(8,128)(2,1)S(1)}, bf16[128,3584]{1,0:T(8,128)(2,1)}, u32[]{:S(2)}) copy-start(bf16[128,3584]{1,0:T(8,128)(2,1)} %get-tuple-element.43) | copy-start | bytes 2752516
  146.3 13.9 %collective-permute-start.35 = (bf16[128,1792]{1,0:T(8,128)(2,1)S(1)}, bf16[128,1792]{1,0:T(8,128)(2,1)S(1)}, u32[]{:S(2)}, u32[]{:S(2)}) collective-permute-start(bf16[128,1792]{1,0:T(8,128)(2,1)S(1)} %copy-done.21), channel_id=1, source_target_pairs={{0,6},{2,0},{4,2},{6,4},{1,7},{3,1},{5,3},{7,5},{8,14},{10,8},{12,... | collective-permute-start | bytes 1376264 | tf_op jit(solution)/shard_map/ppermute | solution.py:373
  150.4 22.1 %collective-permute-start.34 = (bf16[128,3584]{1,0:T(8,128)(2,1)S(1)}, bf16[128,3584]{1,0:T(8,128)(2,1)S(1)}, u32[]{:S(2)}, u32[]{:S(2)}) collective-permute-start(bf16[128,3584]{1,0:T(8,128)(2,1)S(1)} %pad_maximum_fusion.2), channel_id=1, source_target_pairs={{0,2},{2,4},{4,6},{6,0},{1,3},{3,5},{5,7},{7,1},{8,10},{10,12},{12... | collective-permute-start | bytes 2752520 | tf_op jit(solution)/shard_map/ppermute | solution.py:377
  161.3 23.0 %collective-permute-start.36 = (bf16[128,3584]{1,0:T(8,128)(2,1)}, bf16[128,3584]{1,0:T(8,128)(2,1)S(1)}, u32[]{:S(2)}, u32[]{:S(2)}) collective-permute-start(bf16[128,3584]{1,0:T(8,128)(2,1)} %pad_maximum_fusion.3), channel_id=1, source_target_pairs={{0,6},{2,0},{4,2},{6,4},{1,7},{3,1},{5,3},{7,5},{8,14},{10,8},{12,... | collective-permute-start | bytes 2752520 | tf_op jit(solution)/shard_map/ppermute | solution.py:378
  (12 other events, 57.8 us)

commit v2 on v1

--- a/solution.py
+++ b/solution.py
@@ -124,10 +124,10 @@
 
 
 def head_body(mod, mask, tab, *refs):
-    kv_refs, q_refs, o_refs, x_hbm, tables = refs[:6], refs[6:17], refs[17:24], refs[24], refs[25:29]
-    q, k, v = refs[29:32]
-    outs = refs[32:34]
-    x, wk, wq, wo, att, s, inv, xsem, ksem, qsem, osem = refs[34:]
+    kv_refs, q_refs, o_refs, x_hbm, tables = refs[:6], refs[6:18], refs[18:25], refs[25], refs[26:30]
+    q, k, v = refs[30:33]
+    outs = refs[33:35]
+    x, wk, wq, wo, att, s, inv, xsem, ksem, qsem, osem = refs[35:]
     y0, zh = tab[POS], tab[POS + 1]
     for a in range(4):
 
@@ -256,7 +256,7 @@
             HALF_BLOCK,
             HALF_BLOCK,
         ],
-        in_specs=[SM] * 3 + [ANY] * 25 + [VM] * 4,
+        in_specs=[SM] * 3 + [ANY] * 26 + [VM] * 4,
         out_specs=[VM] * 5,
         scratch_shapes=[
             pltpu.VMEM((NBLK + 2, BLK, D), BF),
@@ -318,7 +318,7 @@
     p1p, p1m = along_x(q, 1), along_x(q, -1)
     own = jnp.concatenate([kv[:1], o, kv[1:]], axis=0)
     r1p, r1m = along_z(own, 1), along_z(own, -1)
-    p2p, p2m = along_x(p1p[0], 1), along_x(p1m[1], -1)
+    p2 = along_x(q, 2)
     r2p, r2m = along_z(r1p[:3], 1), along_z(r1m[1:], -1)
     kb = jnp.stack(
         [
@@ -329,7 +329,7 @@
     k1p, k1m = along_x(kb, 1), along_x(kb, -1)
     r2p, r2m = r2p[1:], r2m[:2]
     r3p, r3m = along_z(r2p, 1), along_z(r2m, -1)
-    b = jnp.stack([q, p1p, p1m, jnp.stack([p2p, p2m])])
+    b = jnp.stack([q, p1p, p1m, p2])
     b, r3p, r3m = lax.optimization_barrier((b, r3p, r3m))
     r4 = jnp.stack([along_z(r3p[0], 1), along_z(r3m[1], -1)])
     t1p, t1m = along_z(b, 1), along_z(b, -1)
@@ -338,16 +338,18 @@
     o1p, o1m = along_x(ob, 1), along_x(ob, -1)
     t2p, t2m = along_z(t1p, 1), along_z(t1m, -1)
     k2p, k2m = along_x(k1p[0], 1), along_x(k1m[1], -1)
-    kv_all = [kb, k1p, k1m, k2p, k2m]
-    kv_all.append(swap(jnp.concatenate([kb, k1p, k1m, jnp.stack([k2p, k2m])])))
     t2p, t2m, at = lax.optimization_barrier((t2p, t2m, at))
     tab = piece_tables(*at)
     t3p, t3m = along_z(t2p, 1), along_z(t2m, -1)
+    k2p, k2m = lax.optimization_barrier((k2p, k2m, t3p, t3m))[:2]
+    kv_all = [kb, k1p, k1m, k2p, k2m]
+    kv_all.append(swap(jnp.concatenate([kb, k1p, k1m, jnp.stack([k2p, k2m])])))
     o2p, o2m = along_x(o1p[:4], 1), along_x(o1m[4:], -1)
     t4p, t4m = along_z(t3p[:2], 1), along_z(t3m[2:], -1)
     q_all = [b, t1p, t1m, t2p, t2m, t3p, t3m, t4p, t4m]
     q_all.append(swap(jnp.concatenate([b, t1p, t1m, t2p, t2m])))
-    q_all.append(swap(jnp.concatenate([t3p, t3m, t4p, t4m])))
+    q_all.append(swap(jnp.concatenate([t3p, t3m])))
+    q_all.append(swap(jnp.concatenate([t4p, t4m])))
     o_all = [ob, o1p, o1m, o2p, o2m]
     o_all.append(swap(jnp.concatenate([ob, o1p, o1m])))
     o_all.append(swap(jnp.concatenate([o2p, o2m])))
@@ -372,8 +374,8 @@
     far_a = lax.ppermute(o2a, "y", up)
     far_b = lax.ppermute(o2b, "y", down)
     o3, o1 = tail(3, 2, *small, o_all, q, k, v)
-    p = jnp.concatenate([add(o1[:, :half], far_a), o1[:, half:]], axis=1)
-    m = jnp.concatenate([o3[:, :half], add(o3[:, half:], far_b)], axis=1)
+    p = lax.dynamic_update_slice(o1, add(o1[:, :half], far_a), (0, 0))
+    m = lax.dynamic_update_slice(o3, add(o3[:, half:], far_b), (0, half))
     p = lax.ppermute(p, "y", up)
     m = lax.ppermute(m, "y", down)
     o0 = tail(0, 1, *small, o_all, q, k, v)[0]
@@ -392,4 +394,6 @@
         P(None, dp, None),
         P(None, mp, dp),
     )
-    return jax.shard_map(local, mesh=fine, in_specs=in_specs, out_specs=P(dp, mp, None), check_vma=False)
+    return jax.shard_map(
+        local, mesh=fine, in_specs=in_specs, out_specs=P(dp, mp, None), check_vma=False
+    )

time: 187 us -> 171 us (0.914)
  the two profiles are of different devices: /device:TPU:126 before, /device:TPU:24 now
where the time goes in v2:
time: 171 us; the launch traced here: 170 us
  starting transfers between devices  50.7 us (30%)
  waiting for transfers between devices  46.2 us (27%)
  Pallas kernels  32.7 us (19%)
  local copies, waits for them, and re-layouts  25.9 us (15%)
  other arithmetic  14.2 us (8%)
    ppermute x16, starting transfers between devices, along_z(): lax.ppermute(a, ('zl', 'zh'), [(at[z], at[(z + step) % 8]) for z in range...  31.1 us
    unnamed x59, local copies, waits for them, and re-layouts  17.2 us
    pallas_call x2, Pallas kernels, tail(): pl.pallas_call(functools.partial(tail_body, first, count), out_shape=[jax...  17.1 us
    ppermute x16, waiting for transfers between devices, along_z(): lax.ppermute(a, ('zl', 'zh'), [(at[z], at[(z + step) % 8]) for z in range...  16.7 us
    pallas_call x1, Pallas kernels, head(): pl.pallas_call(head_body, out_shape=[jax.ShapeDtypeStruct((QB, HEADS * BL...  15.6 us
    ppermute x11, starting transfers between devices, along_x(): return lax.ppermute(a, 'x', [(i, (i + step) % 4) for i in range(4)])  15 us
    ppermute x11, waiting for transfers between devices, along_x(): return lax.ppermute(a, 'x', [(i, (i + step) % 4) for i in range(4)])  13.5 us
    ppermute x1, waiting for transfers between devices, local(): p = lax.ppermute(p, 'y', up)  9.85 us
  transfers between devices with their start and end apart: 37, of which 15 were waited for; matrix products, arithmetic and copies ran while one was open for 19% of the time, Pallas kernels for 10%

profile of v2, /device:TPU:24, one launch (start us, length us, event | category | flops | bytes accessed | tf_op | source)
XLA Modules:
  0.0 170.1 jit_solution(4437545078236627191)
XLA Ops:
  1.8 2.0 %collective-permute-start.3 = (bf16[4,112,256]{2,1,0:T(8,128)(2,1)S(1)}, bf16[4,112,256]{2,1,0:T(8,128)(2,1)S(1)}, u32[]{:S(2)}, u32[]{:S(2)}) collective-permute-start(bf16[4,112,256]{2,1,0:T(8,128)(2,1)S(1)} %fusion.3), channel_id=1, source_target_pairs={{0,16},{16,32},{32,48},{48,1},{1,17},{17,33},{33,49},{49,0},{2,18}... | collective-permute-start | bytes 688136 | tf_op jit(solution)/shard_map/ppermute | solution.py:310
  3.8 4.0 %collective-permute-start.6 = (bf16[4,112,256]{2,1,0:T(8,128)(2,1)S(1)}, bf16[4,112,256]{2,1,0:T(8,128)(2,1)S(1)}, u32[]{:S(2)}, u32[]{:S(2)}) collective-permute-start(bf16[4,112,256]{2,1,0:T(8,128)(2,1)S(1)} %fusion.3), channel_id=1, source_target_pairs={{0,49},{16,0},{32,16},{48,32},{1,48},{17,1},{33,17},{49,33},{2,51}... | collective-permute-start | bytes 688136 | tf_op jit(solution)/shard_map/ppermute | solution.py:310
  7.8 1.5 collective-permute-start
  9.3 1.7 %collective-permute-start.1 = (bf16[2,112,256]{2,1,0:T(8,128)(2,1)}, bf16[2,112,256]{2,1,0:T(8,128)(2,1)S(1)}, u32[]{:S(2)}, u32[]{:S(2)}) collective-permute-start(bf16[2,112,256]{2,1,0:T(8,128)(2,1)} %param.19), channel_id=1, source_target_pairs={{0,192},{64,0},{128,64},{192,128},{1,193},{65,1},{129,65},{193,129... | collective-permute-start | bytes 344072 | tf_op jit(solution)/shard_map/ppermute | solution.py:305
  11.0 1.8 %collective-permute-start.2 = (bf16[2,112,256]{2,1,0:T(8,128)(2,1)}, bf16[2,112,256]{2,1,0:T(8,128)(2,1)S(1)}, u32[]{:S(2)}, u32[]{:S(2)}) collective-permute-start(bf16[2,112,256]{2,1,0:T(8,128)(2,1)} %param.19), channel_id=1, source_target_pairs={{0,128},{64,192},{128,0},{192,64},{1,129},{65,193},{129,1},{193,65... | collective-permute-start | bytes 344072 | tf_op jit(solution)/shard_map/ppermute | solution.py:305
  12.9 1.6 bitcast_dynamic-update-slice_fusion.2
  15.4 2.2 %collective-permute-done.2 = bf16[2,112,256]{2,1,0:T(8,128)(2,1)S(1)} collective-permute-done((bf16[2,112,256]{2,1,0:T(8,128)(2,1)}, bf16[2,112,256]{2,1,0:T(8,128)(2,1)S(1)}, u32[]{:S(2)}, u32[]{:S(2)}) %collective-permute-start.2) | collective-permute-done | bytes 114720 | tf_op jit(solution)/shard_map/ppermute | solution.py:305
  18.7 3.3 %collective-permute-start.7 = (bf16[3,112,256]{2,1,0:T(8,128)(2,1)S(1)}, bf16[3,112,256]{2,1,0:T(8,128)(2,1)S(1)}, u32[]{:S(2)}, u32[]{:S(2)}) collective-permute-start(bf16[3,112,256]{2,1,0:T(8,128)(2,1)S(1)} %slice.98), channel_id=1, source_target_pairs={{0,49},{16,0},{32,16},{48,32},{1,48},{17,1},{33,17},{49,33},{2,51}... | collective-permute-start | bytes 516104 | tf_op jit(solution)/shard_map/ppermute | solution.py:310
  23.3 1.9 %collective-permute-done.4 = bf16[3,112,256]{2,1,0:T(8,128)(2,1)S(1)} collective-permute-done((bf16[3,112,256]{2,1,0:T(8,128)(2,1)S(1)}, bf16[3,112,256]{2,1,0:T(8,128)(2,1)S(1)}, u32[]{:S(2)}, u32[]{:S(2)}) %collective-permute-start.4) | collective-permute-done | bytes 172064 | tf_op jit(solution)/shard_map/ppermute | solution.py:310
  26.4 2.4 %collective-permute-start.14 = (bf16[2,4,112,256]{3,2,1,0:T(8,128)(2,1)S(1)}, bf16[2,4,112,256]{3,2,1,0:T(8,128)(2,1)S(1)}, u32[]{:S(2)}, u32[]{:S(2)}) collective-permute-start(bf16[2,4,112,256]{3,2,1,0:T(8,128)(2,1)S(1)} %pad_maximum_fusion.3.refs_0_), channel_id=1, source_target_pairs={{0,192},{64,0},{128,64},{192,128},{1,193},{65,1},{129,65},{193,129... | collective-permute-start | bytes 1376264 | tf_op jit(solution)/shard_map/ppermute | solution.py:305
  29.6 3.3 %collective-permute-start.8 = (bf16[2,112,256]{2,1,0:T(8,128)(2,1)S(1)}, bf16[2,112,256]{2,1,0:T(8,128)(2,1)S(1)}, u32[]{:S(2)}, u32[]{:S(2)}) collective-permute-start(bf16[2,112,256]{2,1,0:T(8,128)(2,1)S(1)} %slice.99), channel_id=1, source_target_pairs={{0,49},{16,0},{32,16},{48,32},{1,48},{17,1},{33,17},{49,33},{2,51}... | collective-permute-start | bytes 344072 | tf_op jit(solution)/shard_map/ppermute | solution.py:310
  35.8 3.7 %collective-permute-start.10 = (bf16[4,2,112,256]{3,2,1,0:T(8,128)(2,1)S(1)}, bf16[4,2,112,256]{3,2,1,0:T(8,128)(2,1)S(1)}, u32[]{:S(2)}, u32[]{:S(2)}) collective-permute-start(bf16[4,2,112,256]{3,2,1,0:T(8,128)(2,1)S(1)} %pad_maximum_fusion.2.refs_6_), channel_id=1, source_target_pairs={{0,49},{16,0},{32,16},{48,32},{1,48},{17,1},{33,17},{49,33},{2,51}... | collective-permute-start | bytes 1376264 | tf_op jit(solution)/shard_map/ppermute | solution.py:310
  39.8 2.9 %collective-permute-start.12 = (bf16[112,256]{1,0:T(8,128)(2,1)S(1)}, bf16[112,256]{1,0:T(8,128)(2,1)S(1)}, u32[]{:S(2)}, u32[]{:S(2)}) collective-permute-start(bf16[112,256]{1,0:T(8,128)(2,1)S(1)} %slice_bitcast_fusion.4), channel_id=1, source_target_pairs={{0,49},{16,0},{32,16},{48,32},{1,48},{17,1},{33,17},{49,33},{2,51}... | collective-permute-start | bytes 172040 | tf_op jit(solution)/shard_map/ppermute | solution.py:310
  44.0 2.9 %collective-permute-done.12 = bf16[112,256]{1,0:T(8,128)(2,1)S(1)} collective-permute-done((bf16[112,256]{1,0:T(8,128)(2,1)S(1)}, bf16[112,256]{1,0:T(8,128)(2,1)S(1)}, u32[]{:S(2)}, u32[]{:S(2)}) %collective-permute-start.12) | collective-permute-done | bytes 57376 | tf_op jit(solution)/shard_map/ppermute | solution.py:310
  46.9 2.2 %collective-permute-start.11 = (bf16[112,256]{1,0:T(8,128)(2,1)S(1)}, bf16[112,256]{1,0:T(8,128)(2,1)S(1)}, u32[]{:S(2)}, u32[]{:S(2)}) collective-permute-start(bf16[112,256]{1,0:T(8,128)(2,1)S(1)} %slice_bitcast_fusion.5), channel_id=1, source_target_pairs={{0,16},{16,32},{32,48},{48,1},{1,17},{17,33},{33,49},{49,0},{2,18}... | collective-permute-start | bytes 172040 | tf_op jit(solution)/shard_map/ppermute | solution.py:310
  50.0 2.3 %collective-permute-done.11 = bf16[112,256]{1,0:T(8,128)(2,1)S(1)} collective-permute-done((bf16[112,256]{1,0:T(8,128)(2,1)S(1)}, bf16[112,256]{1,0:T(8,128)(2,1)S(1)}, u32[]{:S(2)}, u32[]{:S(2)}) %collective-permute-start.11) | collective-permute-done | bytes 57376 | tf_op jit(solution)/shard_map/ppermute | solution.py:310
  53.0 3.2 %collective-permute-start.18 = (bf16[8,2,112,256]{3,2,1,0:T(8,128)(2,1)S(1)}, bf16[8,2,112,256]{3,2,1,0:T(8,128)(2,1)S(1)}, u32[]{:S(2)}, u32[]{:S(2)}) collective-permute-start(bf16[8,2,112,256]{3,2,1,0:T(8,128)(2,1)S(1)} %get-tuple-element.64.refs_18_.refs_0_), channel_id=1, source_target_pairs={{0,192},{64,0},{128,64},{192,128},{1,193},{65,1},{129,65},{193,129... | collective-permute-start | bytes 2752520 | tf_op jit(solution)/shard_map/ppermute | solution.py:305
  56.2 1.1 collective-permute-start.15
  57.4 2.2 %collective-permute-start.16 = (bf16[4,2,112,256]{3,2,1,0:T(8,128)(2,1)S(1)}, bf16[4,2,112,256]{3,2,1,0:T(8,128)(2,1)}, u32[]{:S(2)}, u32[]{:S(2)}) collective-permute-start(bf16[4,2,112,256]{3,2,1,0:T(8,128)(2,1)S(1)} %collective-permute-done.10.refs_8_), channel_id=1, source_target_pairs={{0,49},{16,0},{32,16},{48,32},{1,48},{17,1},{33,17},{49,33},{2,51}... | collective-permute-start | bytes 1376264 | tf_op jit(solution)/shard_map/ppermute | solution.py:310
  62.9 5.9 %collective-permute-done.15.refs_9_ = bf16[4,2,112,256]{3,2,1,0:T(8,128)(2,1)} collective-permute-done((bf16[4,2,112,256]{3,2,1,0:T(8,128)(2,1)S(1)}, bf16[4,2,112,256]{3,2,1,0:T(8,128)(2,1)}, u32[]{:S(2)}, u32[]{:S(2)}) %collective-permute-start.15) | collective-permute-done | bytes 458784 | tf_op jit(solution)/shard_map/ppermute | solution.py:310
  68.8 1.9 %constant_dynamic-update-slice_fusion.7 = bf16[20,2,112,256]{3,2,1,0:T(8,128)(2,1)} fusion(bf16[20,2,112,256]{3,2,1,0:T(8,128)(2,1)} %constant_dynamic-update-slice_fusion.8, bf16[4,2,112,256]{3,2,1,0:T(8,128)(2,1)} %collective-permute-done.15.refs_9_), kind=kLoop, calls=%fused_computation.48 | loop fusion | bytes 917504
  70.7 1.9 %constant_dynamic-update-slice_fusion.6 = bf16[20,2,112,256]{3,2,1,0:T(8,128)(2,1)} fusion(bf16[20,2,112,256]{3,2,1,0:T(8,128)(2,1)} %constant_dynamic-update-slice_fusion.7, bf16[4,2,112,256]{3,2,1,0:T(8,128)(2,1)} %collective-permute-done.16.refs_10_), kind=kLoop, calls=%fused_computation.47 | loop fusion | bytes 917504 | tf_op jit(solution)/shard_map/concatenate | solution.py:350
  72.6 1.0 collective-permute-done.17.refs_19_.refs_1_
  73.6 2.4 %collective-permute-start.26 = (bf16[4,2,112,256]{3,2,1,0:T(8,128)(2,1)}, bf16[4,2,112,256]{3,2,1,0:T(8,128)(2,1)S(1)}, u32[]{:S(2)}, u32[]{:S(2)}) collective-permute-start(bf16[4,2,112,256]{3,2,1,0:T(8,128)(2,1)} %collective-permute-done.16.refs_10_), channel_id=1, source_target_pairs={{0,49},{16,0},{32,16},{48,32},{1,48},{17,1},{33,17},{49,33},{2,51}... | collective-permute-start | bytes 1376264 | tf_op jit(solution)/shard_map/ppermute | solution.py:310
  75.9 1.0 constant_dynamic-update-slice_fusion.1
  77.9 1.0 constant_dynamic-update-slice_fusion
  79.0 1.1 slice.108
  80.7 2.0 %collective-permute-start.19 = (bf16[4,2,112,256]{3,2,1,0:T(8,128)(2,1)S(1)}, bf16[4,2,112,256]{3,2,1,0:T(8,128)(2,1)S(1)}, u32[]{:S(2)}, u32[]{:S(2)}) collective-permute-start(bf16[4,2,112,256]{3,2,1,0:T(8,128)(2,1)S(1)} %slice.108), channel_id=1, source_target_pairs={{0,64},{64,128},{128,192},{192,0},{1,65},{65,129},{129,193},{193,1... | collective-permute-start | bytes 1376264 | tf_op jit(solution)/shard_map/ppermute | solution.py:305
  82.7 1.1 slice.110
  84.4 2.9 %collective-permute-start.29 = (bf16[2,2,112,256]{3,2,1,0:T(8,128)(2,1)S(1)}, bf16[2,2,112,256]{3,2,1,0:T(8,128)(2,1)S(1)}, u32[]{:S(2)}, u32[]{:S(2)}) collective-permute-start(bf16[2,2,112,256]{3,2,1,0:T(8,128)(2,1)S(1)} %slice.111), channel_id=1, source_target_pairs={{0,49},{16,0},{32,16},{48,32},{1,48},{17,1},{33,17},{49,33},{2,51}... | collective-permute-start | bytes 688136 | tf_op jit(solution)/shard_map/ppermute | solution.py:310
  88.0 1.6 bitcast_dynamic-update-slice_fusion
  89.6 2.9 %collective-permute-done.28.refs_13_ = bf16[2,2,112,256]{3,2,1,0:T(8,128)(2,1)S(1)} collective-permute-done((bf16[2,2,112,256]{3,2,1,0:T(8,128)(2,1)S(1)}, bf16[2,2,112,256]{3,2,1,0:T(8,128)(2,1)S(1)}, u32[]{:S(2)}, u32[]{:S(2)}) %collective-permute-start.28) | collective-permute-done | bytes 229408 | tf_op jit(solution)/shard_map/ppermute | solution.py:310
  92.6 1.3 collective-permute-start.20
  94.5 2.2 %pad_maximum_fusion.1 = bf16[8,2,112,256]{3,2,1,0:T(8,128)(2,1)} fusion(bf16[4,2,112,256]{3,2,1,0:T(8,128)(2,1)S(1)} %collective-permute-done.26.refs_12_, bf16[4,2,112,256]{3,2,1,0:T(8,128)(2,1)} %collective-permute-done.25.refs_11_), kind=kLoop, calls=%fused_computation.3 | loop fusion | flops 458752 | bytes 1835008 | tf_op jit(solution)/shard_map/concatenate | solution.py:351
  96.7 9.0 %collective-permute-done.20.refs_22_.refs_4_ = bf16[4,2,112,256]{3,2,1,0:T(8,128)(2,1)S(1)} collective-permute-done((bf16[4,2,112,256]{3,2,1,0:T(8,128)(2,1)S(1)}, bf16[4,2,112,256]{3,2,1,0:T(8,128)(2,1)S(1)}, u32[]{:S(2)}, u32[]{:S(2)}) %collective-permute-start.20) | collective-permute-done | bytes 458784 | tf_op jit(solution)/shard_map/ppermute | solution.py:305
  106.4 1.0 pad_maximum_fusion
  109.5 1.6 collective-permute-done.22.refs_24_.refs_6_
  111.1 1.5 copy-done
  112.6 15.6 %head.1 = (bf16[4,512,128]{2,1,0:T(8,128)(2,1)}, bf16[1024,128]{1,0:T(8,128)(2,1)}, bf16[1024,128]{1,0:T(8,128)(2,1)}, bf16[128,1792]{1,0:T(8,128)(2,1)}, bf16[128,1792]{1,0:T(8,128)(2,1)}) custom-call(s32[8]{0:T(128)} %bitcast.92, s32[8,8]{1,0:T(8,128)} %bitcast.89, s32[162]{0:T(256)} %concatenate.27.tab, bf16[2,4,112,256]{3,2,1,0:T(8,128)(2,1)} %copy-done.11, ...), custom_call_target="tpu_custom_call" | custom-call | flops 3758096384 | bytes 25690112 | tf_op jit(solution)/shard_map/head/pallas_call | solution.py:250
  128.5 1.8 %collective-permute-start.35 = (bf16[128,1792]{1,0:T(8,128)(2,1)}, bf16[128,1792]{1,0:T(8,128)(2,1)S(1)}, u32[]{:S(2)}, u32[]{:S(2)}) collective-permute-start(bf16[128,1792]{1,0:T(8,128)(2,1)} %get-tuple-element.48), channel_id=1, source_target_pairs={{0,6},{2,0},{4,2},{6,4},{1,7},{3,1},{5,3},{7,5},{8,14},{10,8},{12,... | collective-permute-start | bytes 1376264 | tf_op jit(solution)/shard_map/ppermute | solution.py:375
  130.3 9.8 %tail.3 = (bf16[128,3584]{1,0:T(8,128)(2,1)}, bf16[128,3584]{1,0:T(8,128)(2,1)}) custom-call(s32[8]{0:T(128)} %bitcast.93, s32[8,8]{1,0:T(8,128)} %bitcast.90, s32[162]{0:T(256)} %concatenate.27.tab, bf16[8,2,112,256]{3,2,1,0:T(8,128)(2,1)} %copy-done.4, bf16[8,2,112,256]{3,2,1,0:T(8,128)(2,1)} %copy-done.1, bf16[8,2,112,256]{3,2,1,0:T(8,128)(2,1)} %copy-done.2, ...), custom_call_target="tpu_custom_call" | custom-call | flops 1476395008 | bytes 7340032 | tf_op jit(solution)/shard_map/tail/pallas_call | solution.py:284
  140.1 1.9 %fusion.1 = bf16[128,3584]{1,0:T(8,128)(2,1)} fusion(bf16[128,3584]{1,0:T(8,128)(2,1)} %get-tuple-element.45, bf16[128,1792]{1,0:T(8,128)(2,1)S(1)} %collective-permute-done.33), kind=kLoop, calls=%fused_computation.6 | loop fusion | flops 917504 | bytes 1376256 | tf_op jit(solution)/shard_map/dynamic_update_slice | solution.py:377
  142.1 1.5 collective-permute-start.34
  143.6 1.9 %fusion.2 = bf16[128,3584]{1,0:T(8,128)(2,1)} fusion(bf16[128,3584]{1,0:T(8,128)(2,1)} %get-tuple-element.47, bf16[128,1792]{1,0:T(8,128)(2,1)S(1)} %collective-permute-done.35), kind=kLoop, calls=%fused_computation.7 | loop fusion | flops 917504 | bytes 1376256 | tf_op jit(solution)/shard_map/dynamic_update_slice | solution.py:378
  146.0 7.3 %tail.2 = bf16[128,3584]{1,0:T(8,128)(2,1)} custom-call(s32[8]{0:T(128)} %bitcast.94, s32[8,8]{1,0:T(8,128)} %bitcast.91, s32[162]{0:T(256)} %concatenate.27.tab, bf16[8,2,112,256]{3,2,1,0:T(8,128)(2,1)} %copy-done.4, bf16[8,2,112,256]{3,2,1,0:T(8,128)(2,1)} %copy-done.1, bf16[8,2,112,256]{3,2,1,0:T(8,128)(2,1)} %copy-done.2, ...), custom_call_target="tpu_custom_call" | custom-call | flops 738197504 | bytes 7340032 | tf_op jit(solution)/shard_map/tail/pallas_call | solution.py:284
  153.4 9.9 %collective-permute-done.34 = bf16[128,3584]{1,0:T(8,128)(2,1)S(1)} collective-permute-done((bf16[128,3584]{1,0:T(8,128)(2,1)}, bf16[128,3584]{1,0:T(8,128)(2,1)S(1)}, u32[]{:S(2)}, u32[]{:S(2)}) %collective-permute-start.34) | collective-permute-done | bytes 917536 | tf_op jit(solution)/shard_map/ppermute | solution.py:379
  163.2 4.4 %collective-permute-done.36 = bf16[128,3584]{1,0:T(8,128)(2,1)S(1)} collective-permute-done((bf16[128,3584]{1,0:T(8,128)(2,1)}, bf16[128,3584]{1,0:T(8,128)(2,1)S(1)}, u32[]{:S(2)}, u32[]{:S(2)}) %collective-permute-start.36) | collective-permute-done | bytes 917536 | tf_op jit(solution)/shard_map/ppermute | solution.py:380
  167.7 2.4 %fusion = bf16[1,128,3584]{2,1,0:T(8,128)(2,1)} fusion(bf16[128,3584]{1,0:T(8,128)(2,1)S(1)} %collective-permute-done.36, bf16[128,3584]{1,0:T(8,128)(2,1)S(1)} %collective-permute-done.34, bf16[128,3584]{1,0:T(8,128)(2,1)} %tail.2), kind=kLoop, calls=%fused_computation.1 | loop fusion | flops 2752512 | bytes 3670016 | tf_op jit(solution)/shard_map/broadcast_in_dim | solution.py:382
  (137 shorter events, 23.7 us)
Async XLA Ops:
  1.8 16.7 %collective-permute-start.3 = (bf16[4,112,256]{2,1,0:T(8,128)(2,1)S(1)}, bf16[4,112,256]{2,1,0:T(8,128)(2,1)S(1)}, u32[]{:S(2)}, u32[]{:S(2)}) collective-permute-start(bf16[4,112,256]{2,1,0:T(8,128)(2,1)S(1)} %fusion.3), channel_id=1, source_target_pairs={{0,16},{16,32},{32,48},{48,1},{1,17},{17,33},{33,49},{49,0},{2,18}... | collective-permute-start | bytes 688136 | tf_op jit(solution)/shard_map/ppermute | solution.py:310
  3.8 14.9 %collective-permute-start.6 = (bf16[4,112,256]{2,1,0:T(8,128)(2,1)S(1)}, bf16[4,112,256]{2,1,0:T(8,128)(2,1)S(1)}, u32[]{:S(2)}, u32[]{:S(2)}) collective-permute-start(bf16[4,112,256]{2,1,0:T(8,128)(2,1)S(1)} %fusion.3), channel_id=1, source_target_pairs={{0,49},{16,0},{32,16},{48,32},{1,48},{17,1},{33,17},{49,33},{2,51}... | collective-permute-start | bytes 688136 | tf_op jit(solution)/shard_map/ppermute | solution.py:310
  7.8 6.6 %collective-permute-start = (bf16[2,112,256]{2,1,0:T(8,128)(2,1)}, bf16[2,112,256]{2,1,0:T(8,128)(2,1)S(1)}, u32[]{:S(2)}, u32[]{:S(2)}) collective-permute-start(bf16[2,112,256]{2,1,0:T(8,128)(2,1)} %param.19), channel_id=1, source_target_pairs={{0,64},{64,128},{128,192},{192,0},{1,65},{65,129},{129,193},{193,1... | collective-permute-start | bytes 344072 | tf_op jit(solution)/shard_map/ppermute | solution.py:305
  9.3 6.1 %collective-permute-start.1 = (bf16[2,112,256]{2,1,0:T(8,128)(2,1)}, bf16[2,112,256]{2,1,0:T(8,128)(2,1)S(1)}, u32[]{:S(2)}, u32[]{:S(2)}) collective-permute-start(bf16[2,112,256]{2,1,0:T(8,128)(2,1)} %param.19), channel_id=1, source_target_pairs={{0,192},{64,0},{128,64},{192,128},{1,193},{65,1},{129,65},{193,129... | collective-permute-start | bytes 344072 | tf_op jit(solution)/shard_map/ppermute | solution.py:305
  11.0 6.5 %collective-permute-start.2 = (bf16[2,112,256]{2,1,0:T(8,128)(2,1)}, bf16[2,112,256]{2,1,0:T(8,128)(2,1)S(1)}, u32[]{:S(2)}, u32[]{:S(2)}) collective-permute-start(bf16[2,112,256]{2,1,0:T(8,128)(2,1)} %param.19), channel_id=1, source_target_pairs={{0,128},{64,192},{128,0},{192,64},{1,129},{65,193},{129,1},{193,65... | collective-permute-start | bytes 344072 | tf_op jit(solution)/shard_map/ppermute | solution.py:305
  18.5 30.6 %copy-start.7 = (bf16[4,2,112,256]{3,2,1,0:T(8,128)(2,1)}, bf16[4,2,112,256]{3,2,1,0:T(8,128)(2,1)S(1)}, u32[]{:S(2)}) copy-start(bf16[4,2,112,256]{3,2,1,0:T(8,128)(2,1)S(1)} %pad_maximum_fusion.2.refs_6_) | copy-start | bytes 1376260
  18.6 6.7 %collective-permute-start.4 = (bf16[3,112,256]{2,1,0:T(8,128)(2,1)S(1)}, bf16[3,112,256]{2,1,0:T(8,128)(2,1)S(1)}, u32[]{:S(2)}, u32[]{:S(2)}) collective-permute-start(bf16[3,112,256]{2,1,0:T(8,128)(2,1)S(1)} %slice.96), channel_id=1, source_target_pairs={{0,16},{16,32},{32,48},{48,1},{1,17},{17,33},{33,49},{49,0},{2,18}... | collective-permute-start | bytes 516104 | tf_op jit(solution)/shard_map/ppermute | solution.py:310
  18.7 6.6 %collective-permute-start.7 = (bf16[3,112,256]{2,1,0:T(8,128)(2,1)S(1)}, bf16[3,112,256]{2,1,0:T(8,128)(2,1)S(1)}, u32[]{:S(2)}, u32[]{:S(2)}) collective-permute-start(bf16[3,112,256]{2,1,0:T(8,128)(2,1)S(1)} %slice.98), channel_id=1, source_target_pairs={{0,49},{16,0},{32,16},{48,32},{1,48},{17,1},{33,17},{49,33},{2,51}... | collective-permute-start | bytes 516104 | tf_op jit(solution)/shard_map/ppermute | solution.py:310
  25.4 34.2 %copy-start.11 = (bf16[2,4,112,256]{3,2,1,0:T(8,128)(2,1)}, bf16[2,4,112,256]{3,2,1,0:T(8,128)(2,1)S(1)}, u32[]{:S(2)}) copy-start(bf16[2,4,112,256]{3,2,1,0:T(8,128)(2,1)S(1)} %pad_maximum_fusion.3.refs_0_) | copy-start | bytes 1376260
  25.4 27.5 %collective-permute-start.13 = (bf16[2,4,112,256]{3,2,1,0:T(8,128)(2,1)S(1)}, bf16[2,4,112,256]{3,2,1,0:T(8,128)(2,1)S(1)}, u32[]{:S(2)}, u32[]{:S(2)}) collective-permute-start(bf16[2,4,112,256]{3,2,1,0:T(8,128)(2,1)S(1)} %pad_maximum_fusion.3.refs_0_), channel_id=1, source_target_pairs={{0,64},{64,128},{128,192},{192,0},{1,65},{65,129},{129,193},{193,1... | collective-permute-start | bytes 1376264 | tf_op jit(solution)/shard_map/ppermute | solution.py:305
  26.4 29.8 %collective-permute-start.14 = (bf16[2,4,112,256]{3,2,1,0:T(8,128)(2,1)S(1)}, bf16[2,4,112,256]{3,2,1,0:T(8,128)(2,1)S(1)}, u32[]{:S(2)}, u32[]{:S(2)}) collective-permute-start(bf16[2,4,112,256]{3,2,1,0:T(8,128)(2,1)S(1)} %pad_maximum_fusion.3.refs_0_), channel_id=1, source_target_pairs={{0,192},{64,0},{128,64},{192,128},{1,193},{65,1},{129,65},{193,129... | collective-permute-start | bytes 1376264 | tf_op jit(solution)/shard_map/ppermute | solution.py:305
  29.5 6.1 %collective-permute-start.5 = (bf16[2,112,256]{2,1,0:T(8,128)(2,1)S(1)}, bf16[2,112,256]{2,1,0:T(8,128)(2,1)S(1)}, u32[]{:S(2)}, u32[]{:S(2)}) collective-permute-start(bf16[2,112,256]{2,1,0:T(8,128)(2,1)S(1)} %slice.97), channel_id=1, source_target_pairs={{0,16},{16,32},{32,48},{48,1},{1,17},{17,33},{33,49},{49,0},{2,18}... | collective-permute-start | bytes 344072 | tf_op jit(solution)/shard_map/ppermute | solution.py:310
  29.6 6.2 %collective-permute-start.8 = (bf16[2,112,256]{2,1,0:T(8,128)(2,1)S(1)}, bf16[2,112,256]{2,1,0:T(8,128)(2,1)S(1)}, u32[]{:S(2)}, u32[]{:S(2)}) collective-permute-start(bf16[2,112,256]{2,1,0:T(8,128)(2,1)S(1)} %slice.99), channel_id=1, source_target_pairs={{0,49},{16,0},{32,16},{48,32},{1,48},{17,1},{33,17},{49,33},{2,51}... | collective-permute-start | bytes 344072 | tf_op jit(solution)/shard_map/ppermute | solution.py:310
  35.8 20.4 %collective-permute-start.10 = (bf16[4,2,112,256]{3,2,1,0:T(8,128)(2,1)S(1)}, bf16[4,2,112,256]{3,2,1,0:T(8,128)(2,1)S(1)}, u32[]{:S(2)}, u32[]{:S(2)}) collective-permute-start(bf16[4,2,112,256]{3,2,1,0:T(8,128)(2,1)S(1)} %pad_maximum_fusion.2.refs_6_), channel_id=1, source_target_pairs={{0,49},{16,0},{32,16},{48,32},{1,48},{17,1},{33,17},{49,33},{2,51}... | collective-permute-start | bytes 1376264 | tf_op jit(solution)/shard_map/ppermute | solution.py:310
  39.5 16.8 %collective-permute-start.9 = (bf16[4,2,112,256]{3,2,1,0:T(8,128)(2,1)S(1)}, bf16[4,2,112,256]{3,2,1,0:T(8,128)(2,1)S(1)}, u32[]{:S(2)}, u32[]{:S(2)}) collective-permute-start(bf16[4,2,112,256]{3,2,1,0:T(8,128)(2,1)S(1)} %pad_maximum_fusion.2.refs_6_), channel_id=1, source_target_pairs={{0,16},{16,32},{32,48},{48,1},{1,17},{17,33},{33,49},{49,0},{2,18}... | collective-permute-start | bytes 1376264 | tf_op jit(solution)/shard_map/ppermute | solution.py:310
  39.8 7.1 %collective-permute-start.12 = (bf16[112,256]{1,0:T(8,128)(2,1)S(1)}, bf16[112,256]{1,0:T(8,128)(2,1)S(1)}, u32[]{:S(2)}, u32[]{:S(2)}) collective-permute-start(bf16[112,256]{1,0:T(8,128)(2,1)S(1)} %slice_bitcast_fusion.4), channel_id=1, source_target_pairs={{0,49},{16,0},{32,16},{48,32},{1,48},{17,1},{33,17},{49,33},{2,51}... | collective-permute-start | bytes 172040 | tf_op jit(solution)/shard_map/ppermute | solution.py:310
  46.9 5.4 %collective-permute-start.11 = (bf16[112,256]{1,0:T(8,128)(2,1)S(1)}, bf16[112,256]{1,0:T(8,128)(2,1)S(1)}, u32[]{:S(2)}, u32[]{:S(2)}) collective-permute-start(bf16[112,256]{1,0:T(8,128)(2,1)S(1)} %slice_bitcast_fusion.5), channel_id=1, source_target_pairs={{0,16},{16,32},{32,48},{48,1},{1,17},{17,33},{33,49},{49,0},{2,18}... | collective-permute-start | bytes 172040 | tf_op jit(solution)/shard_map/ppermute | solution.py:310
  53.0 20.6 %collective-permute-start.17 = (bf16[8,2,112,256]{3,2,1,0:T(8,128)(2,1)S(1)}, bf16[8,2,112,256]{3,2,1,0:T(8,128)(2,1)S(1)}, u32[]{:S(2)}, u32[]{:S(2)}) collective-permute-start(bf16[8,2,112,256]{3,2,1,0:T(8,128)(2,1)S(1)} %get-tuple-element.64.refs_18_.refs_0_), channel_id=1, source_target_pairs={{0,64},{64,128},{128,192},{192,0},{1,65},{65,129},{129,193},{193,1... | collective-permute-start | bytes 2752520 | tf_op jit(solution)/shard_map/ppermute | solution.py:305
  53.0 23.9 %collective-permute-start.18 = (bf16[8,2,112,256]{3,2,1,0:T(8,128)(2,1)S(1)}, bf16[8,2,112,256]{3,2,1,0:T(8,128)(2,1)S(1)}, u32[]{:S(2)}, u32[]{:S(2)}) collective-permute-start(bf16[8,2,112,256]{3,2,1,0:T(8,128)(2,1)S(1)} %get-tuple-element.64.refs_18_.refs_0_), channel_id=1, source_target_pairs={{0,192},{64,0},{128,64},{192,128},{1,193},{65,1},{129,65},{193,129... | collective-permute-start | bytes 2752520 | tf_op jit(solution)/shard_map/ppermute | solution.py:305
  56.2 12.6 %collective-permute-start.15 = (bf16[4,2,112,256]{3,2,1,0:T(8,128)(2,1)S(1)}, bf16[4,2,112,256]{3,2,1,0:T(8,128)(2,1)}, u32[]{:S(2)}, u32[]{:S(2)}) collective-permute-start(bf16[4,2,112,256]{3,2,1,0:T(8,128)(2,1)S(1)} %collective-permute-done.9.refs_7_), channel_id=1, source_target_pairs={{0,16},{16,32},{32,48},{48,1},{1,17},{17,33},{33,49},{49,0},{2,18}... | collective-permute-start | bytes 1376264 | tf_op jit(solution)/shard_map/ppermute | solution.py:310
  57.4 11.5 %collective-permute-start.16 = (bf16[4,2,112,256]{3,2,1,0:T(8,128)(2,1)S(1)}, bf16[4,2,112,256]{3,2,1,0:T(8,128)(2,1)}, u32[]{:S(2)}, u32[]{:S(2)}) collective-permute-start(bf16[4,2,112,256]{3,2,1,0:T(8,128)(2,1)S(1)} %collective-permute-done.10.refs_8_), channel_id=1, source_target_pairs={{0,49},{16,0},{32,16},{48,32},{1,48},{17,1},{33,17},{49,33},{2,51}... | collective-permute-start | bytes 1376264 | tf_op jit(solution)/shard_map/ppermute | solution.py:310
  59.6 20.6 %collective-permute-start.23 = (bf16[4,112,256]{2,1,0:T(8,128)(2,1)S(1)}, bf16[4,112,256]{2,1,0:T(8,128)(2,1)S(1)}, u32[]{:S(2)}, u32[]{:S(2)}) collective-permute-start(bf16[4,112,256]{2,1,0:T(8,128)(2,1)S(1)} %slice_bitcast_fusion.1), channel_id=1, source_target_pairs={{0,64},{64,128},{128,192},{192,0},{1,65},{65,129},{129,193},{193,1... | collective-permute-start | bytes 688136 | tf_op jit(solution)/shard_map/ppermute | solution.py:305
  61.3 11.3 %copy-start.21 = (s32[1,4,1]{1,2,0:T(1,128)S(1)}, s32[1,4,1]{1,2,0:T(1,128)}, u32[]{:S(2)}) copy-start(s32[1,4,1]{1,2,0:T(1,128)} %constant.74.clone) | copy-start | bytes 52
  61.3 11.3 %copy-start.18 = (s32[1,1,4]{2,1,0:T(1,128)S(1)}, s32[1,1,4]{2,1,0:T(1,128)}, u32[]{:S(2)}) copy-start(s32[1,1,4]{2,1,0:T(1,128)} %constant.19.clone) | copy-start | bytes 52
  68.8 11.9 %collective-permute-start.24 = (bf16[4,112,256]{2,1,0:T(8,128)(2,1)S(1)}, bf16[4,112,256]{2,1,0:T(8,128)(2,1)}, u32[]{:S(2)}, u32[]{:S(2)}) collective-permute-start(bf16[4,112,256]{2,1,0:T(8,128)(2,1)S(1)} %slice_bitcast_fusion), channel_id=1, source_target_pairs={{0,192},{64,0},{128,64},{192,128},{1,193},{65,1},{129,65},{193,129... | collective-permute-start | bytes 688136 | tf_op jit(solution)/shard_map/ppermute | solution.py:305
  68.8 13.9 %collective-permute-start.25 = (bf16[4,2,112,256]{3,2,1,0:T(8,128)(2,1)}, bf16[4,2,112,256]{3,2,1,0:T(8,128)(2,1)}, u32[]{:S(2)}, u32[]{:S(2)}) collective-permute-start(bf16[4,2,112,256]{3,2,1,0:T(8,128)(2,1)} %collective-permute-done.15.refs_9_), channel_id=1, source_target_pairs={{0,16},{16,32},{32,48},{48,1},{1,17},{17,33},{33,49},{49,0},{2,18}... | collective-permute-start | bytes 1376264 | tf_op jit(solution)/shard_map/ppermute | solution.py:310
  73.6 9.2 %collective-permute-start.26 = (bf16[4,2,112,256]{3,2,1,0:T(8,128)(2,1)}, bf16[4,2,112,256]{3,2,1,0:T(8,128)(2,1)S(1)}, u32[]{:S(2)}, u32[]{:S(2)}) collective-permute-start(bf16[4,2,112,256]{3,2,1,0:T(8,128)(2,1)} %collective-permute-done.16.refs_10_), channel_id=1, source_target_pairs={{0,49},{16,0},{32,16},{48,32},{1,48},{17,1},{33,17},{49,33},{2,51}... | collective-permute-start | bytes 1376264 | tf_op jit(solution)/shard_map/ppermute | solution.py:310
  78.9 13.7 %copy-start.3 = (bf16[8,2,112,256]{3,2,1,0:T(8,128)(2,1)S(1)}, bf16[8,2,112,256]{3,2,1,0:T(8,128)(2,1)}, u32[]{:S(2)}) copy-start(bf16[8,2,112,256]{3,2,1,0:T(8,128)(2,1)} %copy-done.2) | copy-start | bytes 2752516
  78.9 32.2 %collective-permute-start.21 = (bf16[24,2,112,256]{3,2,1,0:T(8,128)(2,1)}, bf16[24,2,112,256]{3,2,1,0:T(8,128)(2,1)S(1)}, u32[]{:S(2)}, u32[]{:S(2)}) collective-permute-start(bf16[24,2,112,256]{3,2,1,0:T(8,128)(2,1)} %constant_dynamic-update-slice_fusion), channel_id=1, source_target_pairs={{0,8},{8,0},{1,9},{9,1},{2,10},{10,2},{3,11},{11,3},{4,12},{12,4},... | collective-permute-start | bytes 8257544 | tf_op jit(solution)/shard_map/ppermute | solution.py:314
  79.0 15.4 %copy-start.20 = (s32[1,1,8]{2,1,0:T(1,128)S(1)}, s32[1,1,8]{2,1,0:T(1,128)}, u32[]{:S(2)}) copy-start(s32[1,1,8]{2,1,0:T(1,128)} %constant.20.clone) | copy-start | bytes 100
  80.2 30.9 %copy-start.16 = (bf16[4,112,256]{2,1,0:T(8,128)(2,1)}, bf16[4,112,256]{2,1,0:T(8,128)(2,1)S(1)}, u32[]{:S(2)}) copy-start(bf16[4,112,256]{2,1,0:T(8,128)(2,1)S(1)} %collective-permute-done.23.refs_3_) | copy-start | bytes 688132
  80.2 30.9 %collective-permute-start.30 = (bf16[20,2,112,256]{3,2,1,0:T(8,128)(2,1)}, bf16[20,2,112,256]{3,2,1,0:T(8,128)(2,1)}, u32[]{:S(2)}, u32[]{:S(2)}) collective-permute-start(bf16[20,2,112,256]{3,2,1,0:T(8,128)(2,1)} %constant_dynamic-update-slice_fusion.6), channel_id=1, source_target_pairs={{0,8},{8,0},{1,9},{9,1},{2,10},{10,2},{3,11},{11,3},{4,12},{12,4},... | collective-permute-start | bytes 6881288 | tf_op jit(solution)/shard_map/ppermute | solution.py:314
  80.7 13.7 %collective-permute-start.19 = (bf16[4,2,112,256]{3,2,1,0:T(8,128)(2,1)S(1)}, bf16[4,2,112,256]{3,2,1,0:T(8,128)(2,1)S(1)}, u32[]{:S(2)}, u32[]{:S(2)}) collective-permute-start(bf16[4,2,112,256]{3,2,1,0:T(8,128)(2,1)S(1)} %slice.108), channel_id=1, source_target_pairs={{0,64},{64,128},{128,192},{192,0},{1,65},{65,129},{129,193},{193,1... | collective-permute-start | bytes 1376264 | tf_op jit(solution)/shard_map/ppermute | solution.py:305
  82.7 13.9 %copy-start.10 = (bf16[4,2,112,256]{3,2,1,0:T(8,128)(2,1)}, bf16[4,2,112,256]{3,2,1,0:T(8,128)(2,1)S(1)}, u32[]{:S(2)}) copy-start(bf16[4,2,112,256]{3,2,1,0:T(8,128)(2,1)S(1)} %collective-permute-done.26.refs_12_) | copy-start | bytes 1376260
  83.9 8.6 %collective-permute-start.28 = (bf16[2,2,112,256]{3,2,1,0:T(8,128)(2,1)S(1)}, bf16[2,2,112,256]{3,2,1,0:T(8,128)(2,1)S(1)}, u32[]{:S(2)}, u32[]{:S(2)}) collective-permute-start(bf16[2,2,112,256]{3,2,1,0:T(8,128)(2,1)S(1)} %slice.110), channel_id=1, source_target_pairs={{0,16},{16,32},{32,48},{48,1},{1,17},{17,33},{33,49},{49,0},{2,18}... | collective-permute-start | bytes 688136 | tf_op jit(solution)/shard_map/ppermute | solution.py:310
  84.4 8.2 %collective-permute-start.29 = (bf16[2,2,112,256]{3,2,1,0:T(8,128)(2,1)S(1)}, bf16[2,2,112,256]{3,2,1,0:T(8,128)(2,1)S(1)}, u32[]{:S(2)}, u32[]{:S(2)}) collective-permute-start(bf16[2,2,112,256]{3,2,1,0:T(8,128)(2,1)S(1)} %slice.111), channel_id=1, source_target_pairs={{0,49},{16,0},{32,16},{48,32},{1,48},{17,1},{33,17},{49,33},{2,51}... | collective-permute-start | bytes 688136 | tf_op jit(solution)/shard_map/ppermute | solution.py:310
  92.5 15.0 %copy-start.14 = (bf16[2,2,112,256]{3,2,1,0:T(8,128)(2,1)}, bf16[2,2,112,256]{3,2,1,0:T(8,128)(2,1)S(1)}, u32[]{:S(2)}) copy-start(bf16[2,2,112,256]{3,2,1,0:T(8,128)(2,1)S(1)} %collective-permute-done.28.refs_13_) | copy-start | bytes 688132
  92.5 18.6 %collective-permute-start.27 = (bf16[8,4,112,256]{3,2,1,0:T(8,128)(2,1)}, bf16[8,4,112,256]{3,2,1,0:T(8,128)(2,1)}, u32[]{:S(2)}, u32[]{:S(2)}) collective-permute-start(bf16[8,4,112,256]{3,2,1,0:T(8,128)(2,1)} %bitcast_dynamic-update-slice_fusion), channel_id=1, source_target_pairs={{0,8},{8,0},{1,9},{9,1},{2,10},{10,2},{3,11},{11,3},{4,12},{12,4},... | collective-permute-start | bytes 5505032 | tf_op jit(solution)/shard_map/ppermute | solution.py:314
  92.6 16.0 %copy-start.19 = (s32[1,8,1]{1,2,0:T(1,128)S(1)}, s32[1,8,1]{1,2,0:T(1,128)}, u32[]{:S(2)}) copy-start(s32[1,8,1]{1,2,0:T(1,128)} %constant.18.clone) | copy-start | bytes 100
  92.6 13.0 %collective-permute-start.20 = (bf16[4,2,112,256]{3,2,1,0:T(8,128)(2,1)S(1)}, bf16[4,2,112,256]{3,2,1,0:T(8,128)(2,1)S(1)}, u32[]{:S(2)}, u32[]{:S(2)}) collective-permute-start(bf16[4,2,112,256]{3,2,1,0:T(8,128)(2,1)S(1)} %slice.109), channel_id=1, source_target_pairs={{0,192},{64,0},{128,64},{192,128},{1,193},{65,1},{129,65},{193,129... | collective-permute-start | bytes 1376264 | tf_op jit(solution)/shard_map/ppermute | solution.py:305
  94.4 16.7 %copy-start.5 = (bf16[4,2,112,256]{3,2,1,0:T(8,128)(2,1)}, bf16[4,2,112,256]{3,2,1,0:T(8,128)(2,1)S(1)}, u32[]{:S(2)}) copy-start(bf16[4,2,112,256]{3,2,1,0:T(8,128)(2,1)S(1)} %collective-permute-done.19.refs_21_.refs_3_) | copy-start | bytes 1376260
  94.4 13.0 %collective-permute-start.32 = (bf16[4,2,112,256]{3,2,1,0:T(8,128)(2,1)S(1)}, bf16[4,2,112,256]{3,2,1,0:T(8,128)(2,1)S(1)}, u32[]{:S(2)}, u32[]{:S(2)}) collective-permute-start(bf16[4,2,112,256]{3,2,1,0:T(8,128)(2,1)S(1)} %pad_maximum_fusion.4), channel_id=1, source_target_pairs={{0,8},{8,0},{1,9},{9,1},{2,10},{10,2},{3,11},{11,3},{4,12},{12,4},... | collective-permute-start | bytes 1376264 | tf_op jit(solution)/shard_map/ppermute | solution.py:314
  105.6 3.8 %collective-permute-start.31 = (bf16[8,2,112,256]{3,2,1,0:T(8,128)(2,1)}, bf16[8,2,112,256]{3,2,1,0:T(8,128)(2,1)}, u32[]{:S(2)}, u32[]{:S(2)}) collective-permute-start(bf16[8,2,112,256]{3,2,1,0:T(8,128)(2,1)} %pad_maximum_fusion.1), channel_id=1, source_target_pairs={{0,8},{8,0},{1,9},{9,1},{2,10},{10,2},{3,11},{11,3},{4,12},{12,4},... | collective-permute-start | bytes 2752520 | tf_op jit(solution)/shard_map/ppermute | solution.py:314
  108.3 2.8 %collective-permute-start.22 = (bf16[8,2,112,256]{3,2,1,0:T(8,128)(2,1)}, bf16[8,2,112,256]{3,2,1,0:T(8,128)(2,1)}, u32[]{:S(2)}, u32[]{:S(2)}) collective-permute-start(bf16[8,2,112,256]{3,2,1,0:T(8,128)(2,1)} %pad_maximum_fusion), channel_id=1, source_target_pairs={{0,8},{8,0},{1,9},{9,1},{2,10},{10,2},{3,11},{11,3},{4,12},{12,4},... | collective-permute-start | bytes 2752520 | tf_op jit(solution)/shard_map/ppermute | solution.py:314
  128.2 11.9 %collective-permute-start.33 = (bf16[128,1792]{1,0:T(8,128)(2,1)}, bf16[128,1792]{1,0:T(8,128)(2,1)S(1)}, u32[]{:S(2)}, u32[]{:S(2)}) collective-permute-start(bf16[128,1792]{1,0:T(8,128)(2,1)} %get-tuple-element.46), channel_id=1, source_target_pairs={{0,2},{2,4},{4,6},{6,0},{1,3},{3,5},{5,7},{7,1},{8,10},{10,12},{12... | collective-permute-start | bytes 1376264 | tf_op jit(solution)/shard_map/ppermute | solution.py:374
  128.5 15.1 %collective-permute-start.35 = (bf16[128,1792]{1,0:T(8,128)(2,1)}, bf16[128,1792]{1,0:T(8,128)(2,1)S(1)}, u32[]{:S(2)}, u32[]{:S(2)}) collective-permute-start(bf16[128,1792]{1,0:T(8,128)(2,1)} %get-tuple-element.48), channel_id=1, source_target_pairs={{0,6},{2,0},{4,2},{6,4},{1,7},{3,1},{5,3},{7,5},{8,14},{10,8},{12,... | collective-permute-start | bytes 1376264 | tf_op jit(solution)/shard_map/ppermute | solution.py:375
  142.1 21.1 %collective-permute-start.34 = (bf16[128,3584]{1,0:T(8,128)(2,1)}, bf16[128,3584]{1,0:T(8,128)(2,1)S(1)}, u32[]{:S(2)}, u32[]{:S(2)}) collective-permute-start(bf16[128,3584]{1,0:T(8,128)(2,1)} %fusion.1), channel_id=1, source_target_pairs={{0,2},{2,4},{4,6},{6,0},{1,3},{3,5},{5,7},{7,1},{8,10},{10,12},{12... | collective-permute-start | bytes 2752520 | tf_op jit(solution)/shard_map/ppermute | solution.py:379
  145.5 22.1 %collective-permute-start.36 = (bf16[128,3584]{1,0:T(8,128)(2,1)}, bf16[128,3584]{1,0:T(8,128)(2,1)S(1)}, u32[]{:S(2)}, u32[]{:S(2)}) collective-permute-start(bf16[128,3584]{1,0:T(8,128)(2,1)} %fusion.2), channel_id=1, source_target_pairs={{0,6},{2,0},{4,2},{6,4},{1,7},{3,1},{5,3},{7,5},{8,14},{10,8},{12,... | collective-permute-start | bytes 2752520 | tf_op jit(solution)/shard_map/ppermute | solution.py:380
  (11 other events, 49.2 us)

commit v3 on v2

--- a/solution.py
+++ b/solution.py
@@ -124,10 +124,10 @@
 
 
 def head_body(mod, mask, tab, *refs):
-    kv_refs, q_refs, o_refs, x_hbm, tables = refs[:6], refs[6:18], refs[18:25], refs[25], refs[26:30]
-    q, k, v = refs[30:33]
-    outs = refs[33:35]
-    x, wk, wq, wo, att, s, inv, xsem, ksem, qsem, osem = refs[35:]
+    kv_refs, q_refs, o_refs, x_hbm, tables = refs[:7], refs[7:20], refs[20:28], refs[28], refs[29:33]
+    q, k, v = refs[33:36]
+    outs = refs[36:38]
+    x, wk, wq, wo, att, s, inv, xsem, ksem, qsem, osem = refs[38:]
     y0, zh = tab[POS], tab[POS + 1]
     for a in range(4):
 
@@ -138,7 +138,7 @@
             else:
                 for m in range(2):
                     pltpu.make_async_copy(kv_refs[3 + m].at[j], wk.at[m, at[0]], ksem).start()
-            src = kv_refs[5].at[pl.ds(2 * a, 2), j]
+            src = kv_refs[5].at[pl.ds(2 * a, 2), j] if a < 3 else kv_refs[6].at[:, j]
             pltpu.make_async_copy(src, wk.at[:, at[1]], ksem).start()
             return carry
 
@@ -225,7 +225,7 @@
 
 
 def tail_body(first, count, mod, mask, tab, *refs):
-    o_refs, (q, k, v), outs, (wo, att, s, osem) = refs[:7], refs[7:10], refs[10:-4], refs[-4:]
+    o_refs, (q, k, v), outs, (wo, att, s, osem) = refs[:8], refs[8:11], refs[11:-4], refs[-4:]
     y0, zh = tab[POS], tab[POS + 1]
     fetch(tab, O_AT, o_refs, wo, osem)
 
@@ -256,7 +256,7 @@
             HALF_BLOCK,
             HALF_BLOCK,
         ],
-        in_specs=[SM] * 3 + [ANY] * 26 + [VM] * 4,
+        in_specs=[SM] * 3 + [ANY] * 29 + [VM] * 4,
         out_specs=[VM] * 5,
         scratch_shapes=[
             pltpu.VMEM((NBLK + 2, BLK, D), BF),
@@ -284,7 +284,7 @@
     return pl.pallas_call(
         functools.partial(tail_body, first, count),
         out_shape=[jax.ShapeDtypeStruct((BLK, D), BF)] * count,
-        in_specs=[SM] * 3 + [ANY] * 7 + [VM] * 3,
+        in_specs=[SM] * 3 + [ANY] * 8 + [VM] * 3,
         out_specs=[VM] * count,
         scratch_shapes=[
             pltpu.VMEM((2, NG, ROWS, WID), BF),
@@ -329,8 +329,8 @@
     k1p, k1m = along_x(kb, 1), along_x(kb, -1)
     r2p, r2m = r2p[1:], r2m[:2]
     r3p, r3m = along_z(r2p, 1), along_z(r2m, -1)
+    p1p, p1m, p2 = lax.optimization_barrier((p1p, p1m, p2, r3p, r3m))[:3]
     b = jnp.stack([q, p1p, p1m, p2])
-    b, r3p, r3m = lax.optimization_barrier((b, r3p, r3m))
     r4 = jnp.stack([along_z(r3p[0], 1), along_z(r3m[1], -1)])
     t1p, t1m = along_z(b, 1), along_z(b, -1)
     t1p, t1m, _, k1p, k1m = lax.optimization_barrier((t1p, t1m, r4, k1p, k1m))
@@ -338,21 +338,22 @@
     o1p, o1m = along_x(ob, 1), along_x(ob, -1)
     t2p, t2m = along_z(t1p, 1), along_z(t1m, -1)
     k2p, k2m = along_x(k1p[0], 1), along_x(k1m[1], -1)
+    kv_swapped = swap(jnp.concatenate([kb, k1p, k1m]))
     t2p, t2m, at = lax.optimization_barrier((t2p, t2m, at))
     tab = piece_tables(*at)
     t3p, t3m = along_z(t2p, 1), along_z(t2m, -1)
     k2p, k2m = lax.optimization_barrier((k2p, k2m, t3p, t3m))[:2]
     kv_all = [kb, k1p, k1m, k2p, k2m]
-    kv_all.append(swap(jnp.concatenate([kb, k1p, k1m, jnp.stack([k2p, k2m])])))
+    kv_all += [kv_swapped, swap(jnp.stack([k2p, k2m]))]
     o2p, o2m = along_x(o1p[:4], 1), along_x(o1m[4:], -1)
     t4p, t4m = along_z(t3p[:2], 1), along_z(t3m[2:], -1)
     q_all = [b, t1p, t1m, t2p, t2m, t3p, t3m, t4p, t4m]
     q_all.append(swap(jnp.concatenate([b, t1p, t1m, t2p, t2m])))
-    q_all.append(swap(jnp.concatenate([t3p, t3m])))
+    q_all += [swap(t3p), swap(t3m)]
     q_all.append(swap(jnp.concatenate([t4p, t4m])))
     o_all = [ob, o1p, o1m, o2p, o2m]
     o_all.append(swap(jnp.concatenate([ob, o1p, o1m])))
-    o_all.append(swap(jnp.concatenate([o2p, o2m])))
+    o_all += [swap(o2p), swap(o2m)]
     return kv_all, q_all, o_all, tab
 
 

time: 171 us -> 173 us (1.012)
  the two profiles are of different devices: /device:TPU:24 before, /device:TPU:120 now
where the time goes in v3:
time: 173 us; the launch traced here: 172 us
  waiting for transfers between devices  61.1 us (35%)
  starting transfers between devices  41.5 us (24%)
  Pallas kernels  32.8 us (19%)
  local copies, waits for them, and re-layouts  24.8 us (14%)
  other arithmetic  11.6 us (7%)
    ppermute x16, waiting for transfers between devices, along_z(): lax.ppermute(a, ('zl', 'zh'), [(at[z], at[(z + step) % 8]) for z in range...  32.5 us
    ppermute x16, starting transfers between devices, along_z(): lax.ppermute(a, ('zl', 'zh'), [(at[z], at[(z + step) % 8]) for z in range...  23.2 us
    pallas_call x2, Pallas kernels, tail(): pl.pallas_call(functools.partial(tail_body, first, count), out_shape=[jax...  17.2 us
    pallas_call x1, Pallas kernels, head(): pl.pallas_call(head_body, out_shape=[jax.ShapeDtypeStruct((QB, HEADS * BL...  15.6 us
    unnamed x59, local copies, waits for them, and re-layouts  15.4 us
    ppermute x11, starting transfers between devices, along_x(): return lax.ppermute(a, 'x', [(i, (i + step) % 4) for i in range(4)])  12.4 us
    ppermute x11, waiting for transfers between devices, along_x(): return lax.ppermute(a, 'x', [(i, (i + step) % 4) for i in range(4)])  11.2 us
    ppermute x1, waiting for transfers between devices, local(): p = lax.ppermute(p, 'y', up)  10.7 us
  transfers between devices with their start and end apart: 40, of which 16 were waited for; matrix products, arithmetic and copies ran while one was open for 17% of the time, Pallas kernels for 10%

profile of v3, /device:TPU:120, one launch (start us, length us, event | category | flops | bytes accessed | tf_op | source)
XLA Modules:
  0.0 172.2 jit_solution(4500898575229884275)
XLA Ops:
  0.9 0.9 fusion.3
  1.8 3.2 %collective-permute-start.3 = (bf16[4,112,256]{2,1,0:T(8,128)(2,1)S(1)}, bf16[4,112,256]{2,1,0:T(8,128)(2,1)S(1)}, u32[]{:S(2)}, u32[]{:S(2)}) collective-permute-start(bf16[4,112,256]{2,1,0:T(8,128)(2,1)S(1)} %fusion.3), channel_id=1, source_target_pairs={{0,16},{16,32},{32,48},{48,1},{1,17},{17,33},{33,49},{49,0},{2,18}... | collective-permute-start | bytes 688136 | tf_op jit(solution)/shard_map/ppermute | solution.py:310
  5.0 1.5 collective-permute-start
  6.5 1.7 %collective-permute-start.1 = (bf16[2,112,256]{2,1,0:T(8,128)(2,1)}, bf16[2,112,256]{2,1,0:T(8,128)(2,1)S(1)}, u32[]{:S(2)}, u32[]{:S(2)}) collective-permute-start(bf16[2,112,256]{2,1,0:T(8,128)(2,1)} %param.19), channel_id=1, source_target_pairs={{0,192},{64,0},{128,64},{192,128},{1,193},{65,1},{129,65},{193,129... | collective-permute-start | bytes 344072 | tf_op jit(solution)/shard_map/ppermute | solution.py:305
  8.2 1.8 %collective-permute-start.2 = (bf16[2,112,256]{2,1,0:T(8,128)(2,1)}, bf16[2,112,256]{2,1,0:T(8,128)(2,1)S(1)}, u32[]{:S(2)}, u32[]{:S(2)}) collective-permute-start(bf16[2,112,256]{2,1,0:T(8,128)(2,1)} %param.19), channel_id=1, source_target_pairs={{0,128},{64,192},{128,0},{192,64},{1,129},{65,193},{129,1},{193,65... | collective-permute-start | bytes 344072 | tf_op jit(solution)/shard_map/ppermute | solution.py:305
  10.0 1.6 bitcast_dynamic-update-slice_fusion
  11.6 1.6 constant_dynamic-update-slice_fusion.9
  13.2 3.3 %collective-permute-start.4 = (bf16[3,112,256]{2,1,0:T(8,128)(2,1)S(1)}, bf16[3,112,256]{2,1,0:T(8,128)(2,1)S(1)}, u32[]{:S(2)}, u32[]{:S(2)}) collective-permute-start(bf16[3,112,256]{2,1,0:T(8,128)(2,1)S(1)} %slice.96), channel_id=1, source_target_pairs={{0,16},{16,32},{32,48},{48,1},{1,17},{17,33},{33,49},{49,0},{2,18}... | collective-permute-start | bytes 516104 | tf_op jit(solution)/shard_map/ppermute | solution.py:310
  18.0 1.5 collective-permute-done.4
  19.4 3.8 %collective-permute-start.5 = (bf16[2,112,256]{2,1,0:T(8,128)(2,1)S(1)}, bf16[2,112,256]{2,1,0:T(8,128)(2,1)S(1)}, u32[]{:S(2)}, u32[]{:S(2)}) collective-permute-start(bf16[2,112,256]{2,1,0:T(8,128)(2,1)S(1)} %slice.97), channel_id=1, source_target_pairs={{0,16},{16,32},{32,48},{48,1},{1,17},{17,33},{33,49},{49,0},{2,18}... | collective-permute-start | bytes 344072 | tf_op jit(solution)/shard_map/ppermute | solution.py:310
  25.5 2.6 %collective-permute-start.14 = (bf16[2,4,112,256]{3,2,1,0:T(8,128)(2,1)S(1)}, bf16[2,4,112,256]{3,2,1,0:T(8,128)(2,1)S(1)}, u32[]{:S(2)}, u32[]{:S(2)}) collective-permute-start(bf16[2,4,112,256]{3,2,1,0:T(8,128)(2,1)S(1)} %pad_maximum_fusion.2.refs_0_), channel_id=1, source_target_pairs={{0,192},{64,0},{128,64},{192,128},{1,193},{65,1},{129,65},{193,129... | collective-permute-start | bytes 1376264 | tf_op jit(solution)/shard_map/ppermute | solution.py:305
  28.2 1.3 collective-permute-done.8
  29.7 3.2 %collective-permute-start.9 = (bf16[4,2,112,256]{3,2,1,0:T(8,128)(2,1)S(1)}, bf16[4,2,112,256]{3,2,1,0:T(8,128)(2,1)S(1)}, u32[]{:S(2)}, u32[]{:S(2)}) collective-permute-start(bf16[4,2,112,256]{3,2,1,0:T(8,128)(2,1)S(1)} %pad_maximum_fusion.1.refs_7_), channel_id=1, source_target_pairs={{0,16},{16,32},{32,48},{48,1},{1,17},{17,33},{33,49},{49,0},{2,18}... | collective-permute-start | bytes 1376264 | tf_op jit(solution)/shard_map/ppermute | solution.py:310
  34.9 5.5 %collective-permute-done.12 = bf16[112,256]{1,0:T(8,128)(2,1)S(1)} collective-permute-done((bf16[112,256]{1,0:T(8,128)(2,1)S(1)}, bf16[112,256]{1,0:T(8,128)(2,1)S(1)}, u32[]{:S(2)}, u32[]{:S(2)}) %collective-permute-start.12) | collective-permute-done | bytes 57376 | tf_op jit(solution)/shard_map/ppermute | solution.py:310
  40.4 1.0 collective-permute-start.11
  42.0 2.6 %collective-permute-done.11 = bf16[112,256]{1,0:T(8,128)(2,1)S(1)} collective-permute-done((bf16[112,256]{1,0:T(8,128)(2,1)S(1)}, bf16[112,256]{1,0:T(8,128)(2,1)S(1)}, u32[]{:S(2)}, u32[]{:S(2)}) %collective-permute-start.11) | collective-permute-done | bytes 57376 | tf_op jit(solution)/shard_map/ppermute | solution.py:310
  46.5 2.6 %collective-permute-start.18 = (bf16[8,2,112,256]{3,2,1,0:T(8,128)(2,1)S(1)}, bf16[8,2,112,256]{3,2,1,0:T(8,128)(2,1)S(1)}, u32[]{:S(2)}, u32[]{:S(2)}) collective-permute-start(bf16[8,2,112,256]{3,2,1,0:T(8,128)(2,1)S(1)} %get-tuple-element.64.refs_20_.refs_0_), channel_id=1, source_target_pairs={{0,192},{64,0},{128,64},{192,128},{1,193},{65,1},{129,65},{193,129... | collective-permute-start | bytes 2752520 | tf_op jit(solution)/shard_map/ppermute | solution.py:305
  49.2 2.3 %collective-permute-start.15 = (bf16[4,2,112,256]{3,2,1,0:T(8,128)(2,1)S(1)}, bf16[4,2,112,256]{3,2,1,0:T(8,128)(2,1)S(1)}, u32[]{:S(2)}, u32[]{:S(2)}) collective-permute-start(bf16[4,2,112,256]{3,2,1,0:T(8,128)(2,1)S(1)} %collective-permute-done.9.refs_8_), channel_id=1, source_target_pairs={{0,16},{16,32},{32,48},{48,1},{1,17},{17,33},{33,49},{49,0},{2,18}... | collective-permute-start | bytes 1376264 | tf_op jit(solution)/shard_map/ppermute | solution.py:310
  53.1 1.2 pad_maximum_fusion
  55.1 2.6 %collective-permute-done.15.refs_10_ = bf16[4,2,112,256]{3,2,1,0:T(8,128)(2,1)S(1)} collective-permute-done((bf16[4,2,112,256]{3,2,1,0:T(8,128)(2,1)S(1)}, bf16[4,2,112,256]{3,2,1,0:T(8,128)(2,1)S(1)}, u32[]{:S(2)}, u32[]{:S(2)}) %collective-permute-start.15) | collective-permute-done | bytes 458784 | tf_op jit(solution)/shard_map/ppermute | solution.py:310
  58.3 2.9 %collective-permute-done.16.refs_11_ = bf16[4,2,112,256]{3,2,1,0:T(8,128)(2,1)} collective-permute-done((bf16[4,2,112,256]{3,2,1,0:T(8,128)(2,1)S(1)}, bf16[4,2,112,256]{3,2,1,0:T(8,128)(2,1)}, u32[]{:S(2)}, u32[]{:S(2)}) %collective-permute-start.16) | collective-permute-done | bytes 458784 | tf_op jit(solution)/shard_map/ppermute | solution.py:310
  61.2 4.3 %collective-permute-done.17.refs_21_.refs_1_ = bf16[8,2,112,256]{3,2,1,0:T(8,128)(2,1)S(1)} collective-permute-done((bf16[8,2,112,256]{3,2,1,0:T(8,128)(2,1)S(1)}, bf16[8,2,112,256]{3,2,1,0:T(8,128)(2,1)S(1)}, u32[]{:S(2)}, u32[]{:S(2)}) %collective-permute-start.17) | collective-permute-done | bytes 917536 | tf_op jit(solution)/shard_map/ppermute | solution.py:305
  65.6 2.9 %collective-permute-start.26 = (bf16[4,2,112,256]{3,2,1,0:T(8,128)(2,1)S(1)}, bf16[4,2,112,256]{3,2,1,0:T(8,128)(2,1)}, u32[]{:S(2)}, u32[]{:S(2)}) collective-permute-start(bf16[4,2,112,256]{3,2,1,0:T(8,128)(2,1)S(1)} %collective-permute-done.15.refs_10_), channel_id=1, source_target_pairs={{0,16},{16,32},{32,48},{48,1},{1,17},{17,33},{33,49},{49,0},{2,18}... | collective-permute-start | bytes 1376264 | tf_op jit(solution)/shard_map/ppermute | solution.py:310
  68.4 1.0 constant_dynamic-update-slice_fusion.1
  69.4 1.0 constant_dynamic-update-slice_fusion
  71.4 1.8 %constant_dynamic-update-slice_fusion.2 = bf16[20,2,112,256]{3,2,1,0:T(8,128)(2,1)} fusion(bf16[20,2,112,256]{3,2,1,0:T(8,128)(2,1)} %constant_dynamic-update-slice_fusion.3, bf16[4,2,112,256]{3,2,1,0:T(8,128)(2,1)} %collective-permute-done.16.refs_11_), kind=kLoop, calls=%fused_computation.43 | loop fusion | bytes 917504 | tf_op jit(solution)/shard_map/concatenate | solution.py:351
  73.8 1.1 slice.110
  74.9 1.1 slice.111
  76.0 9.8 %collective-permute-done.27.refs_13_ = bf16[4,2,112,256]{3,2,1,0:T(8,128)(2,1)} collective-permute-done((bf16[4,2,112,256]{3,2,1,0:T(8,128)(2,1)}, bf16[4,2,112,256]{3,2,1,0:T(8,128)(2,1)}, u32[]{:S(2)}, u32[]{:S(2)}) %collective-permute-start.27) | collective-permute-done | bytes 458784 | tf_op jit(solution)/shard_map/ppermute | solution.py:310
  86.0 1.0 slice.112
  87.0 1.0 slice.113
  87.9 1.8 %collective-permute-done.19.refs_23_.refs_3_ = bf16[4,2,112,256]{3,2,1,0:T(8,128)(2,1)S(1)} collective-permute-done((bf16[4,2,112,256]{3,2,1,0:T(8,128)(2,1)S(1)}, bf16[4,2,112,256]{3,2,1,0:T(8,128)(2,1)S(1)}, u32[]{:S(2)}, u32[]{:S(2)}) %collective-permute-start.19) | collective-permute-done | bytes 458784 | tf_op jit(solution)/shard_map/ppermute | solution.py:305
  89.7 3.2 %collective-permute-start.30 = (bf16[2,2,112,256]{3,2,1,0:T(8,128)(2,1)S(1)}, bf16[2,2,112,256]{3,2,1,0:T(8,128)(2,1)S(1)}, u32[]{:S(2)}, u32[]{:S(2)}) collective-permute-start(bf16[2,2,112,256]{3,2,1,0:T(8,128)(2,1)S(1)} %slice.112), channel_id=1, source_target_pairs={{0,16},{16,32},{32,48},{48,1},{1,17},{17,33},{33,49},{49,0},{2,18}... | collective-permute-start | bytes 688136 | tf_op jit(solution)/shard_map/ppermute | solution.py:310
  92.9 5.1 %collective-permute-done.20.refs_24_.refs_4_ = bf16[4,2,112,256]{3,2,1,0:T(8,128)(2,1)} collective-permute-done((bf16[4,2,112,256]{3,2,1,0:T(8,128)(2,1)S(1)}, bf16[4,2,112,256]{3,2,1,0:T(8,128)(2,1)}, u32[]{:S(2)}, u32[]{:S(2)}) %collective-permute-start.20) | collective-permute-done | bytes 458784 | tf_op jit(solution)/shard_map/ppermute | solution.py:305
  98.0 1.0 pad_maximum_fusion.3
  99.1 6.4 %collective-permute-done.31.refs_15_ = bf16[2,2,112,256]{3,2,1,0:T(8,128)(2,1)S(1)} collective-permute-done((bf16[2,2,112,256]{3,2,1,0:T(8,128)(2,1)S(1)}, bf16[2,2,112,256]{3,2,1,0:T(8,128)(2,1)S(1)}, u32[]{:S(2)}, u32[]{:S(2)}) %collective-permute-start.31) | collective-permute-done | bytes 229408 | tf_op jit(solution)/shard_map/ppermute | solution.py:310
  111.4 1.5 copy-done
  112.8 15.6 %head.1 = (bf16[4,512,128]{2,1,0:T(8,128)(2,1)}, bf16[1024,128]{1,0:T(8,128)(2,1)}, bf16[1024,128]{1,0:T(8,128)(2,1)}, bf16[128,1792]{1,0:T(8,128)(2,1)}, bf16[128,1792]{1,0:T(8,128)(2,1)}) custom-call(s32[8]{0:T(128)} %bitcast.91, s32[8,8]{1,0:T(8,128)} %bitcast.88, s32[162]{0:T(256)} %concatenate.22.tab, bf16[2,4,112,256]{3,2,1,0:T(8,128)(2,1)} %copy-done.7, ...), custom_call_target="tpu_custom_call" | custom-call | flops 3758096384 | bytes 25690112 | tf_op jit(solution)/shard_map/head/pallas_call | solution.py:250
  128.8 1.8 %collective-permute-start.38 = (bf16[128,1792]{1,0:T(8,128)(2,1)}, bf16[128,1792]{1,0:T(8,128)(2,1)S(1)}, u32[]{:S(2)}, u32[]{:S(2)}) collective-permute-start(bf16[128,1792]{1,0:T(8,128)(2,1)} %get-tuple-element.48), channel_id=1, source_target_pairs={{0,6},{2,0},{4,2},{6,4},{1,7},{3,1},{5,3},{7,5},{8,14},{10,8},{12,... | collective-permute-start | bytes 1376264 | tf_op jit(solution)/shard_map/ppermute | solution.py:376
  130.6 9.8 %tail.3 = (bf16[128,3584]{1,0:T(8,128)(2,1)}, bf16[128,3584]{1,0:T(8,128)(2,1)}) custom-call(s32[8]{0:T(128)} %bitcast.92, s32[8,8]{1,0:T(8,128)} %bitcast.89, s32[162]{0:T(256)} %concatenate.22.tab, bf16[8,2,112,256]{3,2,1,0:T(8,128)(2,1)} %copy-done.3, bf16[8,2,112,256]{3,2,1,0:T(8,128)(2,1)} %copy-done.1, bf16[8,2,112,256]{3,2,1,0:T(8,128)(2,1)} %copy-done.2, ...), custom_call_target="tpu_custom_call" | custom-call | flops 1476395008 | bytes 7340032 | tf_op jit(solution)/shard_map/tail/pallas_call | solution.py:284
  140.4 1.1 collective-permute-done.36
  141.5 1.9 %fusion.1 = bf16[128,3584]{1,0:T(8,128)(2,1)} fusion(bf16[128,3584]{1,0:T(8,128)(2,1)} %get-tuple-element.45, bf16[128,1792]{1,0:T(8,128)(2,1)S(1)} %collective-permute-done.36), kind=kLoop, calls=%fused_computation.5 | loop fusion | flops 917504 | bytes 1376256 | tf_op jit(solution)/shard_map/dynamic_update_slice | solution.py:378
  143.5 1.5 collective-permute-start.37
  145.0 1.9 %fusion.2 = bf16[128,3584]{1,0:T(8,128)(2,1)} fusion(bf16[128,3584]{1,0:T(8,128)(2,1)} %get-tuple-element.47, bf16[128,1792]{1,0:T(8,128)(2,1)S(1)} %collective-permute-done.38), kind=kLoop, calls=%fused_computation.6 | loop fusion | flops 917504 | bytes 1376256 | tf_op jit(solution)/shard_map/dynamic_update_slice | solution.py:379
  147.4 7.3 %tail.2 = bf16[128,3584]{1,0:T(8,128)(2,1)} custom-call(s32[8]{0:T(128)} %bitcast.93, s32[8,8]{1,0:T(8,128)} %bitcast.90, s32[162]{0:T(256)} %concatenate.22.tab, bf16[8,2,112,256]{3,2,1,0:T(8,128)(2,1)} %copy-done.3, bf16[8,2,112,256]{3,2,1,0:T(8,128)(2,1)} %copy-done.1, bf16[8,2,112,256]{3,2,1,0:T(8,128)(2,1)} %copy-done.2, ...), custom_call_target="tpu_custom_call" | custom-call | flops 738197504 | bytes 7340032 | tf_op jit(solution)/shard_map/tail/pallas_call | solution.py:284
  154.7 10.7 %collective-permute-done.37 = bf16[128,3584]{1,0:T(8,128)(2,1)S(1)} collective-permute-done((bf16[128,3584]{1,0:T(8,128)(2,1)}, bf16[128,3584]{1,0:T(8,128)(2,1)S(1)}, u32[]{:S(2)}, u32[]{:S(2)}) %collective-permute-start.37) | collective-permute-done | bytes 917536 | tf_op jit(solution)/shard_map/ppermute | solution.py:380
  165.4 4.4 %collective-permute-done.39 = bf16[128,3584]{1,0:T(8,128)(2,1)S(1)} collective-permute-done((bf16[128,3584]{1,0:T(8,128)(2,1)}, bf16[128,3584]{1,0:T(8,128)(2,1)S(1)}, u32[]{:S(2)}, u32[]{:S(2)}) %collective-permute-start.39) | collective-permute-done | bytes 917536 | tf_op jit(solution)/shard_map/ppermute | solution.py:381
  169.8 2.4 %fusion = bf16[1,128,3584]{2,1,0:T(8,128)(2,1)} fusion(bf16[128,3584]{1,0:T(8,128)(2,1)S(1)} %collective-permute-done.39, bf16[128,3584]{1,0:T(8,128)(2,1)S(1)} %collective-permute-done.37, bf16[128,3584]{1,0:T(8,128)(2,1)} %tail.2), kind=kLoop, calls=%fused_computation.2 | loop fusion | flops 2752512 | bytes 3670016 | tf_op jit(solution)/shard_map/broadcast_in_dim | solution.py:383
  (140 shorter events, 20.9 us)
Async XLA Ops:
  1.8 11.4 %collective-permute-start.3 = (bf16[4,112,256]{2,1,0:T(8,128)(2,1)S(1)}, bf16[4,112,256]{2,1,0:T(8,128)(2,1)S(1)}, u32[]{:S(2)}, u32[]{:S(2)}) collective-permute-start(bf16[4,112,256]{2,1,0:T(8,128)(2,1)S(1)} %fusion.3), channel_id=1, source_target_pairs={{0,16},{16,32},{32,48},{48,1},{1,17},{17,33},{33,49},{49,0},{2,18}... | collective-permute-start | bytes 688136 | tf_op jit(solution)/shard_map/ppermute | solution.py:310
  5.0 11.5 %collective-permute-start.6 = (bf16[4,112,256]{2,1,0:T(8,128)(2,1)S(1)}, bf16[4,112,256]{2,1,0:T(8,128)(2,1)S(1)}, u32[]{:S(2)}, u32[]{:S(2)}) collective-permute-start(bf16[4,112,256]{2,1,0:T(8,128)(2,1)S(1)} %fusion.3), channel_id=1, source_target_pairs={{0,49},{16,0},{32,16},{48,32},{1,48},{17,1},{33,17},{49,33},{2,51}... | collective-permute-start | bytes 688136 | tf_op jit(solution)/shard_map/ppermute | solution.py:310
  5.0 19.8 %collective-permute-start = (bf16[2,112,256]{2,1,0:T(8,128)(2,1)}, bf16[2,112,256]{2,1,0:T(8,128)(2,1)S(1)}, u32[]{:S(2)}, u32[]{:S(2)}) collective-permute-start(bf16[2,112,256]{2,1,0:T(8,128)(2,1)} %param.19), channel_id=1, source_target_pairs={{0,64},{64,128},{128,192},{192,0},{1,65},{65,129},{129,193},{193,1... | collective-permute-start | bytes 344072 | tf_op jit(solution)/shard_map/ppermute | solution.py:305
  6.5 19.0 %collective-permute-start.1 = (bf16[2,112,256]{2,1,0:T(8,128)(2,1)}, bf16[2,112,256]{2,1,0:T(8,128)(2,1)S(1)}, u32[]{:S(2)}, u32[]{:S(2)}) collective-permute-start(bf16[2,112,256]{2,1,0:T(8,128)(2,1)} %param.19), channel_id=1, source_target_pairs={{0,192},{64,0},{128,64},{192,128},{1,193},{65,1},{129,65},{193,129... | collective-permute-start | bytes 344072 | tf_op jit(solution)/shard_map/ppermute | solution.py:305
  8.2 19.9 %collective-permute-start.2 = (bf16[2,112,256]{2,1,0:T(8,128)(2,1)}, bf16[2,112,256]{2,1,0:T(8,128)(2,1)S(1)}, u32[]{:S(2)}, u32[]{:S(2)}) collective-permute-start(bf16[2,112,256]{2,1,0:T(8,128)(2,1)} %param.19), channel_id=1, source_target_pairs={{0,128},{64,192},{128,0},{192,64},{1,129},{65,193},{129,1},{193,65... | collective-permute-start | bytes 344072 | tf_op jit(solution)/shard_map/ppermute | solution.py:305
  13.2 16.3 %copy-start.15 = (bf16[2,112,256]{2,1,0:T(8,128)(2,1)S(1)}, bf16[2,112,256]{2,1,0:T(8,128)(2,1)}, u32[]{:S(2)}) copy-start(bf16[2,112,256]{2,1,0:T(8,128)(2,1)} %param.19) | copy-start | bytes 344068
  13.2 6.2 %collective-permute-start.4 = (bf16[3,112,256]{2,1,0:T(8,128)(2,1)S(1)}, bf16[3,112,256]{2,1,0:T(8,128)(2,1)S(1)}, u32[]{:S(2)}, u32[]{:S(2)}) collective-permute-start(bf16[3,112,256]{2,1,0:T(8,128)(2,1)S(1)} %slice.96), channel_id=1, source_target_pairs={{0,16},{16,32},{32,48},{48,1},{1,17},{17,33},{33,49},{49,0},{2,18}... | collective-permute-start | bytes 516104 | tf_op jit(solution)/shard_map/ppermute | solution.py:310
  16.5 6.7 %collective-permute-start.7 = (bf16[3,112,256]{2,1,0:T(8,128)(2,1)S(1)}, bf16[3,112,256]{2,1,0:T(8,128)(2,1)S(1)}, u32[]{:S(2)}, u32[]{:S(2)}) collective-permute-start(bf16[3,112,256]{2,1,0:T(8,128)(2,1)S(1)} %slice.98), channel_id=1, source_target_pairs={{0,49},{16,0},{32,16},{48,32},{1,48},{17,1},{33,17},{49,33},{2,51}... | collective-permute-start | bytes 516104 | tf_op jit(solution)/shard_map/ppermute | solution.py:310
  19.4 8.7 %collective-permute-start.5 = (bf16[2,112,256]{2,1,0:T(8,128)(2,1)S(1)}, bf16[2,112,256]{2,1,0:T(8,128)(2,1)S(1)}, u32[]{:S(2)}, u32[]{:S(2)}) collective-permute-start(bf16[2,112,256]{2,1,0:T(8,128)(2,1)S(1)} %slice.97), channel_id=1, source_target_pairs={{0,16},{16,32},{32,48},{48,1},{1,17},{17,33},{33,49},{49,0},{2,18}... | collective-permute-start | bytes 344072 | tf_op jit(solution)/shard_map/ppermute | solution.py:310
  23.2 6.3 %collective-permute-start.8 = (bf16[2,112,256]{2,1,0:T(8,128)(2,1)S(1)}, bf16[2,112,256]{2,1,0:T(8,128)(2,1)S(1)}, u32[]{:S(2)}, u32[]{:S(2)}) collective-permute-start(bf16[2,112,256]{2,1,0:T(8,128)(2,1)S(1)} %slice.99), channel_id=1, source_target_pairs={{0,49},{16,0},{32,16},{48,32},{1,48},{17,1},{33,17},{49,33},{2,51}... | collective-permute-start | bytes 344072 | tf_op jit(solution)/shard_map/ppermute | solution.py:310
  24.8 24.3 %copy-start.7 = (bf16[2,4,112,256]{3,2,1,0:T(8,128)(2,1)}, bf16[2,4,112,256]{3,2,1,0:T(8,128)(2,1)S(1)}, u32[]{:S(2)}) copy-start(bf16[2,4,112,256]{3,2,1,0:T(8,128)(2,1)S(1)} %pad_maximum_fusion.2.refs_0_) | copy-start | bytes 1376260
  24.8 21.6 %collective-permute-start.13 = (bf16[2,4,112,256]{3,2,1,0:T(8,128)(2,1)S(1)}, bf16[2,4,112,256]{3,2,1,0:T(8,128)(2,1)S(1)}, u32[]{:S(2)}, u32[]{:S(2)}) collective-permute-start(bf16[2,4,112,256]{3,2,1,0:T(8,128)(2,1)S(1)} %pad_maximum_fusion.2.refs_0_), channel_id=1, source_target_pairs={{0,64},{64,128},{128,192},{192,0},{1,65},{65,129},{129,193},{193,1... | collective-permute-start | bytes 1376264 | tf_op jit(solution)/shard_map/ppermute | solution.py:305
  25.5 23.6 %collective-permute-start.14 = (bf16[2,4,112,256]{3,2,1,0:T(8,128)(2,1)S(1)}, bf16[2,4,112,256]{3,2,1,0:T(8,128)(2,1)S(1)}, u32[]{:S(2)}, u32[]{:S(2)}) collective-permute-start(bf16[2,4,112,256]{3,2,1,0:T(8,128)(2,1)S(1)} %pad_maximum_fusion.2.refs_0_), channel_id=1, source_target_pairs={{0,192},{64,0},{128,64},{192,128},{1,193},{65,1},{129,65},{193,129... | collective-permute-start | bytes 1376264 | tf_op jit(solution)/shard_map/ppermute | solution.py:305
  29.6 19.6 %copy-start.8 = (bf16[4,2,112,256]{3,2,1,0:T(8,128)(2,1)}, bf16[4,2,112,256]{3,2,1,0:T(8,128)(2,1)S(1)}, u32[]{:S(2)}) copy-start(bf16[4,2,112,256]{3,2,1,0:T(8,128)(2,1)S(1)} %pad_maximum_fusion.1.refs_7_) | copy-start | bytes 1376260
  29.6 19.5 %collective-permute-start.10 = (bf16[4,2,112,256]{3,2,1,0:T(8,128)(2,1)S(1)}, bf16[4,2,112,256]{3,2,1,0:T(8,128)(2,1)S(1)}, u32[]{:S(2)}, u32[]{:S(2)}) collective-permute-start(bf16[4,2,112,256]{3,2,1,0:T(8,128)(2,1)S(1)} %pad_maximum_fusion.1.refs_7_), channel_id=1, source_target_pairs={{0,49},{16,0},{32,16},{48,32},{1,48},{17,1},{33,17},{49,33},{2,51}... | collective-permute-start | bytes 1376264 | tf_op jit(solution)/shard_map/ppermute | solution.py:310
  29.7 19.5 %collective-permute-start.9 = (bf16[4,2,112,256]{3,2,1,0:T(8,128)(2,1)S(1)}, bf16[4,2,112,256]{3,2,1,0:T(8,128)(2,1)S(1)}, u32[]{:S(2)}, u32[]{:S(2)}) collective-permute-start(bf16[4,2,112,256]{3,2,1,0:T(8,128)(2,1)S(1)} %pad_maximum_fusion.1.refs_7_), channel_id=1, source_target_pairs={{0,16},{16,32},{32,48},{48,1},{1,17},{17,33},{33,49},{49,0},{2,18}... | collective-permute-start | bytes 1376264 | tf_op jit(solution)/shard_map/ppermute | solution.py:310
  33.6 6.8 %collective-permute-start.12 = (bf16[112,256]{1,0:T(8,128)(2,1)S(1)}, bf16[112,256]{1,0:T(8,128)(2,1)S(1)}, u32[]{:S(2)}, u32[]{:S(2)}) collective-permute-start(bf16[112,256]{1,0:T(8,128)(2,1)S(1)} %slice_bitcast_fusion.4), channel_id=1, source_target_pairs={{0,49},{16,0},{32,16},{48,32},{1,48},{17,1},{33,17},{49,33},{2,51}... | collective-permute-start | bytes 172040 | tf_op jit(solution)/shard_map/ppermute | solution.py:310
  40.4 4.2 %collective-permute-start.11 = (bf16[112,256]{1,0:T(8,128)(2,1)S(1)}, bf16[112,256]{1,0:T(8,128)(2,1)S(1)}, u32[]{:S(2)}, u32[]{:S(2)}) collective-permute-start(bf16[112,256]{1,0:T(8,128)(2,1)S(1)} %slice_bitcast_fusion.5), channel_id=1, source_target_pairs={{0,16},{16,32},{32,48},{48,1},{1,17},{17,33},{33,49},{49,0},{2,18}... | collective-permute-start | bytes 172040 | tf_op jit(solution)/shard_map/ppermute | solution.py:310
  45.2 20.3 %collective-permute-start.17 = (bf16[8,2,112,256]{3,2,1,0:T(8,128)(2,1)S(1)}, bf16[8,2,112,256]{3,2,1,0:T(8,128)(2,1)S(1)}, u32[]{:S(2)}, u32[]{:S(2)}) collective-permute-start(bf16[8,2,112,256]{3,2,1,0:T(8,128)(2,1)S(1)} %get-tuple-element.64.refs_20_.refs_0_), channel_id=1, source_target_pairs={{0,64},{64,128},{128,192},{192,0},{1,65},{65,129},{129,193},{193,1... | collective-permute-start | bytes 2752520 | tf_op jit(solution)/shard_map/ppermute | solution.py:305
  46.5 22.9 %collective-permute-start.18 = (bf16[8,2,112,256]{3,2,1,0:T(8,128)(2,1)S(1)}, bf16[8,2,112,256]{3,2,1,0:T(8,128)(2,1)S(1)}, u32[]{:S(2)}, u32[]{:S(2)}) collective-permute-start(bf16[8,2,112,256]{3,2,1,0:T(8,128)(2,1)S(1)} %get-tuple-element.64.refs_20_.refs_0_), channel_id=1, source_target_pairs={{0,192},{64,0},{128,64},{192,128},{1,193},{65,1},{129,65},{193,129... | collective-permute-start | bytes 2752520 | tf_op jit(solution)/shard_map/ppermute | solution.py:305
  49.2 8.6 %collective-permute-start.15 = (bf16[4,2,112,256]{3,2,1,0:T(8,128)(2,1)S(1)}, bf16[4,2,112,256]{3,2,1,0:T(8,128)(2,1)S(1)}, u32[]{:S(2)}, u32[]{:S(2)}) collective-permute-start(bf16[4,2,112,256]{3,2,1,0:T(8,128)(2,1)S(1)} %collective-permute-done.9.refs_8_), channel_id=1, source_target_pairs={{0,16},{16,32},{32,48},{48,1},{1,17},{17,33},{33,49},{49,0},{2,18}... | collective-permute-start | bytes 1376264 | tf_op jit(solution)/shard_map/ppermute | solution.py:310
  51.4 9.8 %collective-permute-start.16 = (bf16[4,2,112,256]{3,2,1,0:T(8,128)(2,1)S(1)}, bf16[4,2,112,256]{3,2,1,0:T(8,128)(2,1)}, u32[]{:S(2)}, u32[]{:S(2)}) collective-permute-start(bf16[4,2,112,256]{3,2,1,0:T(8,128)(2,1)S(1)} %collective-permute-done.10.refs_9_), channel_id=1, source_target_pairs={{0,49},{16,0},{32,16},{48,32},{1,48},{17,1},{33,17},{49,33},{2,51}... | collective-permute-start | bytes 1376264 | tf_op jit(solution)/shard_map/ppermute | solution.py:310
  51.5 19.8 %collective-permute-start.24 = (bf16[4,112,256]{2,1,0:T(8,128)(2,1)S(1)}, bf16[4,112,256]{2,1,0:T(8,128)(2,1)S(1)}, u32[]{:S(2)}, u32[]{:S(2)}) collective-permute-start(bf16[4,112,256]{2,1,0:T(8,128)(2,1)S(1)} %slice_bitcast_fusion.1), channel_id=1, source_target_pairs={{0,64},{64,128},{128,192},{192,0},{1,65},{65,129},{129,193},{193,1... | collective-permute-start | bytes 688136 | tf_op jit(solution)/shard_map/ppermute | solution.py:305
  57.7 13.5 %copy-start.11 = (bf16[4,2,112,256]{3,2,1,0:T(8,128)(2,1)}, bf16[4,2,112,256]{3,2,1,0:T(8,128)(2,1)S(1)}, u32[]{:S(2)}) copy-start(bf16[4,2,112,256]{3,2,1,0:T(8,128)(2,1)S(1)} %collective-permute-done.15.refs_10_) | copy-start | bytes 1376260
  57.7 15.5 %collective-permute-start.25 = (bf16[4,112,256]{2,1,0:T(8,128)(2,1)}, bf16[4,112,256]{2,1,0:T(8,128)(2,1)}, u32[]{:S(2)}, u32[]{:S(2)}) collective-permute-start(bf16[4,112,256]{2,1,0:T(8,128)(2,1)} %slice_bitcast_fusion), channel_id=1, source_target_pairs={{0,192},{64,0},{128,64},{192,128},{1,193},{65,1},{129,65},{193,129... | collective-permute-start | bytes 688136 | tf_op jit(solution)/shard_map/ppermute | solution.py:305
  61.2 44.3 %collective-permute-start.28 = (bf16[6,4,112,256]{3,2,1,0:T(8,128)(2,1)}, bf16[6,4,112,256]{3,2,1,0:T(8,128)(2,1)}, u32[]{:S(2)}, u32[]{:S(2)}) collective-permute-start(bf16[6,4,112,256]{3,2,1,0:T(8,128)(2,1)} %pad_maximum_fusion), channel_id=1, source_target_pairs={{0,8},{8,0},{1,9},{9,1},{2,10},{10,2},{3,11},{11,3},{4,12},{12,4},... | collective-permute-start | bytes 4128776 | tf_op jit(solution)/shard_map/ppermute | solution.py:314
  65.6 10.4 %collective-permute-start.26 = (bf16[4,2,112,256]{3,2,1,0:T(8,128)(2,1)S(1)}, bf16[4,2,112,256]{3,2,1,0:T(8,128)(2,1)}, u32[]{:S(2)}, u32[]{:S(2)}) collective-permute-start(bf16[4,2,112,256]{3,2,1,0:T(8,128)(2,1)S(1)} %collective-permute-done.15.refs_10_), channel_id=1, source_target_pairs={{0,16},{16,32},{32,48},{48,1},{1,17},{17,33},{33,49},{49,0},{2,18}... | collective-permute-start | bytes 1376264 | tf_op jit(solution)/shard_map/ppermute | solution.py:310
  70.4 27.6 %copy-start.20 = (s32[1,1,8]{2,1,0:T(1,128)S(1)}, s32[1,1,8]{2,1,0:T(1,128)}, u32[]{:S(2)}) copy-start(s32[1,1,8]{2,1,0:T(1,128)} %constant.20.clone) | copy-start | bytes 100
  70.4 40.9 %collective-permute-start.21 = (bf16[24,2,112,256]{3,2,1,0:T(8,128)(2,1)}, bf16[24,2,112,256]{3,2,1,0:T(8,128)(2,1)S(1)}, u32[]{:S(2)}, u32[]{:S(2)}) collective-permute-start(bf16[24,2,112,256]{3,2,1,0:T(8,128)(2,1)} %constant_dynamic-update-slice_fusion), channel_id=1, source_target_pairs={{0,8},{8,0},{1,9},{9,1},{2,10},{10,2},{3,11},{11,3},{4,12},{12,4},... | collective-permute-start | bytes 8257544 | tf_op jit(solution)/shard_map/ppermute | solution.py:314
  71.3 27.7 %copy-start.12 = (bf16[4,112,256]{2,1,0:T(8,128)(2,1)}, bf16[4,112,256]{2,1,0:T(8,128)(2,1)S(1)}, u32[]{:S(2)}) copy-start(bf16[4,112,256]{2,1,0:T(8,128)(2,1)S(1)} %collective-permute-done.24.refs_3_) | copy-start | bytes 688132
  71.3 14.5 %collective-permute-start.27 = (bf16[4,2,112,256]{3,2,1,0:T(8,128)(2,1)}, bf16[4,2,112,256]{3,2,1,0:T(8,128)(2,1)}, u32[]{:S(2)}, u32[]{:S(2)}) collective-permute-start(bf16[4,2,112,256]{3,2,1,0:T(8,128)(2,1)} %collective-permute-done.16.refs_11_), channel_id=1, source_target_pairs={{0,49},{16,0},{32,16},{48,32},{1,48},{17,1},{33,17},{49,33},{2,51}... | collective-permute-start | bytes 1376264 | tf_op jit(solution)/shard_map/ppermute | solution.py:310
  73.2 38.1 %collective-permute-start.32 = (bf16[20,2,112,256]{3,2,1,0:T(8,128)(2,1)}, bf16[20,2,112,256]{3,2,1,0:T(8,128)(2,1)}, u32[]{:S(2)}, u32[]{:S(2)}) collective-permute-start(bf16[20,2,112,256]{3,2,1,0:T(8,128)(2,1)} %constant_dynamic-update-slice_fusion.2), channel_id=1, source_target_pairs={{0,8},{8,0},{1,9},{9,1},{2,10},{10,2},{3,11},{11,3},{4,12},{12,4},... | collective-permute-start | bytes 6881288 | tf_op jit(solution)/shard_map/ppermute | solution.py:314
  73.8 35.2 %copy-start.19 = (s32[1,8,1]{1,2,0:T(1,128)S(1)}, s32[1,8,1]{1,2,0:T(1,128)}, u32[]{:S(2)}) copy-start(s32[1,8,1]{1,2,0:T(1,128)} %constant.18.clone) | copy-start | bytes 100
  75.9 13.7 %collective-permute-start.19 = (bf16[4,2,112,256]{3,2,1,0:T(8,128)(2,1)S(1)}, bf16[4,2,112,256]{3,2,1,0:T(8,128)(2,1)S(1)}, u32[]{:S(2)}, u32[]{:S(2)}) collective-permute-start(bf16[4,2,112,256]{3,2,1,0:T(8,128)(2,1)S(1)} %slice.110), channel_id=1, source_target_pairs={{0,64},{64,128},{128,192},{192,0},{1,65},{65,129},{129,193},{193,1... | collective-permute-start | bytes 1376264 | tf_op jit(solution)/shard_map/ppermute | solution.py:305
  85.8 12.2 %collective-permute-start.20 = (bf16[4,2,112,256]{3,2,1,0:T(8,128)(2,1)S(1)}, bf16[4,2,112,256]{3,2,1,0:T(8,128)(2,1)}, u32[]{:S(2)}, u32[]{:S(2)}) collective-permute-start(bf16[4,2,112,256]{3,2,1,0:T(8,128)(2,1)S(1)} %slice.111), channel_id=1, source_target_pairs={{0,192},{64,0},{128,64},{192,128},{1,193},{65,1},{129,65},{193,129... | collective-permute-start | bytes 1376264 | tf_op jit(solution)/shard_map/ppermute | solution.py:305
  89.7 21.7 %copy-start.4 = (bf16[4,2,112,256]{3,2,1,0:T(8,128)(2,1)}, bf16[4,2,112,256]{3,2,1,0:T(8,128)(2,1)S(1)}, u32[]{:S(2)}) copy-start(bf16[4,2,112,256]{3,2,1,0:T(8,128)(2,1)S(1)} %collective-permute-done.19.refs_23_.refs_3_) | copy-start | bytes 1376260
  89.7 9.3 %collective-permute-start.30 = (bf16[2,2,112,256]{3,2,1,0:T(8,128)(2,1)S(1)}, bf16[2,2,112,256]{3,2,1,0:T(8,128)(2,1)S(1)}, u32[]{:S(2)}, u32[]{:S(2)}) collective-permute-start(bf16[2,2,112,256]{3,2,1,0:T(8,128)(2,1)S(1)} %slice.112), channel_id=1, source_target_pairs={{0,16},{16,32},{32,48},{48,1},{1,17},{17,33},{33,49},{49,0},{2,18}... | collective-permute-start | bytes 688136 | tf_op jit(solution)/shard_map/ppermute | solution.py:310
  98.0 7.5 %collective-permute-start.31 = (bf16[2,2,112,256]{3,2,1,0:T(8,128)(2,1)S(1)}, bf16[2,2,112,256]{3,2,1,0:T(8,128)(2,1)S(1)}, u32[]{:S(2)}, u32[]{:S(2)}) collective-permute-start(bf16[2,2,112,256]{3,2,1,0:T(8,128)(2,1)S(1)} %slice.113), channel_id=1, source_target_pairs={{0,49},{16,0},{32,16},{48,32},{1,48},{17,1},{33,17},{49,33},{2,51}... | collective-permute-start | bytes 688136 | tf_op jit(solution)/shard_map/ppermute | solution.py:310
  99.0 8.0 %collective-permute-start.29 = (bf16[2,4,112,256]{3,2,1,0:T(8,128)(2,1)S(1)}, bf16[2,4,112,256]{3,2,1,0:T(8,128)(2,1)S(1)}, u32[]{:S(2)}, u32[]{:S(2)}) collective-permute-start(bf16[2,4,112,256]{3,2,1,0:T(8,128)(2,1)S(1)} %pad_maximum_fusion.3), channel_id=1, source_target_pairs={{0,8},{8,0},{1,9},{9,1},{2,10},{10,2},{3,11},{11,3},{4,12},{12,4},... | collective-permute-start | bytes 1376264 | tf_op jit(solution)/shard_map/ppermute | solution.py:314
  105.5 2.3 %collective-permute-start.33 = (bf16[4,2,112,256]{3,2,1,0:T(8,128)(2,1)}, bf16[4,2,112,256]{3,2,1,0:T(8,128)(2,1)S(1)}, u32[]{:S(2)}, u32[]{:S(2)}) collective-permute-start(bf16[4,2,112,256]{3,2,1,0:T(8,128)(2,1)} %collective-permute-done.26.refs_12_), channel_id=1, source_target_pairs={{0,8},{8,0},{1,9},{9,1},{2,10},{10,2},{3,11},{11,3},{4,12},{12,4},... | collective-permute-start | bytes 1376264 | tf_op jit(solution)/shard_map/ppermute | solution.py:314
  105.5 3.1 %collective-permute-start.34 = (bf16[4,2,112,256]{3,2,1,0:T(8,128)(2,1)}, bf16[4,2,112,256]{3,2,1,0:T(8,128)(2,1)}, u32[]{:S(2)}, u32[]{:S(2)}) collective-permute-start(bf16[4,2,112,256]{3,2,1,0:T(8,128)(2,1)} %collective-permute-done.27.refs_13_), channel_id=1, source_target_pairs={{0,8},{8,0},{1,9},{9,1},{2,10},{10,2},{3,11},{11,3},{4,12},{12,4},... | collective-permute-start | bytes 1376264 | tf_op jit(solution)/shard_map/ppermute | solution.py:314
  107.0 3.2 %collective-permute-start.22 = (bf16[4,2,112,256]{3,2,1,0:T(8,128)(2,1)S(1)}, bf16[4,2,112,256]{3,2,1,0:T(8,128)(2,1)}, u32[]{:S(2)}, u32[]{:S(2)}) collective-permute-start(bf16[4,2,112,256]{3,2,1,0:T(8,128)(2,1)S(1)} %collective-permute-done.19.refs_23_.refs_3_), channel_id=1, source_target_pairs={{0,8},{8,0},{1,9},{9,1},{2,10},{10,2},{3,11},{11,3},{4,12},{12,4},... | collective-permute-start | bytes 1376264 | tf_op jit(solution)/shard_map/ppermute | solution.py:314
  108.5 2.2 %collective-permute-start.23 = (bf16[4,2,112,256]{3,2,1,0:T(8,128)(2,1)}, bf16[4,2,112,256]{3,2,1,0:T(8,128)(2,1)}, u32[]{:S(2)}, u32[]{:S(2)}) collective-permute-start(bf16[4,2,112,256]{3,2,1,0:T(8,128)(2,1)} %collective-permute-done.20.refs_24_.refs_4_), channel_id=1, source_target_pairs={{0,8},{8,0},{1,9},{9,1},{2,10},{10,2},{3,11},{11,3},{4,12},{12,4},... | collective-permute-start | bytes 1376264 | tf_op jit(solution)/shard_map/ppermute | solution.py:314
  108.6 2.7 %collective-permute-start.35 = (bf16[4,2,112,256]{3,2,1,0:T(8,128)(2,1)}, bf16[4,2,112,256]{3,2,1,0:T(8,128)(2,1)}, u32[]{:S(2)}, u32[]{:S(2)}) collective-permute-start(bf16[4,2,112,256]{3,2,1,0:T(8,128)(2,1)} %pad_maximum_fusion.4), channel_id=1, source_target_pairs={{0,8},{8,0},{1,9},{9,1},{2,10},{10,2},{3,11},{11,3},{4,12},{12,4},... | collective-permute-start | bytes 1376264 | tf_op jit(solution)/shard_map/ppermute | solution.py:314
  128.5 13.1 %collective-permute-start.36 = (bf16[128,1792]{1,0:T(8,128)(2,1)}, bf16[128,1792]{1,0:T(8,128)(2,1)S(1)}, u32[]{:S(2)}, u32[]{:S(2)}) collective-permute-start(bf16[128,1792]{1,0:T(8,128)(2,1)} %get-tuple-element.46), channel_id=1, source_target_pairs={{0,2},{2,4},{4,6},{6,0},{1,3},{3,5},{5,7},{7,1},{8,10},{10,12},{12... | collective-permute-start | bytes 1376264 | tf_op jit(solution)/shard_map/ppermute | solution.py:375
  128.8 16.2 %collective-permute-start.38 = (bf16[128,1792]{1,0:T(8,128)(2,1)}, bf16[128,1792]{1,0:T(8,128)(2,1)S(1)}, u32[]{:S(2)}, u32[]{:S(2)}) collective-permute-start(bf16[128,1792]{1,0:T(8,128)(2,1)} %get-tuple-element.48), channel_id=1, source_target_pairs={{0,6},{2,0},{4,2},{6,4},{1,7},{3,1},{5,3},{7,5},{8,14},{10,8},{12,... | collective-permute-start | bytes 1376264 | tf_op jit(solution)/shard_map/ppermute | solution.py:376
  143.5 22.0 %collective-permute-start.37 = (bf16[128,3584]{1,0:T(8,128)(2,1)}, bf16[128,3584]{1,0:T(8,128)(2,1)S(1)}, u32[]{:S(2)}, u32[]{:S(2)}) collective-permute-start(bf16[128,3584]{1,0:T(8,128)(2,1)} %fusion.1), channel_id=1, source_target_pairs={{0,2},{2,4},{4,6},{6,0},{1,3},{3,5},{5,7},{7,1},{8,10},{10,12},{12... | collective-permute-start | bytes 2752520 | tf_op jit(solution)/shard_map/ppermute | solution.py:380
  146.9 22.9 %collective-permute-start.39 = (bf16[128,3584]{1,0:T(8,128)(2,1)}, bf16[128,3584]{1,0:T(8,128)(2,1)S(1)}, u32[]{:S(2)}, u32[]{:S(2)}) collective-permute-start(bf16[128,3584]{1,0:T(8,128)(2,1)} %fusion.2), channel_id=1, source_target_pairs={{0,6},{2,0},{4,2},{6,4},{1,7},{3,1},{5,3},{7,5},{8,14},{10,8},{12,... | collective-permute-start | bytes 2752520 | tf_op jit(solution)/shard_map/ppermute | solution.py:381
  (14 other events, 61.1 us)
